TPU v7x, 32 devices: a whole 2x2x4 slice. The times are simulated.
32 devices in a mesh: grp: 4 (over x, core), tile: 8 (over z, y).
Axes of the slice: x: 2, y: 2, z: 4, core: 2. Of those that a mesh axis runs over, the one named last changes fastest.
Arguments:
- start_field: float32 [512, 128, 512], P('grp', 'tile'), may hold values from -4 to 4
- class_ids: int32 [128, 512], P('tile'), may hold values from 0 to 7
- run_levels: int32 [512, 8], replicated, may hold values from 0 to 7
- steepness: float32 [512], replicated, may hold values from 0.1 to 1
- step_pick: int32 [512], replicated, may hold values from 1 to 4
- input_layer: float32 [69, 2048], replicated, may hold values from -2 to 2
- output_layer: bfloat16 [2048, 65536], P(None, ('grp', 'tile')), may hold values from -0.125 to 0.125
- output_bias: float32 [65536], P(('grp', 'tile')), may hold values from -1.5 to 1.5
Outputs:
- misfit: bfloat16 [512, 65536], P(None, ('grp', 'tile'))
- output_next: bfloat16 [2048, 65536], P(None, ('grp', 'tile'))
- bias_next: float32 [65536], P(('grp', 'tile'))
- input_next: float32 [69, 2048], replicated
All inputs are finite; a program needn't handle non-finite values.
Results may differ from a plain program's by a relative error of at most 0.0029.
The roundings to bfloat16 on the way count: a program that leaves them out, or rounds other values in their place, can miss the bound.
Values sent between devices are 32-bit elements; how exact they have to be, the bound alone decides.
No kernel may reach another device: no remote copies, remote signals or barrier semaphores. Data moves between devices by JAX's collectives and lax.ppermute only.
A program may use at most 128 MiB of HBM per device.

v0:
```python
import functools

import jax
import jax.numpy as jnp
from jax import lax
from jax.experimental import pallas as pl
from jax.experimental.pallas import tpu as pltpu
from jax.sharding import PartitionSpec as P


STEPS = 4
LEVELS = 8
LANES = 128
SUB = 8
CHUNKS = 2
F32 = jnp.float32
BF16 = jnp.bfloat16
SPACE = pl.BlockSpec(memory_space=pltpu.VMEM)
ANY = pl.BlockSpec(memory_space=pl.ANY)


def cost(flops, nbytes, transcendentals=0):
    return pl.CostEstimate(
        flops=int(flops), bytes_accessed=int(nbytes), transcendentals=int(transcendentals)
    )


def spans(cols, chunks):
    width = cols // chunks
    out = []
    for c in range(chunks):
        low = max(c * width - SUB, 0)
        high = min((c + 1) * width + SUB, cols)
        sent = 0 if c == 0 else c * width + SUB
        out.append((low, high, sent))
    return out


def pack_kernel(parts, field_ref, ids_ref, *outs):
    rows, cols = ids_ref.shape
    for side in range(2):
        for r in range(STEPS):
            row = r if side == 0 else rows - STEPS + r
            for j in range(cols // LANES):
                tile = jnp.transpose(field_ref[:, row, j * LANES : (j + 1) * LANES])
                for c, (_, high, sent) in enumerate(parts):
                    first, last = max(sent, j * LANES), min(high, (j + 1) * LANES)
                    if first < last:
                        at = r * (high - sent) + first - sent
                        outs[2 * c + side][at : at + last - first, :] = tile[
                            first - j * LANES : last - j * LANES, :
                        ]
                at = STEPS * (parts[0][1] - parts[0][2]) + r * (cols // LANES) + j
                outs[side][at : at + 1, :] = ids_ref[
                    row : row + 1, j * LANES : (j + 1) * LANES
                ].astype(F32)


def pack_edges(start_field, ids, parts):
    runs, rows, cols = start_field.shape
    shapes = []
    for c, (_, high, sent) in enumerate(parts):
        extra = STEPS * cols // LANES if c == 0 else 0
        shapes += [jax.ShapeDtypeStruct((STEPS * (high - sent) + extra, runs), F32)] * 2
    return pl.pallas_call(
        functools.partial(pack_kernel, parts),
        in_specs=[SPACE, SPACE],
        out_specs=[SPACE] * len(shapes),
        out_shape=shapes,
        cost_estimate=cost(0, 6 * runs * rows * cols),
        name="pack_edges",
    )(start_field, ids)


def diffuse_kernel(chunk, chunks, ends_ref, field_ref, ids_ref, runs_ref, *refs):
    edges, (out_ref, raw_ref, u0_ref, u1_ref, d_ref, a_ref, b_ref, fx_ref, v_ref, sem) = (
        refs[:-10],
        refs[-10:],
    )
    cols = ids_ref.shape[2]
    rows = field_ref.shape[1]
    total = rows + 2 * STEPS
    parts = spans(cols, chunks)
    low, high, sent = parts[chunk]
    width = high - low
    own = cols // chunks
    tile0, tile1 = low // LANES, -(-high // LANES)
    copy = pltpu.make_async_copy(field_ref.at[:, :, tile0 * LANES : tile1 * LANES], raw_ref, sem)
    copy.start()

    level, pick, steep = runs_ref[0:LEVELS], runs_ref[LEVELS : LEVELS + 1], runs_ref[LEVELS + 1 : LEVELS + 2]
    table = 0.03 * jnp.exp(level * jnp.log(F32(1.35)))
    both = jnp.concatenate([table * (0.5 * steep), table * (0.5 * (1.0 - steep))], axis=1)
    pieces = []
    for _ in range(3):
        piece = both.astype(BF16).astype(F32)
        pieces.append(piece)
        both = both - piece
    pieces.append(jnp.zeros_like(both))
    tables = jnp.concatenate(pieces, axis=0).astype(BF16)
    klass = lax.broadcasted_iota(jnp.int32, (4 * LEVELS, LANES), 0) % LEVELS
    pick8 = jnp.broadcast_to(pick, (SUB, LANES))
    has_top, has_bottom = ends_ref[0], ends_ref[1]
    zeros = jnp.zeros((SUB, LANES), F32)

    def inside(r):
        return jnp.where(r < STEPS, has_top, jnp.where(r >= total - STEPS, has_bottom, 1.0))

    def coefficients(r, carry):
        valid = inside(r)
        ids = ids_ref[r]
        for j in range(tile0, tile1):
            here = jnp.broadcast_to(ids[:, j * LANES : (j + 1) * LANES], klass.shape)
            onehot = jnp.where(here == klass, valid, 0.0)
            ab = lax.dot_general(
                onehot.astype(BF16), tables, (((0,), (0,)), ((), ())), preferred_element_type=F32
            )
            first, last = max(low, j * LANES), min(high, (j + 1) * LANES)
            at, of = slice(first - low, last - low), slice(first - j * LANES, last - j * LANES)
            a_ref[r, at, :] = ab[of, :LANES]
            b_ref[r, at, :] = ab[of, LANES:]
        for ref in (u0_ref, u1_ref, d_ref):
            ref[r, 0:SUB, :] = zeros
            ref[r, SUB + width : 2 * SUB + width, :] = zeros
        return carry

    lax.fori_loop(0, total, coefficients, 0, unroll=4)

    for side in range(2):
        here = edges[side]
        for r in range(STEPS):
            row = r if side == 0 else total - STEPS + r
            n = high - sent
            at = SUB + sent - low
            u0_ref[row, at : at + n, :] = here[r * n : (r + 1) * n, :]
            if chunk:
                prior = edges[2 + side]
                n0 = parts[chunk - 1][1] - parts[chunk - 1][2]
                m = sent - low
                u0_ref[row, SUB : SUB + m, :] = prior[(r + 1) * n0 - m : (r + 1) * n0, :]
    copy.wait()
    for i in range(rows):
        for j in range(tile0, tile1):
            tile = jnp.transpose(raw_ref[:, i, (j - tile0) * LANES : (j - tile0 + 1) * LANES])
            first, last = max(low, j * LANES), min(high, (j + 1) * LANES)
            at = SUB + first - low
            u0_ref[STEPS + i, at : at + last - first, :] = tile[first - j * LANES : last - j * LANES, :]

    blocks = range(width // SUB)
    for step in range(1, STEPS + 1):
        src, dst = (u0_ref, u1_ref) if step % 2 else (u1_ref, u0_ref)

        def conduct(r, k, u, src=src):
            at = slice(k * SUB, (k + 1) * SUB)
            d = a_ref[r, at, :] + b_ref[r, at, :] * (1.0 / (1.0 + u * u))
            d_ref[r, SUB + k * SUB : 2 * SUB + k * SUB, :] = d
            return d

        top = step - 1
        for k in blocks:
            at = slice(SUB + k * SUB, 2 * SUB + k * SUB)
            u, un = src[top, at, :], src[top + 1, at, :]
            d, dn = conduct(top, k, u), conduct(top + 1, k, un)
            v_ref[k * SUB : (k + 1) * SUB, :] = (d + dn) * (un - u)

        def advance(r, carry, src=src, dst=dst, step=step, conduct=conduct):
            for k in range(-1, width // SUB):
                p = SUB + k * SUB
                flux = (d_ref[r, p : p + SUB, :] + d_ref[r, p + 1 : p + 1 + SUB, :]) * (
                    src[r, p + 1 : p + 1 + SUB, :] - src[r, p : p + SUB, :]
                )
                fx_ref[p : p + SUB, :] = flux
            active = pick8 >= jnp.where(inside(r) > 0.0, F32(step), F32(2 * STEPS))
            for k in blocks:
                p = SUB + k * SUB
                at = slice(k * SUB, (k + 1) * SUB)
                u, un = src[r, p : p + SUB, :], src[r + 1, p : p + SUB, :]
                d = d_ref[r, p : p + SUB, :]
                dn = conduct(r + 1, k, un)
                down = (d + dn) * (un - u)
                across = fx_ref[p : p + SUB, :] - fx_ref[p - 1 : p - 1 + SUB, :]
                new = u + across + (down - v_ref[at, :])
                v_ref[at, :] = down
                dst[r, p : p + SUB, :] = jnp.where(active, new, u)
            return carry

        lax.fori_loop(step, total - step, advance, 0)

    result = u0_ref if STEPS % 2 == 0 else u1_ref
    per_block = rows // out_ref.shape[0]
    for i in range(rows):
        for j in range(own // LANES):
            p = SUB + chunk * own + j * LANES - low
            at = (i % per_block) * own + j * LANES
            out_ref[i // per_block, :, at : at + LANES] = jnp.transpose(
                result[STEPS + i, p : p + LANES, :]
            )


def diffuse(chunk, chunks, start_field, edges, ids_wide, run_rows, ends, blocks):
    runs, rows, cols = start_field.shape
    total = rows + 2 * STEPS
    low, high, _ = spans(cols, chunks)[chunk]
    width = high - low
    tiles = -(-high // LANES) - low // LANES
    own = cols // chunks
    edges = list(edges[chunk]) + (list(edges[chunk - 1]) if chunk else [])
    state = pltpu.VMEM((total, width + 2 * SUB, runs), F32)
    return pl.pallas_call(
        functools.partial(diffuse_kernel, chunk, chunks),
        in_specs=[pl.BlockSpec(memory_space=pltpu.SMEM), ANY, SPACE, SPACE] + [SPACE] * len(edges),
        out_specs=SPACE,
        out_shape=jax.ShapeDtypeStruct((blocks, runs, rows * own // blocks), F32),
        scratch_shapes=[
            pltpu.VMEM((runs, rows, tiles * LANES), F32),
            state,
            state,
            state,
            pltpu.VMEM((total, width, runs), F32),
            pltpu.VMEM((total, width, runs), F32),
            pltpu.VMEM((width + 2 * SUB, runs), F32),
            pltpu.VMEM((width, runs), F32),
            pltpu.SemaphoreType.DMA,
        ],
        cost_estimate=cost(100 * runs * total * width, 12 * runs * total * width),
        name="diffuse",
    )(ends, start_field, ids_wide, run_rows, *edges)


PITCH = 80


def hidden_kernel(
    runs_ref, layer_ref, hidden_ref, hidden_t_ref, gain_t_ref, project_ref, f_ref, ft_ref, rest_ref, stack_ref
):
    depth, runs = ft_ref.shape
    n_feat, block = layer_ref.shape
    n_exact = n_feat - 1
    steep = runs_ref[LEVELS + 1 : LEVELS + 2]
    rest = steep - steep.astype(BF16).astype(F32)

    @pl.when(pl.program_id(0) == 0)
    def _():
        held = runs_ref[...]
        row = lax.broadcasted_iota(jnp.int32, (depth, held.shape[0]), 0)
        col = lax.broadcasted_iota(jnp.int32, (depth, held.shape[0]), 1)

        def place(row):
            return jnp.where(row < 3 * PITCH, row % PITCH, PITCH)

        n_level = LEVELS * LEVELS
        at = place(row)
        source = jnp.where(
            at < n_level,
            at // LEVELS,
            jnp.where(at < n_exact, LEVELS, jnp.where(at == n_exact, LEVELS + 1, -1)),
        )
        spread = jnp.where(col == source, 1.0, 0.0).astype(BF16)
        value = jnp.dot(spread, held.astype(BF16), preferred_element_type=F32)
        at = place(lax.broadcasted_iota(jnp.int32, (depth, runs), 0))
        wanted = jnp.where(at < n_level, at % LEVELS, at - n_level + 1).astype(F32)
        feats = jnp.where(at < n_exact, jnp.where(value == wanted, 1.0, 0.0), value)
        ft_ref[...] = feats.astype(BF16)
        f_ref[...] = jnp.transpose(feats).astype(BF16)
        line = lax.broadcasted_iota(jnp.int32, (LANES, runs), 0)
        wide_rest = jnp.broadcast_to(rest, (LANES, runs))
        project = jnp.where(
            line < n_feat, feats[:LANES], jnp.where(line == n_feat, wide_rest, 0.0)
        )
        project_ref[...] = jnp.transpose(project).astype(BF16)
        rest_ref[...] = jnp.transpose(wide_rest)
        stack_ref[...] = jnp.zeros(stack_ref.shape, F32)

    layer = layer_ref[...]
    left = layer
    for piece in range(3):
        part = left.astype(BF16).astype(F32)
        stack_ref[piece * PITCH : piece * PITCH + n_feat, :] = part
        left = left - part
    stack = stack_ref[...]
    column = jnp.concatenate([rest_ref[...]] * (block // LANES), axis=1)
    pre = jnp.dot(f_ref[...], stack.astype(BF16), preferred_element_type=F32)
    pre = pre + column * layer[n_exact:n_feat, :]
    hidden_ref[...] = (pre * jax.nn.sigmoid(pre)).astype(BF16)
    stack_t = jnp.transpose(stack)
    last = sum(stack_t[:, p * PITCH + n_exact : p * PITCH + n_feat] for p in range(3))
    pre = jnp.dot(stack_t.astype(BF16), ft_ref[...], preferred_element_type=F32)
    pre = pre + last * rest
    logistic = jax.nn.sigmoid(pre)
    hidden_t_ref[...] = (pre * logistic).astype(BF16)
    gain_t_ref[...] = logistic * (1.0 + pre * (1.0 - logistic))


def hidden_units(run_rows, layer, block=512):
    held, runs = run_rows.shape
    n_feat, hid = layer.shape
    depth = -(-3 * PITCH // LANES) * LANES
    return pl.pallas_call(
        hidden_kernel,
        grid=(hid // block,),
        in_specs=[
            pl.BlockSpec((held, runs), lambda i: (0, 0)),
            pl.BlockSpec((n_feat, block), lambda i: (0, i)),
        ],
        out_specs=[
            pl.BlockSpec((runs, block), lambda i: (0, i)),
            pl.BlockSpec((block, runs), lambda i: (i, 0)),
            pl.BlockSpec((block, runs), lambda i: (i, 0)),
            pl.BlockSpec((runs, LANES), lambda i: (0, 0)),
        ],
        out_shape=[
            jax.ShapeDtypeStruct((runs, hid), BF16),
            jax.ShapeDtypeStruct((hid, runs), BF16),
            jax.ShapeDtypeStruct((hid, runs), F32),
            jax.ShapeDtypeStruct((runs, LANES), BF16),
        ],
        scratch_shapes=[
            pltpu.VMEM((runs, depth), BF16),
            pltpu.VMEM((depth, runs), BF16),
            pltpu.VMEM((runs, LANES), F32),
            pltpu.VMEM((depth, block), F32),
        ],
        cost_estimate=cost(4 * runs * hid * depth, 10 * runs * hid, 4 * runs * hid),
        name="hidden_units",
    )(run_rows, layer)


def predict_kernel(hidden_ref, weight_ref, bias_ref, out_ref):
    out_ref[...] = (
        jnp.dot(hidden_ref[...], weight_ref[...], preferred_element_type=F32) + bias_ref[...]
    )


def predict(hidden, weight, bias, block=512):
    runs, hid = hidden.shape
    cells = weight.shape[1]
    return pl.pallas_call(
        predict_kernel,
        grid=(cells // block,),
        in_specs=[
            pl.BlockSpec((runs, hid), lambda i: (0, 0)),
            pl.BlockSpec((hid, block), lambda i: (0, i)),
            pl.BlockSpec((1, block), lambda i: (0, i)),
        ],
        out_specs=pl.BlockSpec((runs, block), lambda i: (0, i)),
        out_shape=jax.ShapeDtypeStruct((runs, cells), F32),
        cost_estimate=cost(2 * runs * hid * cells, 2 * hid * cells + 4 * runs * cells),
        name="predict",
    )(hidden, weight, bias)


def learn_kernel(last, has_before, scale, *refs):
    guess_ref, target_ref, weight_ref, bias_ref, gain_ref, feats_ref = refs[:6]
    rest = refs[6:]
    if has_before:
        acc_in_ref = rest[3]
        rest = rest[4:]
    misfit_ref, slope_ref, bias_out_ref, acc_ref, back_ref = rest
    sources, per_source, own = target_ref.shape
    step = pl.program_id(0)
    total = jnp.zeros((1, own), F32)
    for s in range(sources):
        at = slice(s * per_source, (s + 1) * per_source)
        error = guess_ref[at, :] - target_ref[s]
        misfit_ref[at, :] = error.astype(BF16)
        slope = (error * scale).astype(BF16)
        slope_ref[at, :] = slope
        total = total + jnp.sum(slope.astype(F32), axis=0, keepdims=True)
    bias_out_ref[...] = bias_ref[...] - 0.5 * total
    back = lax.dot_general(
        weight_ref[...], slope_ref[...], (((1,), (1,)), ((), ())), preferred_element_type=F32
    )

    @pl.when(step == 0)
    def _():
        back_ref[...] = back

    @pl.when(step > 0)
    def _():
        back_ref[...] += back

    @pl.when(step == pl.num_programs(0) - 1)
    def _():
        full = back_ref[...] * gain_ref[...]
        high = full.astype(BF16)
        low = (full - high.astype(F32)).astype(BF16)
        feats = feats_ref[...]
        acc = jnp.dot(high, feats, preferred_element_type=F32)
        acc = acc + jnp.dot(low, feats, preferred_element_type=F32)
        if has_before:
            acc = acc + acc_in_ref[...]
        if last:
            acc_ref[...] = jnp.transpose(acc)[: acc_ref.shape[0], :]
        else:
            acc_ref[...] = acc


def learn_chunk(chunk, chunks, cols, guess, target, weight, bias, gain_t, feats, before, kept, scale):
    hid, cells = weight.shape
    sources, per_source, mine = target.shape
    runs = sources * per_source
    own = cols // chunks
    last, has_before = chunk == chunks - 1, before is not None
    strip = lambda i: (0, i * chunks + chunk)
    in_specs = [
        pl.BlockSpec((runs, own), strip),
        pl.BlockSpec((sources, per_source, own), lambda i: (0, 0, i)),
        pl.BlockSpec((hid, own), strip),
        pl.BlockSpec((1, own), strip),
        SPACE,
        SPACE,
    ]
    args = [guess, target, weight, bias, gain_t, feats]
    aliases = {}
    if has_before:
        in_specs += [ANY, ANY, ANY, SPACE]
        args += list(before)
        aliases = {6: 0, 7: 1, 8: 2}
    acc_shape = (kept, hid) if last else (hid, LANES)
    return pl.pallas_call(
        functools.partial(learn_kernel, last, has_before, scale),
        grid=(mine // own,),
        in_specs=in_specs,
        out_specs=[
            pl.BlockSpec((runs, own), strip),
            pl.BlockSpec((runs, own), strip),
            pl.BlockSpec((1, own), strip),
            pl.BlockSpec(acc_shape, lambda i: (0, 0)),
        ],
        out_shape=[
            jax.ShapeDtypeStruct((runs, cells), BF16),
            jax.ShapeDtypeStruct((runs, cells), BF16),
            jax.ShapeDtypeStruct((1, cells), F32),
            jax.ShapeDtypeStruct(acc_shape, F32),
        ],
        scratch_shapes=[pltpu.VMEM((hid, runs), F32)],
        input_output_aliases=aliases,
        cost_estimate=cost(2 * runs * hid * (mine + 2 * LANES), 2 * hid * mine + 12 * runs * mine),
        name="learn",
    )(*args)


def update_kernel(hidden_t_ref, slope_ref, weight_ref, out_ref):
    grad = jnp.dot(hidden_t_ref[...], slope_ref[...], preferred_element_type=F32)
    out_ref[...] = (weight_ref[...].astype(F32) - 0.5 * grad).astype(BF16)


def update(hidden_t, slope, weight, block=256):
    hid, cells = weight.shape
    runs = slope.shape[0]
    return pl.pallas_call(
        update_kernel,
        grid=(hid // block,),
        in_specs=[
            pl.BlockSpec((block, runs), lambda i: (i, 0)),
            pl.BlockSpec((runs, cells), lambda i: (0, 0)),
            pl.BlockSpec((block, cells), lambda i: (i, 0)),
        ],
        out_specs=pl.BlockSpec((block, cells), lambda i: (i, 0)),
        out_shape=jax.ShapeDtypeStruct((hid, cells), BF16),
        cost_estimate=cost(2 * runs * hid * cells, 4 * hid * cells + 4 * runs * cells),
        name="update",
    )(hidden_t, slope, weight)


def halve(x, axis, bit):
    size = lax.axis_size(axis)
    upper = (lax.axis_index(axis) & bit) != 0
    half = x.shape[0] // 2
    kept = lax.dynamic_slice_in_dim(x, jnp.where(upper, half, 0), half, 0)
    sent = lax.dynamic_slice_in_dim(x, jnp.where(upper, 0, half), half, 0)
    return kept + lax.ppermute(sent, axis, [(i, i ^ bit) for i in range(size)])


def rejoin(x, axis, bit):
    size = lax.axis_size(axis)
    upper = (lax.axis_index(axis) & bit) != 0
    other = lax.ppermute(x, axis, [(i, i ^ bit) for i in range(size)])
    return jnp.where(
        upper, jnp.concatenate([other, x], axis=0), jnp.concatenate([x, other], axis=0)
    )


def sum_over_devices(x):
    grp, tile = lax.axis_size("grp"), lax.axis_size("tile")
    bits = [1 << b for b in range(grp.bit_length() - 1)]
    for bit in bits:
        x = halve(x, "grp", bit)
    n = x.shape[0] // tile
    x = lax.all_to_all(x.reshape(tile, n, LANES), "tile", 0, 0, tiled=True)
    x = jnp.sum(x.reshape(tile, n, LANES), axis=0)
    x = lax.all_to_all(jnp.broadcast_to(x[None], (tile, n, LANES)), "tile", 0, 0, tiled=True)
    x = x.reshape(tile * n, LANES)
    for bit in bits[::-1]:
        x = rejoin(x, "grp", bit)
    return x


def on_device(
    start_field, class_ids, run_levels, steepness, step_pick, input_layer, output_layer, output_bias
):
    local_runs, _, cols = start_field.shape
    n_grp, n_tile = lax.axis_size("grp"), lax.axis_size("tile")
    tile = lax.axis_index("tile")
    first_run = lax.axis_index("grp") * local_runs
    chunks = CHUNKS
    parts = spans(cols, chunks)
    runs_total, classes = run_levels.shape
    n_feat, hid = input_layer.shape

    up = [(i, i + 1) for i in range(n_tile - 1)]
    down = [(j, i) for i, j in up]
    packed = pack_edges(start_field, class_ids, parts)
    edges = []
    for c in range(chunks):
        top, bottom = packed[2 * c], packed[2 * c + 1]
        above = lax.ppermute(bottom, "tile", up)
        below = lax.ppermute(top, "tile", down)
        edges.append((above, below))

    run_rows = jnp.concatenate(
        [
            run_levels.T.astype(F32),
            step_pick[None, :].astype(F32),
            steepness[None, :],
            jnp.zeros((2 * LEVELS - classes - 2, runs_total), F32),
        ],
        axis=0,
    )
    run_rows_here = lax.dynamic_slice_in_dim(run_rows, first_run, local_runs, 1)
    ends = jnp.stack([(tile > 0).astype(F32), (tile < n_tile - 1).astype(F32)])
    brought = STEPS * (parts[0][1] - parts[0][2])
    ids_wide = jnp.concatenate(
        [
            edges[0][0][brought:].reshape(STEPS, cols).astype(jnp.int32),
            class_ids,
            edges[0][1][brought:].reshape(STEPS, cols).astype(jnp.int32),
        ],
        axis=0,
    )[:, None, :]

    hidden, hidden_t, gain_t, project = hidden_units(run_rows, input_layer)
    bias_row = output_bias[None, :]
    guess = predict(hidden, output_layer, bias_row)
    kept = -(-(n_feat + 1) // SUB) * SUB

    state = None
    scale = 2.0 / runs_total
    for c in range(chunks):
        snap = diffuse(c, chunks, start_field, edges, ids_wide, run_rows_here, ends, n_grp)
        target = lax.all_to_all(snap, "grp", split_axis=0, concat_axis=0, tiled=True)
        state = learn_chunk(
            c, chunks, cols, guess, target, output_layer, bias_row, gain_t, project, state, kept, scale
        )
    misfit, slope, bias_next, partial = state
    output_next = update(hidden_t, slope, output_layer)
    flat = partial.reshape(-1, LANES)
    unit = SUB * n_grp * n_tile
    padded = -(-flat.shape[0] // unit) * unit
    flat = jnp.pad(flat, ((0, padded - flat.shape[0]), (0, 0)))
    total = sum_over_devices(flat)[: kept * hid // LANES].reshape(kept, hid)
    grad_in = jnp.concatenate(
        [total[: n_feat - 1], total[n_feat - 1 : n_feat] + total[n_feat : n_feat + 1]], axis=0
    )
    input_next = input_layer - 2.0 * grad_in
    return misfit, output_next, bias_next.reshape(-1), input_next


def solution(mesh):
    in_specs = (
        P("grp", "tile", None),
        P("tile", None),
        P(),
        P(),
        P(),
        P(),
        P(None, ("grp", "tile")),
        P(("grp", "tile")),
    )
    out_specs = (P(None, ("grp", "tile")), P(None, ("grp", "tile")), P(("grp", "tile")), P())

    return jax.shard_map(
        on_device, mesh=mesh, in_specs=in_specs, out_specs=out_specs, check_vma=False
    )
```

profile of v0, /device:TPU:0, one launch (start us, length us, event | category | flops | bytes accessed | tf_op | source)
XLA Modules:
  0.0 194.1 jit_solution(7206226466328874032)
XLA Ops:
  0.7 4.6 %pack_edges.1 = (f32[1072,128]{1,0:T(8,128)}, f32[1072,128]{1,0:T(8,128)}, f32[992,128]{1,0:T(8,128)}, f32[992,128]{1,0:T(8,128)}) custom-call(f32[128,16,512]{2,1,0:T(8,128)} %field_ref.5, s32[16,512]{1,0:T(8,128)} %ids_ref.1), custom_call_target="tpu_custom_call" | custom-call | bytes 6291456 | tf_op jit(solution)/shard_map/pack_edges/pallas_call | solution.py:65
  5.2 4.9 %collective-permute-start = (f32[1072,128]{1,0:T(8,128)}, f32[1072,128]{1,0:T(8,128)S(1)}, u32[]{:S(2)}, u32[]{:S(2)}) collective-permute-start(f32[1072,128]{1,0:T(8,128)} %get-tuple-element.21), channel_id=1, source_target_pairs={{0,1},{1,2},{2,3},{3,4},{4,5},{5,6},{6,7},{8,9},{9,10},{10,11},{11... | collective-permute-start | bytes 1646600 | tf_op jit(solution)/shard_map/ppermute | solution.py:517
  10.2 1.3 collective-permute-start.1
  11.6 0.6 add_convert_fusion.ends_ref
  12.3 0.6 constant_dynamic-slice_fusion.1.runs_ref
  12.9 21.0 %collective-permute-done.refs_2_.refs_0_ = f32[1072,128]{1,0:T(8,128)S(1)} collective-permute-done((f32[1072,128]{1,0:T(8,128)}, f32[1072,128]{1,0:T(8,128)S(1)}, u32[]{:S(2)}, u32[]{:S(2)}) %collective-permute-start) | collective-permute-done | bytes 548896 | tf_op jit(solution)/shard_map/ppermute | solution.py:517
  34.0 0.9 broadcast_in_dim.22.ids_ref
  34.9 15.3 %diffuse.3 = f32[4,128,1024]{2,1,0:T(8,128)} custom-call(f32[2]{0:T(128)} %add_convert_fusion.ends_ref, f32[128,16,512]{2,1,0:T(8,128)} %field_ref.5, s32[24,1,512]{2,1,0:T(1,128)} %broadcast_in_dim.22.ids_ref, f32[16,128]{1,0:T(8,128)} %constant_dynamic-slice_fusion.1.runs_ref, f32[1072,128]{1,0:T(8,128)} %copy-done.1, f32[1072,128]{1,0:T(8,128)} %copy-done.2), custom_call_target="tpu_custom_call" | custom-call | flops 81100800 | bytes 9732096 | tf_op jit(solution)/shard_map/diffuse/pallas_call | solution.py:209
  50.2 3.6 %all-to-all-start.1 = ((f32[4,128,1024]{2,1,0:T(8,128)}), f32[4,128,1024]{2,1,0:T(8,128)S(1)}, u32[]{:S(2)}, u32[]{:S(2)}) async-start(f32[4,128,1024]{2,1,0:T(8,128)} %diffuse.3), calls=%async_computation.1 | async-start | bytes 4194304 | tf_op jit(solution)/shard_map/all_to_all | solution.py:551
  53.8 4.3 %collective-permute-start.2 = (f32[992,128]{1,0:T(8,128)}, f32[992,128]{1,0:T(8,128)S(1)}, u32[]{:S(2)}, u32[]{:S(2)}) collective-permute-start(f32[992,128]{1,0:T(8,128)} %get-tuple-element.23), channel_id=1, source_target_pairs={{0,1},{1,2},{2,3},{3,4},{4,5},{5,6},{6,7},{8,9},{9,10},{10,11},{11... | collective-permute-start | bytes 1523720 | tf_op jit(solution)/shard_map/ppermute | solution.py:517
  58.2 1.3 collective-permute-start.3
  59.5 21.3 %collective-permute-done.2.refs_0_ = f32[992,128]{1,0:T(8,128)S(1)} collective-permute-done((f32[992,128]{1,0:T(8,128)}, f32[992,128]{1,0:T(8,128)S(1)}, u32[]{:S(2)}, u32[]{:S(2)}) %collective-permute-start.2) | collective-permute-done | bytes 507936 | tf_op jit(solution)/shard_map/ppermute | solution.py:517
  80.8 0.8 copy-done.4
  81.6 0.8 copy-done.5
  82.4 15.6 %diffuse.2 = f32[4,128,1024]{2,1,0:T(8,128)} custom-call(f32[2]{0:T(128)} %add_convert_fusion.ends_ref, f32[128,16,512]{2,1,0:T(8,128)} %field_ref.5, s32[24,1,512]{2,1,0:T(1,128)} %broadcast_in_dim.22.ids_ref, f32[16,128]{1,0:T(8,128)} %constant_dynamic-slice_fusion.1.runs_ref, f32[992,128]{1,0:T(8,128)} %copy-done.4, f32[992,128]{1,0:T(8,128)} %copy-done.5, ...), custom_call_target="tpu_custom_call" | custom-call | flops 81100800 | bytes 9732096 | tf_op jit(solution)/shard_map/diffuse/pallas_call | solution.py:209
  98.0 1.3 copy-done
  99.4 4.7 %all-to-all-start = ((f32[4,128,1024]{2,1,0:T(8,128)}), f32[4,128,1024]{2,1,0:T(8,128)}, u32[]{:S(2)}, u32[]{:S(2)}) async-start(f32[4,128,1024]{2,1,0:T(8,128)} %diffuse.2), calls=%async_computation | async-start | bytes 4194304 | tf_op jit(solution)/shard_map/all_to_all | solution.py:551
  104.1 6.3 %hidden_units.1 = (bf16[512,2048]{1,0:T(8,128)(2,1)}, bf16[2048,512]{1,0:T(8,128)(2,1)}, f32[2048,512]{1,0:T(8,128)}, bf16[512,128]{1,0:T(8,128)(2,1)}) custom-call(f32[16,512]{1,0:T(8,128)} %copy-done.7, f32[69,2048]{1,0:T(8,128)} %layer_ref.1), custom_call_target="tpu_custom_call" | custom-call | flops 1073741824 | bytes 10485760 | tf_op jit(solution)/shard_map/hidden_units/pallas_call | solution.py:298
  110.4 9.2 %predict.1.refs_0_ = f32[512,2048]{1,0:T(8,128)} custom-call(bf16[512,2048]{1,0:T(8,128)(2,1)} %get-tuple-element.20.hidden_ref, bf16[2048,2048]{1,0:T(8,128)(2,1)} %weight_ref.3, f32[1,2048]{1,0:T(1,128)} %bitcast.14), custom_call_target="tpu_custom_call" | custom-call | flops 4294967296 | bytes 12582912 | tf_op jit(solution)/shard_map/predict/pallas_call | solution.py:337
  119.6 10.8 %learn.2 = (bf16[512,2048]{1,0:T(8,128)(2,1)}, bf16[512,2048]{1,0:T(8,128)(2,1)}, f32[1,2048]{1,0:T(1,128)}, f32[2048,128]{1,0:T(8,128)}) custom-call(f32[512,2048]{1,0:T(8,128)} %predict.1.refs_0_, f32[4,128,1024]{2,1,0:T(8,128)} %copy-done, bf16[2048,2048]{1,0:T(8,128)(2,1)} %weight_ref.3, f32[1,2048]{1,0:T(1,128)} %bitcast.15, ...), custom_call_target="tpu_custom_call" | custom-call | flops 2684354560 | bytes 10485760 | tf_op jit(solution)/shard_map/learn/pallas_call | solution.py:420
  130.4 11.0 %learn.3 = (bf16[512,2048]{1,0:T(8,128)(2,1)}, bf16[512,2048]{1,0:T(8,128)(2,1)}, f32[1,2048]{1,0:T(1,128)}, f32[72,2048]{1,0:T(8,128)}) custom-call(f32[512,2048]{1,0:T(8,128)} %predict.1.refs_0_, f32[4,128,1024]{2,1,0:T(8,128)} %all-to-all-done.refs_1_, bf16[2048,2048]{1,0:T(8,128)(2,1)} %weight_ref.3, ...), custom_call_target="tpu_custom_call", output_to_operand_aliasing={{0}: (6, {}), {1}: (7, {}), {2}: (8, {})} | custom-call | flops 2684354560 | bytes 10485760 | tf_op jit(solution)/shard_map/learn/pallas_call | solution.py:420
  141.4 1.2 reshape.52
  142.9 1.4 collective-permute-done.4
  144.4 1.8 collective-permute-start.5
  146.2 4.6 %collective-permute-done.5 = f32[320,128]{1,0:T(8,128)S(1)} collective-permute-done((f32[320,128]{1,0:T(8,128)S(1)}, f32[320,128]{1,0:T(8,128)S(1)}, u32[]{:S(2)}, u32[]{:S(2)}) %collective-permute-start.5) | collective-permute-done | bytes 163872 | tf_op jit(solution)/shard_map/ppermute | solution.py:472
  150.8 13.9 %all_to_all.20 = f32[8,40,128]{2,1,0:T(8,128)S(1)} all-to-all(f32[8,40,128]{2,1,0:T(8,128)S(1)} %bitcast.11), channel_id=1, replica_groups=mesh['grp'=4,'tile'=8] {'tile'}, dimensions={0} | all-to-all | bytes 327680 | tf_op jit(solution)/shard_map/all_to_all | solution.py:490
  164.8 10.0 %all_to_all.21 = f32[8,40,128]{2,1,0:T(8,128)S(1)} all-to-all(f32[8,40,128]{2,1,0:T(8,128)S(1)} %broadcast_in_dim.23), channel_id=1, replica_groups=mesh['grp'=4,'tile'=8] {'tile'}, dimensions={0} | all-to-all | bytes 327680 | tf_op jit(solution)/shard_map/all_to_all | solution.py:492
  174.7 1.7 collective-permute-start.6
  176.4 3.7 %collective-permute-done.6 = f32[320,128]{1,0:T(8,128)S(1)} collective-permute-done((f32[320,128]{1,0:T(8,128)S(1)}, f32[320,128]{1,0:T(8,128)S(1)}, u32[]{:S(2)}, u32[]{:S(2)}) %collective-permute-start.6) | collective-permute-done | bytes 163872 | tf_op jit(solution)/shard_map/ppermute | solution.py:478
  180.2 12.0 %update.1 = bf16[2048,2048]{1,0:T(8,128)(2,1)} custom-call(bf16[2048,512]{1,0:T(8,128)(2,1)} %get-tuple-element.32.hidden_t_ref, bf16[512,2048]{1,0:T(8,128)(2,1)} %get-tuple-element.33.slope_ref, bf16[2048,2048]{1,0:T(8,128)(2,1)} %weight_ref.3), custom_call_target="tpu_custom_call" | custom-call | flops 4294967296 | bytes 20971520 | tf_op jit(solution)/shard_map/update/pallas_call | solution.py:451
  192.4 0.9 copy-done.3
  193.2 0.9 fusion
  (46 shorter events, 1.0 us)
Async XLA Ops:
  0.6 33.3 %copy-start.6 = (s32[16,512]{1,0:T(8,128)S(1)}, s32[16,512]{1,0:T(8,128)}, u32[]{:S(2)}) copy-start(s32[16,512]{1,0:T(8,128)} %ids_ref.1) | copy-start | bytes 98308
  0.6 10.8 %copy-start.9 = (s32[512]{0:T(512)S(1)}, s32[512]{0:T(512)}, u32[]{:S(2)}) copy-start(s32[512]{0:T(512)} %param.12) | copy-start | bytes 6148
  0.7 11.6 %copy-start.8 = (s32[512,8]{0,1:T(8,128)S(1)}, s32[512,8]{0,1:T(8,128)}, u32[]{:S(2)}) copy-start(s32[512,8]{0,1:T(8,128)} %param.10) | copy-start | bytes 49156
  0.7 11.6 %copy-start.10 = (f32[512]{0:T(512)S(1)}, f32[512]{0:T(512)}, u32[]{:S(2)}) copy-start(f32[512]{0:T(512)} %param.11) | copy-start | bytes 6148
  5.2 28.7 %collective-permute-start = (f32[1072,128]{1,0:T(8,128)}, f32[1072,128]{1,0:T(8,128)S(1)}, u32[]{:S(2)}, u32[]{:S(2)}) collective-permute-start(f32[1072,128]{1,0:T(8,128)} %get-tuple-element.21), channel_id=1, source_target_pairs={{0,1},{1,2},{2,3},{3,4},{4,5},{5,6},{6,7},{8,9},{9,10},{10,11},{11... | collective-permute-start | bytes 1646600 | tf_op jit(solution)/shard_map/ppermute | solution.py:517
  10.2 23.8 %collective-permute-start.1 = (f32[1072,128]{1,0:T(8,128)}, f32[1072,128]{1,0:T(8,128)S(1)}, u32[]{:S(2)}, u32[]{:S(2)}) collective-permute-start(f32[1072,128]{1,0:T(8,128)} %get-tuple-element.22), channel_id=1, source_target_pairs={{1,0},{2,1},{3,2},{4,3},{5,4},{6,5},{7,6},{9,8},{10,9},{11,10},{12... | collective-permute-start | bytes 1646600 | tf_op jit(solution)/shard_map/ppermute | solution.py:518
  12.3 37.9 %copy-start.7 = (f32[16,512]{1,0:T(8,128)}, f32[16,512]{1,0:T(8,128)S(1)}, u32[]{:S(2)}) copy-start(f32[16,512]{1,0:T(8,128)S(1)} %maximum_maximum_fusion.runs_ref) | copy-start | bytes 98308
  33.9 0.9 copy-start.1
  33.9 1.0 copy-start.2
  50.2 47.8 %all-to-all-start.1 = ((f32[4,128,1024]{2,1,0:T(8,128)}), f32[4,128,1024]{2,1,0:T(8,128)S(1)}, u32[]{:S(2)}, u32[]{:S(2)}) async-start(f32[4,128,1024]{2,1,0:T(8,128)} %diffuse.3), calls=%async_computation.1 | async-start | bytes 4194304 | tf_op jit(solution)/shard_map/all_to_all | solution.py:551
  53.8 26.9 %collective-permute-start.2 = (f32[992,128]{1,0:T(8,128)}, f32[992,128]{1,0:T(8,128)S(1)}, u32[]{:S(2)}, u32[]{:S(2)}) collective-permute-start(f32[992,128]{1,0:T(8,128)} %get-tuple-element.23), channel_id=1, source_target_pairs={{0,1},{1,2},{2,3},{3,4},{4,5},{5,6},{6,7},{8,9},{9,10},{10,11},{11... | collective-permute-start | bytes 1523720 | tf_op jit(solution)/shard_map/ppermute | solution.py:517
  58.2 22.6 %collective-permute-start.3 = (f32[992,128]{1,0:T(8,128)}, f32[992,128]{1,0:T(8,128)S(1)}, u32[]{:S(2)}, u32[]{:S(2)}) collective-permute-start(f32[992,128]{1,0:T(8,128)} %get-tuple-element.24), channel_id=1, source_target_pairs={{1,0},{2,1},{3,2},{4,3},{5,4},{6,5},{7,6},{9,8},{10,9},{11,10},{12... | collective-permute-start | bytes 1523720 | tf_op jit(solution)/shard_map/ppermute | solution.py:518
  80.8 0.8 copy-start.4
  81.6 0.8 copy-start.5
  98.0 1.4 copy-start
  99.4 31.0 %all-to-all-start = ((f32[4,128,1024]{2,1,0:T(8,128)}), f32[4,128,1024]{2,1,0:T(8,128)}, u32[]{:S(2)}, u32[]{:S(2)}) async-start(f32[4,128,1024]{2,1,0:T(8,128)} %diffuse.2), calls=%async_computation | async-start | bytes 4194304 | tf_op jit(solution)/shard_map/all_to_all | solution.py:551
  142.6 1.7 collective-permute-start.4
  144.4 6.4 %collective-permute-start.5 = (f32[320,128]{1,0:T(8,128)S(1)}, f32[320,128]{1,0:T(8,128)S(1)}, u32[]{:S(2)}, u32[]{:S(2)}) collective-permute-start(f32[320,128]{1,0:T(8,128)S(1)} %constant_dynamic-slice_fusion), channel_id=1, source_target_pairs={{0,16},{8,24},{16,0},{24,8},{1,17},{9,25},{17,1},{25,9},{2,18},{10... | collective-permute-start | bytes 491528 | tf_op jit(solution)/shard_map/ppermute | solution.py:472
  174.7 5.3 %collective-permute-start.6 = (f32[320,128]{1,0:T(8,128)S(1)}, f32[320,128]{1,0:T(8,128)S(1)}, u32[]{:S(2)}, u32[]{:S(2)}) collective-permute-start(f32[320,128]{1,0:T(8,128)S(1)} %bitcast.12), channel_id=1, source_target_pairs={{0,16},{8,24},{16,0},{24,8},{1,17},{9,25},{17,1},{25,9},{2,18},{10... | collective-permute-start | bytes 491528 | tf_op jit(solution)/shard_map/ppermute | solution.py:478
  180.1 12.1 %collective-permute-start.7 = (f32[640,128]{1,0:T(8,128)S(1)}, f32[640,128]{1,0:T(8,128)S(1)}, u32[]{:S(2)}, u32[]{:S(2)}) collective-permute-start(f32[640,128]{1,0:T(8,128)S(1)} %maximum_select_fusion.1), channel_id=1, source_target_pairs={{0,8},{8,0},{16,24},{24,16},{1,9},{9,1},{17,25},{25,17},{2,10},{10... | collective-permute-start | bytes 983048 | tf_op jit(solution)/shard_map/ppermute | solution.py:478
  192.2 1.1 copy-start.3
where the time goes:
time: 195 us; the launch traced here: 194 us
  Pallas kernels  84.8 us (43%)
  waiting for transfers between devices  51.9 us (27%)
  starting transfers between devices  24 us (12%)
  blocking collectives  23.9 us (12%)
  local copies, waits for them, and re-layouts  6.79 us (3%)
    ppermute x2, waiting for transfers between devices, on_device(): above = lax.ppermute(bottom, 'tile', up)  42.3 us
    pallas_call x2, Pallas kernels, diffuse(): pl.pallas_call(functools.partial(diffuse_kernel, chunk, chunks), in_specs...  30.9 us
    pallas_call x2, Pallas kernels, learn_chunk(): pl.pallas_call(functools.partial(learn_kernel, last, has_before, scale),...  21.8 us
    all_to_all x1, blocking collectives, sum_over_devices(): x = lax.all_to_all(x.reshape(tile, n, LANES), 'tile', 0, 0, tiled=True)  13.9 us
    pallas_call x1, Pallas kernels, update(): pl.pallas_call(update_kernel, grid=(hid // block,), in_specs=[pl.BlockSpe...  12 us
    all_to_all x1, blocking collectives, sum_over_devices(): lax.all_to_all(jnp.broadcast_to(x[None], (tile, n, LANES)), 'tile', 0, 0,...  9.96 us
    ppermute x2, starting transfers between devices, on_device(): above = lax.ppermute(bottom, 'tile', up)  9.23 us
    pallas_call x1, Pallas kernels, predict(): pl.pallas_call(predict_kernel, grid=(cells // block,), in_specs=[pl.Block...  9.22 us
  transfers between devices with their start and end apart: 10, of which 5 were waited for; matrix products, arithmetic and copies ran while one was open for 1% of the time, Pallas kernels for 28%

commit v1 on v0

--- a/solution.py
+++ b/solution.py
@@ -17,6 +17,7 @@
 BF16 = jnp.bfloat16
 SPACE = pl.BlockSpec(memory_space=pltpu.VMEM)
 ANY = pl.BlockSpec(memory_space=pl.ANY)
+SCALARS = pl.BlockSpec(memory_space=pltpu.SMEM)
 
 
 def cost(flops, nbytes, transcendentals=0):
@@ -72,11 +73,9 @@
     )(start_field, ids)
 
 
-def diffuse_kernel(chunk, chunks, ends_ref, field_ref, ids_ref, runs_ref, *refs):
-    edges, (out_ref, raw_ref, u0_ref, u1_ref, d_ref, a_ref, b_ref, fx_ref, v_ref, sem) = (
-        refs[:-10],
-        refs[-10:],
-    )
+def diffuse_kernel(chunk, chunks, ends_ref, grp_ref, field_ref, ids_ref, runs_ref, *refs):
+    edges, outs = refs[: 2 + 2 * (chunk > 0)], refs[2 + 2 * (chunk > 0) : -9]
+    raw_ref, u0_ref, u1_ref, d_ref, a_ref, b_ref, fx_ref, v_ref, sem = refs[-9:]
     cols = ids_ref.shape[2]
     rows = field_ref.shape[1]
     total = rows + 2 * STEPS
@@ -187,17 +186,17 @@
         lax.fori_loop(step, total - step, advance, 0)
 
     result = u0_ref if STEPS % 2 == 0 else u1_ref
-    per_block = rows // out_ref.shape[0]
-    for i in range(rows):
-        for j in range(own // LANES):
-            p = SUB + chunk * own + j * LANES - low
-            at = (i % per_block) * own + j * LANES
-            out_ref[i // per_block, :, at : at + LANES] = jnp.transpose(
-                result[STEPS + i, p : p + LANES, :]
-            )
-
-
-def diffuse(chunk, chunks, start_field, edges, ids_wide, run_rows, ends, blocks):
+    per_block = rows // len(outs)
+    for offset, out_ref in enumerate(outs):
+        row = STEPS + (grp_ref[0] ^ offset) * per_block
+        for i in range(per_block):
+            for j in range(own // LANES):
+                p = SUB + chunk * own + j * LANES - low
+                at = i * own + j * LANES
+                out_ref[:, at : at + LANES] = jnp.transpose(result[row + i, p : p + LANES, :])
+
+
+def diffuse(chunk, chunks, start_field, edges, ids_wide, run_rows, ends, grp, blocks):
     runs, rows, cols = start_field.shape
     total = rows + 2 * STEPS
     low, high, _ = spans(cols, chunks)[chunk]
@@ -208,9 +207,9 @@
     state = pltpu.VMEM((total, width + 2 * SUB, runs), F32)
     return pl.pallas_call(
         functools.partial(diffuse_kernel, chunk, chunks),
-        in_specs=[pl.BlockSpec(memory_space=pltpu.SMEM), ANY, SPACE, SPACE] + [SPACE] * len(edges),
-        out_specs=SPACE,
-        out_shape=jax.ShapeDtypeStruct((blocks, runs, rows * own // blocks), F32),
+        in_specs=[SCALARS, SCALARS, ANY, SPACE, SPACE] + [SPACE] * len(edges),
+        out_specs=[SPACE] * blocks,
+        out_shape=[jax.ShapeDtypeStruct((runs, rows * own // blocks), F32)] * blocks,
         scratch_shapes=[
             pltpu.VMEM((runs, rows, tiles * LANES), F32),
             state,
@@ -224,7 +223,7 @@
         ],
         cost_estimate=cost(100 * runs * total * width, 12 * runs * total * width),
         name="diffuse",
-    )(ends, start_field, ids_wide, run_rows, *edges)
+    )(ends, grp, start_field, ids_wide, run_rows, *edges)
 
 
 PITCH = 80
@@ -349,19 +348,30 @@
     )(hidden, weight, bias)
 
 
-def learn_kernel(last, has_before, scale, *refs):
-    guess_ref, target_ref, weight_ref, bias_ref, gain_ref, feats_ref = refs[:6]
-    rest = refs[6:]
+def learn_kernel(last, has_before, scale, sources, *refs):
+    grp_ref, guess_ref = refs[:2]
+    targets, refs = refs[2 : 2 + sources], refs[2 + sources :]
+    weight_ref, bias_ref, gain_any, feats_ref = refs[:4]
+    refs = refs[4:]
+    if not last:
+        hidden_t_ref, refs = refs[0], refs[1:]
     if has_before:
-        acc_in_ref = rest[3]
-        rest = rest[4:]
-    misfit_ref, slope_ref, bias_out_ref, acc_ref, back_ref = rest
-    sources, per_source, own = target_ref.shape
-    step = pl.program_id(0)
+        acc_in_ref, refs = refs[2], refs[3:]
+    misfit_ref, bias_out_ref, acc_ref, extra_ref = refs[:4]
+    back_ref, gain_ref, sem = refs[4:7]
+    slope_ref = extra_ref if last else refs[7]
+    step, steps = pl.program_id(0), pl.num_programs(0)
+    load = pltpu.make_async_copy(gain_any, gain_ref, sem)
+
+    @pl.when(step == 0)
+    def _():
+        load.start()
+
+    per_source, own = targets[0].shape
     total = jnp.zeros((1, own), F32)
-    for s in range(sources):
-        at = slice(s * per_source, (s + 1) * per_source)
-        error = guess_ref[at, :] - target_ref[s]
+    for offset, target_ref in enumerate(targets):
+        at = pl.ds(pl.multiple_of((grp_ref[0] ^ offset) * per_source, per_source), per_source)
+        error = guess_ref[at, :] - target_ref[...]
         misfit_ref[at, :] = error.astype(BF16)
         slope = (error * scale).astype(BF16)
         slope_ref[at, :] = slope
@@ -379,8 +389,13 @@
     def _():
         back_ref[...] += back
 
-    @pl.when(step == pl.num_programs(0) - 1)
+    if not last:
+        grad = jnp.dot(hidden_t_ref[...], slope_ref[...], preferred_element_type=F32)
+        extra_ref[...] = (weight_ref[...].astype(F32) - 0.5 * grad).astype(BF16)
+
+    @pl.when(step == steps - 1)
     def _():
+        load.wait()
         full = back_ref[...] * gain_ref[...]
         high = full.astype(BF16)
         low = (full - high.astype(F32)).astype(BF16)
@@ -395,72 +410,90 @@
             acc_ref[...] = acc
 
 
-def learn_chunk(chunk, chunks, cols, guess, target, weight, bias, gain_t, feats, before, kept, scale):
+def learn(chunk, chunks, cols, grp, guess, targets, weight, bias, gain_t, feats, hidden_t, before, kept, scale):
     hid, cells = weight.shape
-    sources, per_source, mine = target.shape
+    sources = len(targets)
+    per_source, mine = targets[0].shape
     runs = sources * per_source
     own = cols // chunks
     last, has_before = chunk == chunks - 1, before is not None
     strip = lambda i: (0, i * chunks + chunk)
-    in_specs = [
-        pl.BlockSpec((runs, own), strip),
-        pl.BlockSpec((sources, per_source, own), lambda i: (0, 0, i)),
-        pl.BlockSpec((hid, own), strip),
-        pl.BlockSpec((1, own), strip),
-        SPACE,
-        SPACE,
-    ]
-    args = [guess, target, weight, bias, gain_t, feats]
+    in_specs = [SCALARS, pl.BlockSpec((runs, own), strip)]
+    in_specs += [pl.BlockSpec((per_source, own), lambda i: (0, i))] * sources
+    in_specs += [pl.BlockSpec((hid, own), strip), pl.BlockSpec((1, own), strip), ANY, SPACE]
+    args = [grp, guess, *targets, weight, bias, gain_t, feats]
+    if not last:
+        in_specs.append(SPACE)
+        args.append(hidden_t)
     aliases = {}
     if has_before:
-        in_specs += [ANY, ANY, ANY, SPACE]
-        args += list(before)
-        aliases = {6: 0, 7: 1, 8: 2}
+        aliases = {len(args): 0, len(args) + 1: 1}
+        in_specs += [ANY, ANY, SPACE]
+        args += list(before[:3])
+        if not last:
+            aliases[len(args)] = 3
+            in_specs.append(ANY)
+            args.append(before[3])
     acc_shape = (kept, hid) if last else (hid, LANES)
+    extra = (runs, own, runs) if last else (hid, own, hid)
+    scratch = [
+        pltpu.VMEM((hid, runs), F32),
+        pltpu.VMEM((hid, runs), F32),
+        pltpu.SemaphoreType.DMA,
+    ]
+    if not last:
+        scratch.append(pltpu.VMEM((runs, own), BF16))
+    products = 1 if last else 2
     return pl.pallas_call(
-        functools.partial(learn_kernel, last, has_before, scale),
+        functools.partial(learn_kernel, last, has_before, scale, sources),
         grid=(mine // own,),
         in_specs=in_specs,
         out_specs=[
             pl.BlockSpec((runs, own), strip),
-            pl.BlockSpec((runs, own), strip),
             pl.BlockSpec((1, own), strip),
             pl.BlockSpec(acc_shape, lambda i: (0, 0)),
+            pl.BlockSpec((extra[0], own), (lambda i: (0, i)) if last else strip),
         ],
         out_shape=[
-            jax.ShapeDtypeStruct((runs, cells), BF16),
             jax.ShapeDtypeStruct((runs, cells), BF16),
             jax.ShapeDtypeStruct((1, cells), F32),
             jax.ShapeDtypeStruct(acc_shape, F32),
-        ],
-        scratch_shapes=[pltpu.VMEM((hid, runs), F32)],
+            jax.ShapeDtypeStruct((runs, mine) if last else (hid, cells), BF16),
+        ],
+        scratch_shapes=scratch,
         input_output_aliases=aliases,
-        cost_estimate=cost(2 * runs * hid * (mine + 2 * LANES), 2 * hid * mine + 12 * runs * mine),
+        cost_estimate=cost(
+            2 * runs * hid * (products * mine + 2 * LANES), 2 * hid * mine * products + 12 * runs * mine
+        ),
         name="learn",
     )(*args)
 
 
-def update_kernel(hidden_t_ref, slope_ref, weight_ref, out_ref):
+def update_kernel(hidden_t_ref, slope_ref, weight_ref, _, out_ref):
     grad = jnp.dot(hidden_t_ref[...], slope_ref[...], preferred_element_type=F32)
     out_ref[...] = (weight_ref[...].astype(F32) - 0.5 * grad).astype(BF16)
 
 
-def update(hidden_t, slope, weight, block=256):
+def update(chunks, cols, hidden_t, slope, weight, so_far):
     hid, cells = weight.shape
-    runs = slope.shape[0]
+    runs, mine = slope.shape
+    own = cols // chunks
+    strip = lambda i: (0, i * chunks + chunks - 1)
     return pl.pallas_call(
         update_kernel,
-        grid=(hid // block,),
+        grid=(mine // own,),
         in_specs=[
-            pl.BlockSpec((block, runs), lambda i: (i, 0)),
-            pl.BlockSpec((runs, cells), lambda i: (0, 0)),
-            pl.BlockSpec((block, cells), lambda i: (i, 0)),
-        ],
-        out_specs=pl.BlockSpec((block, cells), lambda i: (i, 0)),
+            pl.BlockSpec((hid, runs), lambda i: (0, 0)),
+            pl.BlockSpec((runs, own), lambda i: (0, i)),
+            pl.BlockSpec((hid, own), strip),
+            ANY,
+        ],
+        out_specs=pl.BlockSpec((hid, own), strip),
         out_shape=jax.ShapeDtypeStruct((hid, cells), BF16),
-        cost_estimate=cost(2 * runs * hid * cells, 4 * hid * cells + 4 * runs * cells),
+        input_output_aliases={3: 0},
+        cost_estimate=cost(2 * runs * hid * mine, 4 * hid * mine + 4 * runs * mine),
         name="update",
-    )(hidden_t, slope, weight)
+    )(hidden_t, slope, weight, so_far)
 
 
 def halve(x, axis, bit):
@@ -546,14 +579,20 @@
 
     state = None
     scale = 2.0 / runs_total
+    grp = lax.axis_index("grp").astype(jnp.int32)[None]
     for c in range(chunks):
-        snap = diffuse(c, chunks, start_field, edges, ids_wide, run_rows_here, ends, n_grp)
-        target = lax.all_to_all(snap, "grp", split_axis=0, concat_axis=0, tiled=True)
-        state = learn_chunk(
-            c, chunks, cols, guess, target, output_layer, bias_row, gain_t, project, state, kept, scale
+        snaps = diffuse(c, chunks, start_field, edges, ids_wide, run_rows_here, ends, grp, n_grp)
+        targets = [snaps[0]]
+        for offset in range(1, n_grp):
+            pairs = [(i, i ^ offset) for i in range(n_grp)]
+            targets.append(lax.ppermute(snaps[offset], "grp", pairs))
+        before = state
+        state = learn(
+            c, chunks, cols, grp, guess, targets, output_layer, bias_row,
+            gain_t, project, hidden_t, before, kept, scale,
         )
-    misfit, slope, bias_next, partial = state
-    output_next = update(hidden_t, slope, output_layer)
+    misfit, bias_next, partial, slope = state
+    output_next = update(chunks, cols, hidden_t, slope, output_layer, before[3])
     flat = partial.reshape(-1, LANES)
     unit = SUB * n_grp * n_tile
     padded = -(-flat.shape[0] // unit) * unit

time: 195 us -> 184 us (0.944)
  waiting for transfers between devices: 51.9 us -> 44.3 us
  starting transfers between devices: 24 us -> 19.1 us
    all_to_all x2 -> x0, starting transfers between devices: 8.32 us -> none  [on_device(): lax.all_to_all(snap, 'grp', split_axis=0, concat_axis=0, tiled=True)]
    ppermute x2, waiting for transfers between devices: 42.3 us -> 34.2 us  [on_device(): above = lax.ppermute(bottom, 'tile', up)]
    ppermute x0 -> x6, starting transfers between devices: none -> 3.61 us  [on_device(): targets.append(lax.ppermute(snaps[offset], 'grp', pairs))]
    pallas_call x3, Pallas kernels: 33.8 us -> 36.1 us  [the longest x2 29 us: learn(): pl.pallas_call(functools.partial(learn_kernel, last, has_before, scale, s...]
  transfers between devices with their start and end apart: 10 -> 14, of which waited for: 5 -> 5; matrix products, arithmetic and copies ran while one was open for 1% -> 1% of each run, Pallas kernels for 28% -> 30%
where the time goes in v1:
time: 184 us; the launch traced here: 183 us
  Pallas kernels  86.4 us (47%)
  waiting for transfers between devices  44.3 us (24%)
  blocking collectives  23.9 us (13%)
  starting transfers between devices  19.1 us (10%)
  local copies, waits for them, and re-layouts  6.73 us (4%)
    ppermute x2, waiting for transfers between devices, on_device(): above = lax.ppermute(bottom, 'tile', up)  34.2 us
    pallas_call x2, Pallas kernels, diffuse(): pl.pallas_call(functools.partial(diffuse_kernel, chunk, chunks), in_specs...  30.2 us
    pallas_call x2, Pallas kernels, learn(): pl.pallas_call(functools.partial(learn_kernel, last, has_before, scale, s...  29 us
    all_to_all x1, blocking collectives, sum_over_devices(): x = lax.all_to_all(x.reshape(tile, n, LANES), 'tile', 0, 0, tiled=True)  13.9 us
    all_to_all x1, blocking collectives, sum_over_devices(): lax.all_to_all(jnp.broadcast_to(x[None], (tile, n, LANES)), 'tile', 0, 0,...  9.96 us
    pallas_call x1, Pallas kernels, predict(): pl.pallas_call(predict_kernel, grid=(cells // block,), in_specs=[pl.Block...  9.23 us
    ppermute x2, starting transfers between devices, on_device(): above = lax.ppermute(bottom, 'tile', up)  9.23 us
    pallas_call x1, Pallas kernels, update(): pl.pallas_call(update_kernel, grid=(mine // own,), in_specs=[pl.BlockSpec...  7.1 us
  transfers between devices with their start and end apart: 14, of which 5 were waited for; matrix products, arithmetic and copies ran while one was open for 1% of the time, Pallas kernels for 30%

profile of v1, /device:TPU:0, one launch (start us, length us, event | category | flops | bytes accessed | tf_op | source)
XLA Modules:
  0.0 183.2 jit_solution(8133800992814080020)
XLA Ops:
  0.7 4.6 %pack_edges.1 = (f32[1072,128]{1,0:T(8,128)}, f32[1072,128]{1,0:T(8,128)}, f32[992,128]{1,0:T(8,128)}, f32[992,128]{1,0:T(8,128)}) custom-call(f32[128,16,512]{2,1,0:T(8,128)} %field_ref.5, s32[16,512]{1,0:T(8,128)} %ids_ref.1), custom_call_target="tpu_custom_call" | custom-call | bytes 6291456 | tf_op jit(solution)/shard_map/pack_edges/pallas_call | solution.py:66
  5.2 4.9 %collective-permute-start = (f32[1072,128]{1,0:T(8,128)}, f32[1072,128]{1,0:T(8,128)S(1)}, u32[]{:S(2)}, u32[]{:S(2)}) collective-permute-start(f32[1072,128]{1,0:T(8,128)} %get-tuple-element.29), channel_id=1, source_target_pairs={{0,1},{1,2},{2,3},{3,4},{4,5},{5,6},{6,7},{8,9},{9,10},{10,11},{11... | collective-permute-start | bytes 1646600 | tf_op jit(solution)/shard_map/ppermute | solution.py:550
  10.2 1.3 collective-permute-start.1
  11.6 0.7 add_convert_fusion.ends_ref
  12.3 0.6 constant_dynamic-slice_fusion.1.runs_ref
  13.0 20.9 %collective-permute-done.refs_2_.refs_0_ = f32[1072,128]{1,0:T(8,128)S(1)} collective-permute-done((f32[1072,128]{1,0:T(8,128)}, f32[1072,128]{1,0:T(8,128)S(1)}, u32[]{:S(2)}, u32[]{:S(2)}) %collective-permute-start) | collective-permute-done | bytes 548896 | tf_op jit(solution)/shard_map/ppermute | solution.py:550
  34.0 0.9 broadcast_in_dim.26.ids_ref
  34.9 15.0 %diffuse.3 = (f32[128,1024]{1,0:T(8,128)}, f32[128,1024]{1,0:T(8,128)}, f32[128,1024]{1,0:T(8,128)}, f32[128,1024]{1,0:T(8,128)}) custom-call(f32[2]{0:T(128)} %add_convert_fusion.ends_ref, s32[1]{0:T(128)} %bitcast.grp_ref.refs_0_, f32[128,16,512]{2,1,0:T(8,128)} %field_ref.5, s32[24,1,512]{2,1,0:T(1,128)} %broadcast_in_dim.26.ids_ref, ...), custom_call_target="tpu_custom_call" | custom-call | flops 81100800 | bytes 9732096 | tf_op jit(solution)/shard_map/diffuse/pallas_call | solution.py:208
  50.0 4.3 %collective-permute-start.2 = (f32[992,128]{1,0:T(8,128)}, f32[992,128]{1,0:T(8,128)S(1)}, u32[]{:S(2)}, u32[]{:S(2)}) collective-permute-start(f32[992,128]{1,0:T(8,128)} %get-tuple-element.31), channel_id=1, source_target_pairs={{0,1},{1,2},{2,3},{3,4},{4,5},{5,6},{6,7},{8,9},{9,10},{10,11},{11... | collective-permute-start | bytes 1523720 | tf_op jit(solution)/shard_map/ppermute | solution.py:550
  54.3 1.5 collective-permute-start.3
  55.8 1.6 collective-permute-start.8
  57.4 6.3 %hidden_units.1 = (bf16[512,2048]{1,0:T(8,128)(2,1)}, bf16[2048,512]{1,0:T(8,128)(2,1)}, f32[2048,512]{1,0:T(8,128)}, bf16[512,128]{1,0:T(8,128)(2,1)}) custom-call(f32[16,512]{1,0:T(8,128)} %copy-done.12, f32[69,2048]{1,0:T(8,128)} %layer_ref.1), custom_call_target="tpu_custom_call" | custom-call | flops 1073741824 | bytes 10485760 | tf_op jit(solution)/shard_map/hidden_units/pallas_call | solution.py:297
  63.7 13.2 %collective-permute-done.2.refs_0_ = f32[992,128]{1,0:T(8,128)S(1)} collective-permute-done((f32[992,128]{1,0:T(8,128)}, f32[992,128]{1,0:T(8,128)S(1)}, u32[]{:S(2)}, u32[]{:S(2)}) %collective-permute-start.2) | collective-permute-done | bytes 507936 | tf_op jit(solution)/shard_map/ppermute | solution.py:550
  77.0 0.8 copy-done.9
  77.8 0.8 copy-done.10
  78.6 15.2 %diffuse.2 = (f32[128,1024]{1,0:T(8,128)}, f32[128,1024]{1,0:T(8,128)}, f32[128,1024]{1,0:T(8,128)}, f32[128,1024]{1,0:T(8,128)}) custom-call(f32[2]{0:T(128)} %add_convert_fusion.ends_ref, s32[1]{0:T(128)} %bitcast.grp_ref.refs_0_, f32[128,16,512]{2,1,0:T(8,128)} %field_ref.5, s32[24,1,512]{2,1,0:T(1,128)} %broadcast_in_dim.26.ids_ref, ...), custom_call_target="tpu_custom_call" | custom-call | flops 81100800 | bytes 9732096 | tf_op jit(solution)/shard_map/diffuse/pallas_call | solution.py:208
  93.9 1.6 collective-permute-start.5
  95.7 9.2 %predict.1.refs_1_ = f32[512,2048]{1,0:T(8,128)} custom-call(bf16[512,2048]{1,0:T(8,128)(2,1)} %get-tuple-element.28.hidden_ref, bf16[2048,2048]{1,0:T(8,128)(2,1)} %weight_ref.3, f32[1,2048]{1,0:T(1,128)} %bitcast.15), custom_call_target="tpu_custom_call" | custom-call | flops 4294967296 | bytes 12582912 | tf_op jit(solution)/shard_map/predict/pallas_call | solution.py:336
  105.0 0.8 copy-done.4
  106.0 17.6 %learn.2 = (bf16[512,2048]{1,0:T(8,128)(2,1)}, f32[1,2048]{1,0:T(1,128)}, f32[2048,128]{1,0:T(8,128)}, bf16[2048,2048]{1,0:T(8,128)(2,1)}) custom-call(s32[1]{0:T(128)} %bitcast.grp_ref.refs_0_, f32[512,2048]{1,0:T(8,128)} %predict.1.refs_1_, f32[128,1024]{1,0:T(8,128)} %get-tuple-element.39.refs_2_, f32[128,1024]{1,0:T(8,128)} %copy-done.3, ...), custom_call_target="tpu_custom_call" | custom-call | flops 4831838208 | bytes 14680064 | tf_op jit(solution)/shard_map/learn/pallas_call | solution.py:447
  123.6 0.8 copy-done.6
  124.7 11.4 %learn.3 = (bf16[512,2048]{1,0:T(8,128)(2,1)}, f32[1,2048]{1,0:T(1,128)}, f32[72,2048]{1,0:T(8,128)}, bf16[512,1024]{1,0:T(8,128)(2,1)}) custom-call(s32[1]{0:T(128)} %bitcast.grp_ref.refs_0_, f32[512,2048]{1,0:T(8,128)} %predict.1.refs_1_, f32[128,1024]{1,0:T(8,128)} %get-tuple-element.33.refs_2_, ...), custom_call_target="tpu_custom_call", output_to_operand_aliasing={{0}: (10, {}), {1}: (11, {})} | custom-call | flops 2684354560 | bytes 10485760 | tf_op jit(solution)/shard_map/learn/pallas_call | solution.py:447
  136.1 1.2 reshape.52
  137.8 1.3 collective-permute-done.10
  139.1 1.6 collective-permute-start.11
  140.7 5.0 %collective-permute-done.11 = f32[320,128]{1,0:T(8,128)S(1)} collective-permute-done((f32[320,128]{1,0:T(8,128)S(1)}, f32[320,128]{1,0:T(8,128)S(1)}, u32[]{:S(2)}, u32[]{:S(2)}) %collective-permute-start.11) | collective-permute-done | bytes 163872 | tf_op jit(solution)/shard_map/ppermute | solution.py:505
  145.7 13.9 %all_to_all.10 = f32[8,40,128]{2,1,0:T(8,128)S(1)} all-to-all(f32[8,40,128]{2,1,0:T(8,128)S(1)} %bitcast.12), channel_id=1, replica_groups=mesh['grp'=4,'tile'=8] {'tile'}, dimensions={0} | all-to-all | bytes 327680 | tf_op jit(solution)/shard_map/all_to_all | solution.py:523
  159.6 10.0 %all_to_all.11 = f32[8,40,128]{2,1,0:T(8,128)S(1)} all-to-all(f32[8,40,128]{2,1,0:T(8,128)S(1)} %broadcast_in_dim.27), channel_id=1, replica_groups=mesh['grp'=4,'tile'=8] {'tile'}, dimensions={0} | all-to-all | bytes 327680 | tf_op jit(solution)/shard_map/all_to_all | solution.py:525
  169.6 1.5 collective-permute-start.12
  171.1 3.8 %collective-permute-done.12 = f32[320,128]{1,0:T(8,128)S(1)} collective-permute-done((f32[320,128]{1,0:T(8,128)S(1)}, f32[320,128]{1,0:T(8,128)S(1)}, u32[]{:S(2)}, u32[]{:S(2)}) %collective-permute-start.12) | collective-permute-done | bytes 163872 | tf_op jit(solution)/shard_map/ppermute | solution.py:511
  175.0 7.1 %update.1 = bf16[2048,2048]{1,0:T(8,128)(2,1)} custom-call(bf16[2048,512]{1,0:T(8,128)(2,1)} %get-tuple-element.43.refs_10_.hidden_t_ref, bf16[512,1024]{1,0:T(8,128)(2,1)} %get-tuple-element.48.slope_ref, bf16[2048,2048]{1,0:T(8,128)(2,1)} %weight_ref.3, bf16[2048,2048]{1,0:T(8,128)(2,1)} %get-tuple-element.49._), custom_call_target="tpu_custom_call", output_to_operand_aliasing={{}: (3, {})} | custom-call | flops 2147483648 | bytes 10485760 | tf_op jit(solution)/shard_map/update/pallas_call | solution.py:482
  182.3 0.9 fusion
  (64 shorter events, 2.2 us)
Async XLA Ops:
  0.6 33.3 %copy-start.11 = (s32[16,512]{1,0:T(8,128)S(1)}, s32[16,512]{1,0:T(8,128)}, u32[]{:S(2)}) copy-start(s32[16,512]{1,0:T(8,128)} %ids_ref.1) | copy-start | bytes 98308
  0.6 10.8 %copy-start.14 = (s32[512]{0:T(512)S(1)}, s32[512]{0:T(512)}, u32[]{:S(2)}) copy-start(s32[512]{0:T(512)} %param.12) | copy-start | bytes 6148
  0.7 11.6 %copy-start.13 = (s32[512,8]{0,1:T(8,128)S(1)}, s32[512,8]{0,1:T(8,128)}, u32[]{:S(2)}) copy-start(s32[512,8]{0,1:T(8,128)} %param.10) | copy-start | bytes 49156
  0.7 11.6 %copy-start.15 = (f32[512]{0:T(512)S(1)}, f32[512]{0:T(512)}, u32[]{:S(2)}) copy-start(f32[512]{0:T(512)} %param.11) | copy-start | bytes 6148
  5.2 28.7 %collective-permute-start = (f32[1072,128]{1,0:T(8,128)}, f32[1072,128]{1,0:T(8,128)S(1)}, u32[]{:S(2)}, u32[]{:S(2)}) collective-permute-start(f32[1072,128]{1,0:T(8,128)} %get-tuple-element.29), channel_id=1, source_target_pairs={{0,1},{1,2},{2,3},{3,4},{4,5},{5,6},{6,7},{8,9},{9,10},{10,11},{11... | collective-permute-start | bytes 1646600 | tf_op jit(solution)/shard_map/ppermute | solution.py:550
  10.2 23.8 %collective-permute-start.1 = (f32[1072,128]{1,0:T(8,128)}, f32[1072,128]{1,0:T(8,128)S(1)}, u32[]{:S(2)}, u32[]{:S(2)}) collective-permute-start(f32[1072,128]{1,0:T(8,128)} %get-tuple-element.30), channel_id=1, source_target_pairs={{1,0},{2,1},{3,2},{4,3},{5,4},{6,5},{7,6},{9,8},{10,9},{11,10},{12... | collective-permute-start | bytes 1646600 | tf_op jit(solution)/shard_map/ppermute | solution.py:551
  12.3 45.1 %copy-start.12 = (f32[16,512]{1,0:T(8,128)}, f32[16,512]{1,0:T(8,128)S(1)}, u32[]{:S(2)}) copy-start(f32[16,512]{1,0:T(8,128)S(1)} %maximum_maximum_fusion.runs_ref) | copy-start | bytes 98308
  33.9 0.9 copy-start
  33.9 1.0 copy-start.1
  49.9 45.5 %collective-permute-start.7 = (f32[128,1024]{1,0:T(8,128)}, f32[128,1024]{1,0:T(8,128)S(1)}, u32[]{:S(2)}, u32[]{:S(2)}) collective-permute-start(f32[128,1024]{1,0:T(8,128)} %get-tuple-element.40), channel_id=1, source_target_pairs={{0,8},{8,0},{16,24},{24,16},{1,9},{9,1},{17,25},{25,17},{2,10},{10... | collective-permute-start | bytes 1572872 | tf_op jit(solution)/shard_map/ppermute | solution.py:588
  50.0 26.9 %collective-permute-start.2 = (f32[992,128]{1,0:T(8,128)}, f32[992,128]{1,0:T(8,128)S(1)}, u32[]{:S(2)}, u32[]{:S(2)}) collective-permute-start(f32[992,128]{1,0:T(8,128)} %get-tuple-element.31), channel_id=1, source_target_pairs={{0,1},{1,2},{2,3},{3,4},{4,5},{5,6},{6,7},{8,9},{9,10},{10,11},{11... | collective-permute-start | bytes 1523720 | tf_op jit(solution)/shard_map/ppermute | solution.py:550
  54.3 22.6 %collective-permute-start.3 = (f32[992,128]{1,0:T(8,128)}, f32[992,128]{1,0:T(8,128)S(1)}, u32[]{:S(2)}, u32[]{:S(2)}) collective-permute-start(f32[992,128]{1,0:T(8,128)} %get-tuple-element.32), channel_id=1, source_target_pairs={{1,0},{2,1},{3,2},{4,3},{5,4},{6,5},{7,6},{9,8},{10,9},{11,10},{12... | collective-permute-start | bytes 1523720 | tf_op jit(solution)/shard_map/ppermute | solution.py:551
  55.8 49.2 %collective-permute-start.8 = (f32[128,1024]{1,0:T(8,128)}, f32[128,1024]{1,0:T(8,128)S(1)}, u32[]{:S(2)}, u32[]{:S(2)}) collective-permute-start(f32[128,1024]{1,0:T(8,128)} %get-tuple-element.41), channel_id=1, source_target_pairs={{0,16},{8,24},{16,0},{24,8},{1,17},{9,25},{17,1},{25,9},{2,18},{10... | collective-permute-start | bytes 1572872 | tf_op jit(solution)/shard_map/ppermute | solution.py:588
  57.4 47.6 %collective-permute-start.9 = (f32[128,1024]{1,0:T(8,128)}, f32[128,1024]{1,0:T(8,128)S(1)}, u32[]{:S(2)}, u32[]{:S(2)}) collective-permute-start(f32[128,1024]{1,0:T(8,128)} %get-tuple-element.42), channel_id=1, source_target_pairs={{0,24},{8,16},{16,8},{24,0},{1,25},{9,17},{17,9},{25,1},{2,26},{10... | collective-permute-start | bytes 1572872 | tf_op jit(solution)/shard_map/ppermute | solution.py:588
  76.9 0.8 copy-start.9
  77.7 0.8 copy-start.10
  93.8 29.7 %collective-permute-start.4 = (f32[128,1024]{1,0:T(8,128)}, f32[128,1024]{1,0:T(8,128)S(1)}, u32[]{:S(2)}, u32[]{:S(2)}) collective-permute-start(f32[128,1024]{1,0:T(8,128)} %get-tuple-element.34), channel_id=1, source_target_pairs={{0,8},{8,0},{16,24},{24,16},{1,9},{9,1},{17,25},{25,17},{2,10},{10... | collective-permute-start | bytes 1572872 | tf_op jit(solution)/shard_map/ppermute | solution.py:588
  93.9 29.7 %collective-permute-start.5 = (f32[128,1024]{1,0:T(8,128)}, f32[128,1024]{1,0:T(8,128)S(1)}, u32[]{:S(2)}, u32[]{:S(2)}) collective-permute-start(f32[128,1024]{1,0:T(8,128)} %get-tuple-element.35), channel_id=1, source_target_pairs={{0,16},{8,24},{16,0},{24,8},{1,17},{9,25},{17,1},{25,9},{2,18},{10... | collective-permute-start | bytes 1572872 | tf_op jit(solution)/shard_map/ppermute | solution.py:588
  95.4 9.5 %copy-start.3 = (f32[128,1024]{1,0:T(8,128)}, f32[128,1024]{1,0:T(8,128)S(1)}, u32[]{:S(2)}) copy-start(f32[128,1024]{1,0:T(8,128)S(1)} %collective-permute-done.7.refs_3_) | copy-start | bytes 1572868
  95.4 28.1 %collective-permute-start.6 = (f32[128,1024]{1,0:T(8,128)}, f32[128,1024]{1,0:T(8,128)S(1)}, u32[]{:S(2)}, u32[]{:S(2)}) collective-permute-start(f32[128,1024]{1,0:T(8,128)} %get-tuple-element.36), channel_id=1, source_target_pairs={{0,24},{8,16},{16,8},{24,0},{1,25},{9,17},{17,9},{25,1},{2,26},{10... | collective-permute-start | bytes 1572872 | tf_op jit(solution)/shard_map/ppermute | solution.py:588
  105.0 0.8 copy-start.4
  105.0 1.0 copy-start.5
  123.5 0.8 copy-start.6
  123.6 1.0 copy-start.7
  123.6 1.1 copy-start.8
  137.3 1.7 collective-permute-start.10
  139.1 6.5 %collective-permute-start.11 = (f32[320,128]{1,0:T(8,128)S(1)}, f32[320,128]{1,0:T(8,128)S(1)}, u32[]{:S(2)}, u32[]{:S(2)}) collective-permute-start(f32[320,128]{1,0:T(8,128)S(1)} %constant_dynamic-slice_fusion), channel_id=1, source_target_pairs={{0,16},{8,24},{16,0},{24,8},{1,17},{9,25},{17,1},{25,9},{2,18},{10... | collective-permute-start | bytes 491528 | tf_op jit(solution)/shard_map/ppermute | solution.py:505
  169.6 5.3 %collective-permute-start.12 = (f32[320,128]{1,0:T(8,128)S(1)}, f32[320,128]{1,0:T(8,128)S(1)}, u32[]{:S(2)}, u32[]{:S(2)}) collective-permute-start(f32[320,128]{1,0:T(8,128)S(1)} %bitcast.13), channel_id=1, source_target_pairs={{0,16},{8,24},{16,0},{24,8},{1,17},{9,25},{17,1},{25,9},{2,18},{10... | collective-permute-start | bytes 491528 | tf_op jit(solution)/shard_map/ppermute | solution.py:511
  174.9 7.2 %collective-permute-start.13 = (f32[640,128]{1,0:T(8,128)S(1)}, f32[640,128]{1,0:T(8,128)S(1)}, u32[]{:S(2)}, u32[]{:S(2)}) collective-permute-start(f32[640,128]{1,0:T(8,128)S(1)} %maximum_select_fusion.1), channel_id=1, source_target_pairs={{0,8},{8,0},{16,24},{24,16},{1,9},{9,1},{17,25},{25,17},{2,10},{10... | collective-permute-start | bytes 983048 | tf_op jit(solution)/shard_map/ppermute | solution.py:511
  175.0 7.3 %copy-start.2 = (f32[69,2048]{1,0:T(8,128)S(1)}, f32[69,2048]{1,0:T(8,128)}, u32[]{:S(2)}) copy-start(f32[69,2048]{1,0:T(8,128)} %layer_ref.1) | copy-start | bytes 1695748

commit v2 on v1

--- a/solution.py
+++ b/solution.py
@@ -12,7 +12,9 @@
 LEVELS = 8
 LANES = 128
 SUB = 8
+BLOCK = 256
 CHUNKS = 2
+UPDATES = 2
 F32 = jnp.float32
 BF16 = jnp.bfloat16
 SPACE = pl.BlockSpec(memory_space=pltpu.VMEM)
@@ -39,22 +41,25 @@
 
 def pack_kernel(parts, field_ref, ids_ref, *outs):
     rows, cols = ids_ref.shape
-    for side in range(2):
-        for r in range(STEPS):
-            row = r if side == 0 else rows - STEPS + r
-            for j in range(cols // LANES):
-                tile = jnp.transpose(field_ref[:, row, j * LANES : (j + 1) * LANES])
-                for c, (_, high, sent) in enumerate(parts):
-                    first, last = max(sent, j * LANES), min(high, (j + 1) * LANES)
-                    if first < last:
-                        at = r * (high - sent) + first - sent
-                        outs[2 * c + side][at : at + last - first, :] = tile[
-                            first - j * LANES : last - j * LANES, :
-                        ]
-                at = STEPS * (parts[0][1] - parts[0][2]) + r * (cols // LANES) + j
-                outs[side][at : at + 1, :] = ids_ref[
-                    row : row + 1, j * LANES : (j + 1) * LANES
-                ].astype(F32)
+    for j in range(cols // LANES):
+
+        @pl.when(pl.program_id(0) == j)
+        def _(j=j):
+            for side in range(2):
+                for r in range(STEPS):
+                    row = r if side == 0 else rows - STEPS + r
+                    tile = jnp.transpose(field_ref[:, row, :])
+                    for c, (_, high, sent) in enumerate(parts):
+                        first, last = max(sent, j * LANES), min(high, (j + 1) * LANES)
+                        if first < last:
+                            at = r * (high - sent) + first - sent
+                            outs[2 * c + side][at : at + last - first, :] = tile[
+                                first - j * LANES : last - j * LANES, :
+                            ]
+                    at = STEPS * (parts[0][1] - parts[0][2]) + r * (cols // LANES) + j
+                    outs[side][at : at + 1, :] = ids_ref[
+                        row : row + 1, j * LANES : (j + 1) * LANES
+                    ].astype(F32)
 
 
 def pack_edges(start_field, ids, parts):
@@ -65,8 +70,12 @@
         shapes += [jax.ShapeDtypeStruct((STEPS * (high - sent) + extra, runs), F32)] * 2
     return pl.pallas_call(
         functools.partial(pack_kernel, parts),
-        in_specs=[SPACE, SPACE],
-        out_specs=[SPACE] * len(shapes),
+        grid=(cols // LANES,),
+        in_specs=[
+            pl.BlockSpec((runs, rows, LANES), lambda j: (0, 0, j)),
+            pl.BlockSpec((rows, cols), lambda j: (0, 0)),
+        ],
+        out_specs=[pl.BlockSpec(x.shape, lambda j: (0, 0)) for x in shapes],
         out_shape=shapes,
         cost_estimate=cost(0, 6 * runs * rows * cols),
         name="pack_edges",
@@ -163,21 +172,19 @@
             v_ref[k * SUB : (k + 1) * SUB, :] = (d + dn) * (un - u)
 
         def advance(r, carry, src=src, dst=dst, step=step, conduct=conduct):
+            active = pick8 >= jnp.where(inside(r) > 0.0, F32(step), F32(2 * STEPS))
             for k in range(-1, width // SUB):
                 p = SUB + k * SUB
-                flux = (d_ref[r, p : p + SUB, :] + d_ref[r, p + 1 : p + 1 + SUB, :]) * (
-                    src[r, p + 1 : p + 1 + SUB, :] - src[r, p : p + SUB, :]
-                )
+                u, d = src[r, p : p + SUB, :], d_ref[r, p : p + SUB, :]
+                flux = (d + d_ref[r, p + 1 : p + 1 + SUB, :]) * (src[r, p + 1 : p + 1 + SUB, :] - u)
                 fx_ref[p : p + SUB, :] = flux
-            active = pick8 >= jnp.where(inside(r) > 0.0, F32(step), F32(2 * STEPS))
-            for k in blocks:
-                p = SUB + k * SUB
+                if k < 0:
+                    continue
                 at = slice(k * SUB, (k + 1) * SUB)
-                u, un = src[r, p : p + SUB, :], src[r + 1, p : p + SUB, :]
-                d = d_ref[r, p : p + SUB, :]
+                un = src[r + 1, p : p + SUB, :]
                 dn = conduct(r + 1, k, un)
                 down = (d + dn) * (un - u)
-                across = fx_ref[p : p + SUB, :] - fx_ref[p - 1 : p - 1 + SUB, :]
+                across = flux - fx_ref[p - 1 : p - 1 + SUB, :]
                 new = u + across + (down - v_ref[at, :])
                 v_ref[at, :] = down
                 dst[r, p : p + SUB, :] = jnp.where(active, new, u)
@@ -356,16 +363,21 @@
     if not last:
         hidden_t_ref, refs = refs[0], refs[1:]
     if has_before:
-        acc_in_ref, refs = refs[2], refs[3:]
+        acc_in_any, refs = refs[2], refs[3 + (not last) :]
     misfit_ref, bias_out_ref, acc_ref, extra_ref = refs[:4]
-    back_ref, gain_ref, sem = refs[4:7]
-    slope_ref = extra_ref if last else refs[7]
+    back_ref, gain_ref, sem, acc_in_ref = refs[4:8]
+    slope_ref = extra_ref if last else refs[8]
     step, steps = pl.program_id(0), pl.num_programs(0)
-    load = pltpu.make_async_copy(gain_any, gain_ref, sem)
+    load = pltpu.make_async_copy(gain_any, gain_ref, sem.at[0])
+    if has_before:
+        load_acc = pltpu.make_async_copy(acc_in_any, acc_in_ref, sem.at[1])
 
     @pl.when(step == 0)
     def _():
         load.start()
+        if has_before:
+            load_acc.start()
+        back_ref[...] = jnp.zeros(back_ref.shape, F32)
 
     per_source, own = targets[0].shape
     total = jnp.zeros((1, own), F32)
@@ -377,37 +389,38 @@
         slope_ref[at, :] = slope
         total = total + jnp.sum(slope.astype(F32), axis=0, keepdims=True)
     bias_out_ref[...] = bias_ref[...] - 0.5 * total
-    back = lax.dot_general(
-        weight_ref[...], slope_ref[...], (((1,), (1,)), ((), ())), preferred_element_type=F32
-    )
-
-    @pl.when(step == 0)
-    def _():
-        back_ref[...] = back
-
-    @pl.when(step > 0)
-    def _():
-        back_ref[...] += back
-
-    if not last:
-        grad = jnp.dot(hidden_t_ref[...], slope_ref[...], preferred_element_type=F32)
-        extra_ref[...] = (weight_ref[...].astype(F32) - 0.5 * grad).astype(BF16)
+    slope = slope_ref[...]
+    for h in range(0, weight_ref.shape[0], BLOCK):
+        at = slice(h, h + BLOCK)
+        weight = weight_ref[at, :]
+        back_ref[at, :] += lax.dot_general(
+            weight, slope, (((1,), (1,)), ((), ())), preferred_element_type=F32
+        )
+        if not last:
+            grad = jnp.dot(hidden_t_ref[at, :], slope, preferred_element_type=F32)
+            extra_ref[at, :] = (weight.astype(F32) - 0.5 * grad).astype(BF16)
 
     @pl.when(step == steps - 1)
     def _():
         load.wait()
-        full = back_ref[...] * gain_ref[...]
-        high = full.astype(BF16)
-        low = (full - high.astype(F32)).astype(BF16)
+        if has_before:
+            load_acc.wait()
         feats = feats_ref[...]
-        acc = jnp.dot(high, feats, preferred_element_type=F32)
-        acc = acc + jnp.dot(low, feats, preferred_element_type=F32)
-        if has_before:
-            acc = acc + acc_in_ref[...]
-        if last:
-            acc_ref[...] = jnp.transpose(acc)[: acc_ref.shape[0], :]
-        else:
-            acc_ref[...] = acc
+        for h in range(0, back_ref.shape[0], BLOCK):
+            at = slice(h, h + BLOCK)
+            full = back_ref[at, :] * gain_ref[at, :]
+            high = full.astype(BF16)
+            low = (full - high.astype(F32)).astype(BF16)
+            acc = jnp.dot(high, feats, preferred_element_type=F32)
+            acc = acc + jnp.dot(low, feats, preferred_element_type=F32)
+            if has_before:
+                acc = acc + acc_in_ref[at, :]
+            if last:
+                for t in range(0, BLOCK, LANES):
+                    turned = jnp.transpose(acc[t : t + LANES, :])
+                    acc_ref[(h + t) // LANES] = turned[: acc_ref.shape[1], :]
+            else:
+                acc_ref[at, :] = acc
 
 
 def learn(chunk, chunks, cols, grp, guess, targets, weight, bias, gain_t, feats, hidden_t, before, kept, scale):
@@ -428,18 +441,19 @@
     aliases = {}
     if has_before:
         aliases = {len(args): 0, len(args) + 1: 1}
-        in_specs += [ANY, ANY, SPACE]
+        in_specs += [ANY, ANY, ANY]
         args += list(before[:3])
         if not last:
             aliases[len(args)] = 3
             in_specs.append(ANY)
             args.append(before[3])
-    acc_shape = (kept, hid) if last else (hid, LANES)
+    acc_shape = (hid // LANES, kept, LANES) if last else (hid, LANES)
     extra = (runs, own, runs) if last else (hid, own, hid)
     scratch = [
         pltpu.VMEM((hid, runs), F32),
         pltpu.VMEM((hid, runs), F32),
-        pltpu.SemaphoreType.DMA,
+        pltpu.SemaphoreType.DMA((2,)),
+        pltpu.VMEM((hid, LANES), F32),
     ]
     if not last:
         scratch.append(pltpu.VMEM((runs, own), BF16))
@@ -451,7 +465,7 @@
         out_specs=[
             pl.BlockSpec((runs, own), strip),
             pl.BlockSpec((1, own), strip),
-            pl.BlockSpec(acc_shape, lambda i: (0, 0)),
+            pl.BlockSpec(acc_shape, lambda i: (0,) * len(acc_shape)),
             pl.BlockSpec((extra[0], own), (lambda i: (0, i)) if last else strip),
         ],
         out_shape=[
@@ -470,30 +484,58 @@
 
 
 def update_kernel(hidden_t_ref, slope_ref, weight_ref, _, out_ref):
-    grad = jnp.dot(hidden_t_ref[...], slope_ref[...], preferred_element_type=F32)
-    out_ref[...] = (weight_ref[...].astype(F32) - 0.5 * grad).astype(BF16)
-
-
-def update(chunks, cols, hidden_t, slope, weight, so_far):
+    slope = slope_ref[...]
+    for h in range(0, weight_ref.shape[0], BLOCK):
+        at = slice(h, h + BLOCK)
+        grad = jnp.dot(hidden_t_ref[at, :], slope, preferred_element_type=F32)
+        out_ref[at, :] = (weight_ref[at, :].astype(F32) - 0.5 * grad).astype(BF16)
+
+
+def update(first, count, chunks, cols, hidden_t, slope, weight, so_far):
     hid, cells = weight.shape
-    runs, mine = slope.shape
+    runs, _ = slope.shape
     own = cols // chunks
-    strip = lambda i: (0, i * chunks + chunks - 1)
+    strip = lambda i: (0, (first + i) * chunks + chunks - 1)
     return pl.pallas_call(
         update_kernel,
-        grid=(mine // own,),
+        grid=(count,),
         in_specs=[
             pl.BlockSpec((hid, runs), lambda i: (0, 0)),
-            pl.BlockSpec((runs, own), lambda i: (0, i)),
+            pl.BlockSpec((runs, own), lambda i: (0, first + i)),
             pl.BlockSpec((hid, own), strip),
             ANY,
         ],
         out_specs=pl.BlockSpec((hid, own), strip),
         out_shape=jax.ShapeDtypeStruct((hid, cells), BF16),
         input_output_aliases={3: 0},
-        cost_estimate=cost(2 * runs * hid * mine, 4 * hid * mine + 4 * runs * mine),
+        cost_estimate=cost(2 * runs * hid * own * count, (4 * hid + 4 * runs) * own * count),
         name="update",
     )(hidden_t, slope, weight, so_far)
+
+
+def finish_kernel(total_ref, layer_ref, out_ref):
+    n_feat = layer_ref.shape[0]
+    line = lax.broadcasted_iota(jnp.int32, (n_feat, LANES), 0)
+    for t in range(total_ref.shape[0]):
+        at = slice(t * LANES, (t + 1) * LANES)
+        rest = jnp.broadcast_to(total_ref[t, n_feat : n_feat + 1, :], (n_feat, LANES))
+        grad = total_ref[t, :n_feat, :] + jnp.where(line == n_feat - 1, rest, 0.0)
+        out_ref[:, at] = layer_ref[:, at] - 2.0 * grad
+
+
+def finish(total, layer):
+    return pl.pallas_call(
+        finish_kernel,
+        in_specs=[SPACE, SPACE],
+        out_specs=SPACE,
+        out_shape=jax.ShapeDtypeStruct(layer.shape, F32),
+        cost_estimate=cost(3 * layer.size, 12 * layer.size),
+        name="finish",
+    )(total, layer)
+
+
+def bits_of(size):
+    return [1 << b for b in range(size.bit_length() - 1)]
 
 
 def halve(x, axis, bit):
@@ -516,15 +558,11 @@
 
 def sum_over_devices(x):
     grp, tile = lax.axis_size("grp"), lax.axis_size("tile")
-    bits = [1 << b for b in range(grp.bit_length() - 1)]
-    for bit in bits:
+    for bit in bits_of(grp):
         x = halve(x, "grp", bit)
-    n = x.shape[0] // tile
-    x = lax.all_to_all(x.reshape(tile, n, LANES), "tile", 0, 0, tiled=True)
-    x = jnp.sum(x.reshape(tile, n, LANES), axis=0)
-    x = lax.all_to_all(jnp.broadcast_to(x[None], (tile, n, LANES)), "tile", 0, 0, tiled=True)
-    x = x.reshape(tile * n, LANES)
-    for bit in bits[::-1]:
+    for bit in bits_of(tile):
+        x = x + lax.ppermute(x, "tile", [(i, i ^ bit) for i in range(tile)])
+    for bit in bits_of(grp)[::-1]:
         x = rejoin(x, "grp", bit)
     return x
 
@@ -532,14 +570,14 @@
 def on_device(
     start_field, class_ids, run_levels, steepness, step_pick, input_layer, output_layer, output_bias
 ):
-    local_runs, _, cols = start_field.shape
+    local_runs, rows, cols = start_field.shape
     n_grp, n_tile = lax.axis_size("grp"), lax.axis_size("tile")
     tile = lax.axis_index("tile")
     first_run = lax.axis_index("grp") * local_runs
     chunks = CHUNKS
     parts = spans(cols, chunks)
     runs_total, classes = run_levels.shape
-    n_feat, hid = input_layer.shape
+    n_feat, _ = input_layer.shape
 
     up = [(i, i + 1) for i in range(n_tile - 1)]
     down = [(j, i) for i, j in up]
@@ -592,16 +630,14 @@
             gain_t, project, hidden_t, before, kept, scale,
         )
     misfit, bias_next, partial, slope = state
-    output_next = update(chunks, cols, hidden_t, slope, output_layer, before[3])
-    flat = partial.reshape(-1, LANES)
-    unit = SUB * n_grp * n_tile
-    padded = -(-flat.shape[0] // unit) * unit
-    flat = jnp.pad(flat, ((0, padded - flat.shape[0]), (0, 0)))
-    total = sum_over_devices(flat)[: kept * hid // LANES].reshape(kept, hid)
-    grad_in = jnp.concatenate(
-        [total[: n_feat - 1], total[n_feat - 1 : n_feat] + total[n_feat : n_feat + 1]], axis=0
-    )
-    input_next = input_layer - 2.0 * grad_in
+    output_next, strips = before[3], rows // n_grp
+    for part in range(UPDATES):
+        first, past = part * strips // UPDATES, (part + 1) * strips // UPDATES
+        output_next = update(
+            first, past - first, chunks, cols, hidden_t, slope, output_layer, output_next
+        )
+    total = sum_over_devices(partial.reshape(-1, LANES)).reshape(partial.shape)
+    input_next = finish(total, input_layer)
     return misfit, output_next, bias_next.reshape(-1), input_next
 
 

time: 184 us -> 179 us (0.973)
  blocking collectives: 23.9 us -> 0 us
  waiting for transfers between devices: 44.3 us -> 56 us
  starting transfers between devices: 19.1 us -> 27.4 us
    all_to_all x2 -> x0, blocking collectives: 23.9 us -> none  [the longest x1 13.9 us: sum_over_devices(): x = lax.all_to_all(x.reshape(tile, n, LANES), 'tile', 0, 0, tiled=True)]
    ppermute x0 -> x3, waiting for transfers between devices: none -> 11.3 us  [sum_over_devices(): x = x + lax.ppermute(x, 'tile', [(i, i ^ bit) for i in range(tile)])]
    ppermute x0 -> x3, starting transfers between devices: none -> 8.22 us  [sum_over_devices(): x = x + lax.ppermute(x, 'tile', [(i, i ^ bit) for i in range(tile)])]
    pallas_call x2, Pallas kernels: 29 us -> 22.1 us  [learn(): pl.pallas_call(functools.partial(learn_kernel, last, has_before, scale, s...]
    pallas_call x2 -> x4, Pallas kernels: 11.7 us -> 16.2 us  [the longest x2 8.95 us: update(): pl.pallas_call(update_kernel, grid=(count,), in_specs=[pl.BlockSpec((hid,...]
    unnamed x32 -> x30, local copies, waits for them, and re-layouts: 3.81 us -> 3.48 us
  transfers between devices with their start and end apart: 14 -> 17, of which waited for: 5 -> 9; matrix products, arithmetic and copies ran while one was open for 1% -> 1% of each run, Pallas kernels for 30% -> 29%
where the time goes in v2:
time: 179 us; the launch traced here: 178 us
  Pallas kernels  84.9 us (47%)
  waiting for transfers between devices  56 us (31%)
  starting transfers between devices  27.4 us (15%)
  local copies, waits for them, and re-layouts  6.03 us (3%)
  other arithmetic  2.7 us (2%)
    ppermute x2, waiting for transfers between devices, on_device(): above = lax.ppermute(bottom, 'tile', up)  34.2 us
    pallas_call x2, Pallas kernels, diffuse(): pl.pallas_call(functools.partial(diffuse_kernel, chunk, chunks), in_specs...  31.1 us
    pallas_call x2, Pallas kernels, learn(): pl.pallas_call(functools.partial(learn_kernel, last, has_before, scale, s...  22.1 us
    ppermute x3, waiting for transfers between devices, sum_over_devices(): x = x + lax.ppermute(x, 'tile', [(i, i ^ bit) for i in range(tile)])  11.3 us
    ppermute x2, starting transfers between devices, on_device(): above = lax.ppermute(bottom, 'tile', up)  9.23 us
    pallas_call x1, Pallas kernels, predict(): pl.pallas_call(predict_kernel, grid=(cells // block,), in_specs=[pl.Block...  9.22 us
    pallas_call x2, Pallas kernels, update(): pl.pallas_call(update_kernel, grid=(count,), in_specs=[pl.BlockSpec((hid,...  8.95 us
    ppermute x3, starting transfers between devices, sum_over_devices(): x = x + lax.ppermute(x, 'tile', [(i, i ^ bit) for i in range(tile)])  8.22 us
  transfers between devices with their start and end apart: 17, of which 9 were waited for; matrix products, arithmetic and copies ran while one was open for 1% of the time, Pallas kernels for 29%

profile of v2, /device:TPU:0, one launch (start us, length us, event | category | flops | bytes accessed | tf_op | source)
XLA Modules:
  0.0 178.0 jit_solution(7499634028108067567)
XLA Ops:
  0.7 5.1 %pack_edges.1 = (f32[1072,128]{1,0:T(8,128)}, f32[1072,128]{1,0:T(8,128)}, f32[992,128]{1,0:T(8,128)}, f32[992,128]{1,0:T(8,128)}) custom-call(f32[128,16,512]{2,1,0:T(8,128)} %field_ref.5, s32[16,512]{1,0:T(8,128)} %ids_ref.1), custom_call_target="tpu_custom_call" | custom-call | bytes 6291456 | tf_op jit(solution)/shard_map/pack_edges/pallas_call | solution.py:71
  5.8 4.9 %collective-permute-start = (f32[1072,128]{1,0:T(8,128)}, f32[1072,128]{1,0:T(8,128)S(1)}, u32[]{:S(2)}, u32[]{:S(2)}) collective-permute-start(f32[1072,128]{1,0:T(8,128)} %get-tuple-element.29), channel_id=1, source_target_pairs={{0,1},{1,2},{2,3},{3,4},{4,5},{5,6},{6,7},{8,9},{9,10},{10,11},{11... | collective-permute-start | bytes 1646600 | tf_op jit(solution)/shard_map/ppermute | solution.py:588
  10.7 1.3 collective-permute-start.1
  13.5 21.0 %collective-permute-done.refs_2_.refs_0_ = f32[1072,128]{1,0:T(8,128)S(1)} collective-permute-done((f32[1072,128]{1,0:T(8,128)}, f32[1072,128]{1,0:T(8,128)S(1)}, u32[]{:S(2)}, u32[]{:S(2)}) %collective-permute-start) | collective-permute-done | bytes 548896 | tf_op jit(solution)/shard_map/ppermute | solution.py:588
  35.5 15.4 %diffuse.3 = (f32[128,1024]{1,0:T(8,128)}, f32[128,1024]{1,0:T(8,128)}, f32[128,1024]{1,0:T(8,128)}, f32[128,1024]{1,0:T(8,128)}) custom-call(f32[2]{0:T(128)} %add_convert_fusion.ends_ref, s32[1]{0:T(128)} %bitcast.grp_ref.refs_0_, f32[128,16,512]{2,1,0:T(8,128)} %field_ref.5, s32[24,1,512]{2,1,0:T(1,128)} %broadcast_in_dim.20.ids_ref, ...), custom_call_target="tpu_custom_call" | custom-call | flops 81100800 | bytes 9732096 | tf_op jit(solution)/shard_map/diffuse/pallas_call | solution.py:215
  51.0 4.3 %collective-permute-start.2 = (f32[992,128]{1,0:T(8,128)}, f32[992,128]{1,0:T(8,128)S(1)}, u32[]{:S(2)}, u32[]{:S(2)}) collective-permute-start(f32[992,128]{1,0:T(8,128)} %get-tuple-element.31), channel_id=1, source_target_pairs={{0,1},{1,2},{2,3},{3,4},{4,5},{5,6},{6,7},{8,9},{9,10},{10,11},{11... | collective-permute-start | bytes 1523720 | tf_op jit(solution)/shard_map/ppermute | solution.py:588
  55.3 1.5 collective-permute-start.3
  56.8 1.6 collective-permute-start.8
  58.4 6.3 %hidden_units.1 = (bf16[512,2048]{1,0:T(8,128)(2,1)}, bf16[2048,512]{1,0:T(8,128)(2,1)}, f32[2048,512]{1,0:T(8,128)}, bf16[512,128]{1,0:T(8,128)(2,1)}) custom-call(f32[16,512]{1,0:T(8,128)} %copy-done.11, f32[69,2048]{1,0:T(8,128)} %layer_ref.3), custom_call_target="tpu_custom_call" | custom-call | flops 1073741824 | bytes 10485760 | tf_op jit(solution)/shard_map/hidden_units/pallas_call | solution.py:304
  64.7 13.2 %collective-permute-done.2.refs_0_ = f32[992,128]{1,0:T(8,128)S(1)} collective-permute-done((f32[992,128]{1,0:T(8,128)}, f32[992,128]{1,0:T(8,128)S(1)}, u32[]{:S(2)}, u32[]{:S(2)}) %collective-permute-start.2) | collective-permute-done | bytes 507936 | tf_op jit(solution)/shard_map/ppermute | solution.py:588
  79.6 15.7 %diffuse.2 = (f32[128,1024]{1,0:T(8,128)}, f32[128,1024]{1,0:T(8,128)}, f32[128,1024]{1,0:T(8,128)}, f32[128,1024]{1,0:T(8,128)}) custom-call(f32[2]{0:T(128)} %add_convert_fusion.ends_ref, s32[1]{0:T(128)} %bitcast.grp_ref.refs_0_, f32[128,16,512]{2,1,0:T(8,128)} %field_ref.5, s32[24,1,512]{2,1,0:T(1,128)} %broadcast_in_dim.20.ids_ref, ...), custom_call_target="tpu_custom_call" | custom-call | flops 81100800 | bytes 9732096 | tf_op jit(solution)/shard_map/diffuse/pallas_call | solution.py:215
  95.3 1.6 collective-permute-start.5
  97.2 9.2 %predict.1.refs_1_ = f32[512,2048]{1,0:T(8,128)} custom-call(bf16[512,2048]{1,0:T(8,128)(2,1)} %get-tuple-element.28.hidden_ref, bf16[2048,2048]{1,0:T(8,128)(2,1)} %weight_ref.5, f32[1,2048]{1,0:T(1,128)} %bitcast.14), custom_call_target="tpu_custom_call" | custom-call | flops 4294967296 | bytes 12582912 | tf_op jit(solution)/shard_map/predict/pallas_call | solution.py:343
  107.4 12.2 %learn.2 = (bf16[512,2048]{1,0:T(8,128)(2,1)}, f32[1,2048]{1,0:T(1,128)}, f32[2048,128]{1,0:T(8,128)}, bf16[2048,2048]{1,0:T(8,128)(2,1)}) custom-call(s32[1]{0:T(128)} %bitcast.grp_ref.refs_0_, f32[512,2048]{1,0:T(8,128)} %predict.1.refs_1_, f32[128,1024]{1,0:T(8,128)} %get-tuple-element.39.refs_2_, f32[128,1024]{1,0:T(8,128)} %copy-done.2, ...), custom_call_target="tpu_custom_call" | custom-call | flops 4831838208 | bytes 14680064 | tf_op jit(solution)/shard_map/learn/pallas_call | solution.py:461
  119.6 0.9 collective-permute-done.6.refs_5_
  121.3 9.9 %learn.3 = (bf16[512,2048]{1,0:T(8,128)(2,1)}, f32[1,2048]{1,0:T(1,128)}, f32[16,72,128]{2,1,0:T(8,128)}, bf16[512,1024]{1,0:T(8,128)(2,1)}) custom-call(s32[1]{0:T(128)} %bitcast.grp_ref.refs_0_, f32[512,2048]{1,0:T(8,128)} %predict.1.refs_1_, f32[128,1024]{1,0:T(8,128)} %get-tuple-element.33.refs_2_, ...), custom_call_target="tpu_custom_call", output_to_operand_aliasing={{0}: (10, {}), {1}: (11, {})} | custom-call | flops 2684354560 | bytes 10485760 | tf_op jit(solution)/shard_map/learn/pallas_call | solution.py:461
  131.2 1.0 constant_dynamic-slice_fusion.1
  132.6 1.2 collective-permute-done.10
  133.9 1.0 dynamic-slice_add_fusion
  134.9 1.6 collective-permute-start.11
  136.4 4.6 %collective-permute-done.11 = f32[288,128]{1,0:T(8,128)S(1)} collective-permute-done((f32[288,128]{1,0:T(8,128)S(1)}, f32[288,128]{1,0:T(8,128)S(1)}, u32[]{:S(2)}, u32[]{:S(2)}) %collective-permute-start.11) | collective-permute-done | bytes 147488 | tf_op jit(solution)/shard_map/ppermute | solution.py:547
  141.1 2.4 %collective-permute-start.12 = (f32[288,128]{1,0:T(8,128)S(1)}, f32[288,128]{1,0:T(8,128)S(1)}, u32[]{:S(2)}, u32[]{:S(2)}) collective-permute-start(f32[288,128]{1,0:T(8,128)S(1)} %dynamic-slice_add_fusion.1), channel_id=1, source_target_pairs={{0,1},{1,0},{2,3},{3,2},{4,5},{5,4},{6,7},{7,6},{8,9},{9,8},{10,11... | collective-permute-start | bytes 442376 | tf_op jit(solution)/shard_map/ppermute | solution.py:564
  143.5 3.5 %collective-permute-done.12 = f32[288,128]{1,0:T(8,128)S(1)} collective-permute-done((f32[288,128]{1,0:T(8,128)S(1)}, f32[288,128]{1,0:T(8,128)S(1)}, u32[]{:S(2)}, u32[]{:S(2)}) %collective-permute-start.12) | collective-permute-done | bytes 147488 | tf_op jit(solution)/shard_map/ppermute | solution.py:564
  147.1 2.7 %collective-permute-start.13 = (f32[288,128]{1,0:T(8,128)S(1)}, f32[288,128]{1,0:T(8,128)S(1)}, u32[]{:S(2)}, u32[]{:S(2)}) collective-permute-start(f32[288,128]{1,0:T(8,128)S(1)} %add.25), channel_id=1, source_target_pairs={{0,2},{1,3},{2,0},{3,1},{4,6},{5,7},{6,4},{7,5},{8,10},{9,11},{10,... | collective-permute-start | bytes 442376 | tf_op jit(solution)/shard_map/ppermute | solution.py:564
  149.7 3.1 %collective-permute-done.13 = f32[288,128]{1,0:T(8,128)S(1)} collective-permute-done((f32[288,128]{1,0:T(8,128)S(1)}, f32[288,128]{1,0:T(8,128)S(1)}, u32[]{:S(2)}, u32[]{:S(2)}) %collective-permute-start.13) | collective-permute-done | bytes 147488 | tf_op jit(solution)/shard_map/ppermute | solution.py:564
  152.9 3.1 %collective-permute-start.14 = (f32[288,128]{1,0:T(8,128)S(1)}, f32[288,128]{1,0:T(8,128)S(1)}, u32[]{:S(2)}, u32[]{:S(2)}) collective-permute-start(f32[288,128]{1,0:T(8,128)S(1)} %add.26), channel_id=1, source_target_pairs={{0,4},{1,5},{2,6},{3,7},{4,0},{5,1},{6,2},{7,3},{8,12},{9,13},{10,... | collective-permute-start | bytes 442376 | tf_op jit(solution)/shard_map/ppermute | solution.py:564
  156.0 4.7 %collective-permute-done.14 = f32[288,128]{1,0:T(8,128)S(1)} collective-permute-done((f32[288,128]{1,0:T(8,128)S(1)}, f32[288,128]{1,0:T(8,128)S(1)}, u32[]{:S(2)}, u32[]{:S(2)}) %collective-permute-start.14) | collective-permute-done | bytes 147488 | tf_op jit(solution)/shard_map/ppermute | solution.py:564
  160.7 1.5 collective-permute-start.15
  162.3 3.7 %collective-permute-done.15 = f32[288,128]{1,0:T(8,128)S(1)} collective-permute-done((f32[288,128]{1,0:T(8,128)S(1)}, f32[288,128]{1,0:T(8,128)S(1)}, u32[]{:S(2)}, u32[]{:S(2)}) %collective-permute-start.15) | collective-permute-done | bytes 147488 | tf_op jit(solution)/shard_map/ppermute | solution.py:553
  166.0 4.5 %update.2._ = bf16[2048,2048]{1,0:T(8,128)(2,1)} custom-call(bf16[2048,512]{1,0:T(8,128)(2,1)} %get-tuple-element.43.refs_10_.hidden_t_ref, bf16[512,1024]{1,0:T(8,128)(2,1)} %get-tuple-element.48.slope_ref, bf16[2048,2048]{1,0:T(8,128)(2,1)} %weight_ref.5, bf16[2048,2048]{1,0:T(8,128)(2,1)} %get-tuple-element.49._), custom_call_target="tpu_custom_call", output_to_operand_aliasing={{}: (3, {})} | custom-call | flops 1073741824 | bytes 5242880 | tf_op jit(solution)/shard_map/update/pallas_call | solution.py:499
  170.5 4.5 %update.3 = bf16[2048,2048]{1,0:T(8,128)(2,1)} custom-call(bf16[2048,512]{1,0:T(8,128)(2,1)} %get-tuple-element.43.refs_10_.hidden_t_ref, bf16[512,1024]{1,0:T(8,128)(2,1)} %get-tuple-element.48.slope_ref, bf16[2048,2048]{1,0:T(8,128)(2,1)} %weight_ref.5, bf16[2048,2048]{1,0:T(8,128)(2,1)} %update.2._), custom_call_target="tpu_custom_call", output_to_operand_aliasing={{}: (3, {})} | custom-call | flops 1073741824 | bytes 5242880 | tf_op jit(solution)/shard_map/update/pallas_call | solution.py:499
  175.8 2.1 %finish.1 = f32[69,2048]{1,0:T(8,128)} custom-call(f32[16,72,128]{2,1,0:T(8,128)} %bitcast.11, f32[69,2048]{1,0:T(8,128)} %layer_ref.3), custom_call_target="tpu_custom_call" | custom-call | flops 423936 | bytes 1695744 | tf_op jit(solution)/shard_map/finish/pallas_call | solution.py:527
  (64 shorter events, 7.8 us)
Async XLA Ops:
  0.6 33.9 %copy-start.10 = (s32[16,512]{1,0:T(8,128)S(1)}, s32[16,512]{1,0:T(8,128)}, u32[]{:S(2)}) copy-start(s32[16,512]{1,0:T(8,128)} %ids_ref.1) | copy-start | bytes 98308
  0.6 11.4 %copy-start.13 = (s32[512]{0:T(512)S(1)}, s32[512]{0:T(512)}, u32[]{:S(2)}) copy-start(s32[512]{0:T(512)} %param.12) | copy-start | bytes 6148
  0.7 12.2 %copy-start.12 = (s32[512,8]{0,1:T(8,128)S(1)}, s32[512,8]{0,1:T(8,128)}, u32[]{:S(2)}) copy-start(s32[512,8]{0,1:T(8,128)} %param.10) | copy-start | bytes 49156
  0.7 12.2 %copy-start.14 = (f32[512]{0:T(512)S(1)}, f32[512]{0:T(512)}, u32[]{:S(2)}) copy-start(f32[512]{0:T(512)} %param.11) | copy-start | bytes 6148
  5.8 28.7 %collective-permute-start = (f32[1072,128]{1,0:T(8,128)}, f32[1072,128]{1,0:T(8,128)S(1)}, u32[]{:S(2)}, u32[]{:S(2)}) collective-permute-start(f32[1072,128]{1,0:T(8,128)} %get-tuple-element.29), channel_id=1, source_target_pairs={{0,1},{1,2},{2,3},{3,4},{4,5},{5,6},{6,7},{8,9},{9,10},{10,11},{11... | collective-permute-start | bytes 1646600 | tf_op jit(solution)/shard_map/ppermute | solution.py:588
  10.7 23.8 %collective-permute-start.1 = (f32[1072,128]{1,0:T(8,128)}, f32[1072,128]{1,0:T(8,128)S(1)}, u32[]{:S(2)}, u32[]{:S(2)}) collective-permute-start(f32[1072,128]{1,0:T(8,128)} %get-tuple-element.30), channel_id=1, source_target_pairs={{1,0},{2,1},{3,2},{4,3},{5,4},{6,5},{7,6},{9,8},{10,9},{11,10},{12... | collective-permute-start | bytes 1646600 | tf_op jit(solution)/shard_map/ppermute | solution.py:589
  12.9 45.5 %copy-start.11 = (f32[16,512]{1,0:T(8,128)}, f32[16,512]{1,0:T(8,128)S(1)}, u32[]{:S(2)}) copy-start(f32[16,512]{1,0:T(8,128)S(1)} %maximum_maximum_fusion.runs_ref) | copy-start | bytes 98308
  34.5 0.9 copy-start
  34.5 1.0 copy-start.1
  50.9 46.0 %collective-permute-start.7 = (f32[128,1024]{1,0:T(8,128)}, f32[128,1024]{1,0:T(8,128)S(1)}, u32[]{:S(2)}, u32[]{:S(2)}) collective-permute-start(f32[128,1024]{1,0:T(8,128)} %get-tuple-element.40), channel_id=1, source_target_pairs={{0,8},{8,0},{16,24},{24,16},{1,9},{9,1},{17,25},{25,17},{2,10},{10... | collective-permute-start | bytes 1572872 | tf_op jit(solution)/shard_map/ppermute | solution.py:626
  51.0 26.9 %collective-permute-start.2 = (f32[992,128]{1,0:T(8,128)}, f32[992,128]{1,0:T(8,128)S(1)}, u32[]{:S(2)}, u32[]{:S(2)}) collective-permute-start(f32[992,128]{1,0:T(8,128)} %get-tuple-element.31), channel_id=1, source_target_pairs={{0,1},{1,2},{2,3},{3,4},{4,5},{5,6},{6,7},{8,9},{9,10},{10,11},{11... | collective-permute-start | bytes 1523720 | tf_op jit(solution)/shard_map/ppermute | solution.py:588
  55.3 22.6 %collective-permute-start.3 = (f32[992,128]{1,0:T(8,128)}, f32[992,128]{1,0:T(8,128)S(1)}, u32[]{:S(2)}, u32[]{:S(2)}) collective-permute-start(f32[992,128]{1,0:T(8,128)} %get-tuple-element.32), channel_id=1, source_target_pairs={{1,0},{2,1},{3,2},{4,3},{5,4},{6,5},{7,6},{9,8},{10,9},{11,10},{12... | collective-permute-start | bytes 1523720 | tf_op jit(solution)/shard_map/ppermute | solution.py:589
  56.8 49.6 %collective-permute-start.8 = (f32[128,1024]{1,0:T(8,128)}, f32[128,1024]{1,0:T(8,128)S(1)}, u32[]{:S(2)}, u32[]{:S(2)}) collective-permute-start(f32[128,1024]{1,0:T(8,128)} %get-tuple-element.41), channel_id=1, source_target_pairs={{0,16},{8,24},{16,0},{24,8},{1,17},{9,25},{17,1},{25,9},{2,18},{10... | collective-permute-start | bytes 1572872 | tf_op jit(solution)/shard_map/ppermute | solution.py:626
  58.3 48.1 %collective-permute-start.9 = (f32[128,1024]{1,0:T(8,128)}, f32[128,1024]{1,0:T(8,128)S(1)}, u32[]{:S(2)}, u32[]{:S(2)}) collective-permute-start(f32[128,1024]{1,0:T(8,128)} %get-tuple-element.42), channel_id=1, source_target_pairs={{0,24},{8,16},{16,8},{24,0},{1,25},{9,17},{17,9},{25,1},{2,26},{10... | collective-permute-start | bytes 1572872 | tf_op jit(solution)/shard_map/ppermute | solution.py:626
  77.9 0.8 copy-start.8
  78.8 0.8 copy-start.9
  95.2 24.4 %collective-permute-start.4 = (f32[128,1024]{1,0:T(8,128)}, f32[128,1024]{1,0:T(8,128)S(1)}, u32[]{:S(2)}, u32[]{:S(2)}) collective-permute-start(f32[128,1024]{1,0:T(8,128)} %get-tuple-element.34), channel_id=1, source_target_pairs={{0,8},{8,0},{16,24},{24,16},{1,9},{9,1},{17,25},{25,17},{2,10},{10... | collective-permute-start | bytes 1572872 | tf_op jit(solution)/shard_map/ppermute | solution.py:626
  95.3 24.3 %collective-permute-start.5 = (f32[128,1024]{1,0:T(8,128)}, f32[128,1024]{1,0:T(8,128)S(1)}, u32[]{:S(2)}, u32[]{:S(2)}) collective-permute-start(f32[128,1024]{1,0:T(8,128)} %get-tuple-element.35), channel_id=1, source_target_pairs={{0,16},{8,24},{16,0},{24,8},{1,17},{9,25},{17,1},{25,9},{2,18},{10... | collective-permute-start | bytes 1572872 | tf_op jit(solution)/shard_map/ppermute | solution.py:626
  96.9 9.5 %copy-start.2 = (f32[128,1024]{1,0:T(8,128)}, f32[128,1024]{1,0:T(8,128)S(1)}, u32[]{:S(2)}) copy-start(f32[128,1024]{1,0:T(8,128)S(1)} %collective-permute-done.7.refs_3_) | copy-start | bytes 1572868
  96.9 23.7 %collective-permute-start.6 = (f32[128,1024]{1,0:T(8,128)}, f32[128,1024]{1,0:T(8,128)S(1)}, u32[]{:S(2)}, u32[]{:S(2)}) collective-permute-start(f32[128,1024]{1,0:T(8,128)} %get-tuple-element.36), channel_id=1, source_target_pairs={{0,24},{8,16},{16,8},{24,0},{1,25},{9,17},{17,9},{25,1},{2,26},{10... | collective-permute-start | bytes 1572872 | tf_op jit(solution)/shard_map/ppermute | solution.py:626
  106.4 0.8 copy-start.3
  106.4 1.0 copy-start.4
  119.6 0.9 copy-start.5
  119.6 1.0 copy-start.6
  120.5 0.8 copy-start.7
  132.2 1.6 collective-permute-start.10
  134.9 6.2 %collective-permute-start.11 = (f32[288,128]{1,0:T(8,128)S(1)}, f32[288,128]{1,0:T(8,128)S(1)}, u32[]{:S(2)}, u32[]{:S(2)}) collective-permute-start(f32[288,128]{1,0:T(8,128)S(1)} %constant_dynamic-slice_fusion), channel_id=1, source_target_pairs={{0,16},{8,24},{16,0},{24,8},{1,17},{9,25},{17,1},{25,9},{2,18},{10... | collective-permute-start | bytes 442376 | tf_op jit(solution)/shard_map/ppermute | solution.py:547
  141.1 6.0 %collective-permute-start.12 = (f32[288,128]{1,0:T(8,128)S(1)}, f32[288,128]{1,0:T(8,128)S(1)}, u32[]{:S(2)}, u32[]{:S(2)}) collective-permute-start(f32[288,128]{1,0:T(8,128)S(1)} %dynamic-slice_add_fusion.1), channel_id=1, source_target_pairs={{0,1},{1,0},{2,3},{3,2},{4,5},{5,4},{6,7},{7,6},{8,9},{9,8},{10,11... | collective-permute-start | bytes 442376 | tf_op jit(solution)/shard_map/ppermute | solution.py:564
  147.1 5.8 %collective-permute-start.13 = (f32[288,128]{1,0:T(8,128)S(1)}, f32[288,128]{1,0:T(8,128)S(1)}, u32[]{:S(2)}, u32[]{:S(2)}) collective-permute-start(f32[288,128]{1,0:T(8,128)S(1)} %add.25), channel_id=1, source_target_pairs={{0,2},{1,3},{2,0},{3,1},{4,6},{5,7},{6,4},{7,5},{8,10},{9,11},{10,... | collective-permute-start | bytes 442376 | tf_op jit(solution)/shard_map/ppermute | solution.py:564
  152.9 7.8 %collective-permute-start.14 = (f32[288,128]{1,0:T(8,128)S(1)}, f32[288,128]{1,0:T(8,128)S(1)}, u32[]{:S(2)}, u32[]{:S(2)}) collective-permute-start(f32[288,128]{1,0:T(8,128)S(1)} %add.26), channel_id=1, source_target_pairs={{0,4},{1,5},{2,6},{3,7},{4,0},{5,1},{6,2},{7,3},{8,12},{9,13},{10,... | collective-permute-start | bytes 442376 | tf_op jit(solution)/shard_map/ppermute | solution.py:564
  160.7 5.2 %collective-permute-start.15 = (f32[288,128]{1,0:T(8,128)S(1)}, f32[288,128]{1,0:T(8,128)S(1)}, u32[]{:S(2)}, u32[]{:S(2)}) collective-permute-start(f32[288,128]{1,0:T(8,128)S(1)} %add.27), channel_id=1, source_target_pairs={{0,16},{8,24},{16,0},{24,8},{1,17},{9,25},{17,1},{25,9},{2,18},{10... | collective-permute-start | bytes 442376 | tf_op jit(solution)/shard_map/ppermute | solution.py:553
  165.9 9.0 %collective-permute-start.16 = (f32[576,128]{1,0:T(8,128)S(1)}, f32[576,128]{1,0:T(8,128)S(1)}, u32[]{:S(2)}, u32[]{:S(2)}) collective-permute-start(f32[576,128]{1,0:T(8,128)S(1)} %maximum_select_fusion.1), channel_id=1, source_target_pairs={{0,8},{8,0},{16,24},{24,16},{1,9},{9,1},{17,25},{25,17},{2,10},{10... | collective-permute-start | bytes 884744 | tf_op jit(solution)/shard_map/ppermute | solution.py:553

commit v3 on v2

--- a/solution.py
+++ b/solution.py
@@ -20,6 +20,10 @@
 SPACE = pl.BlockSpec(memory_space=pltpu.VMEM)
 ANY = pl.BlockSpec(memory_space=pl.ANY)
 SCALARS = pl.BlockSpec(memory_space=pltpu.SMEM)
+
+
+def in_vmem(x):
+    return pltpu.with_memory_space_constraint(x, pltpu.VMEM)
 
 
 def cost(flops, nbytes, transcendentals=0):
@@ -83,18 +87,26 @@
 
 
 def diffuse_kernel(chunk, chunks, ends_ref, grp_ref, field_ref, ids_ref, runs_ref, *refs):
-    edges, outs = refs[: 2 + 2 * (chunk > 0)], refs[2 + 2 * (chunk > 0) : -9]
-    raw_ref, u0_ref, u1_ref, d_ref, a_ref, b_ref, fx_ref, v_ref, sem = refs[-9:]
-    cols = ids_ref.shape[2]
-    rows = field_ref.shape[1]
+    edges, outs = refs[: 2 + 2 * (chunk > 0)], refs[2 + 2 * (chunk > 0) : -11]
+    raw_ref, u0_ref, u1_ref, d_ref, a_ref, b_ref, fx_ref, v_ref, wide_ref, made_ref, sem = refs[-11:]
+    rows, cols = ids_ref.shape
     total = rows + 2 * STEPS
     parts = spans(cols, chunks)
     low, high, sent = parts[chunk]
     width = high - low
     own = cols // chunks
     tile0, tile1 = low // LANES, -(-high // LANES)
-    copy = pltpu.make_async_copy(field_ref.at[:, :, tile0 * LANES : tile1 * LANES], raw_ref, sem)
+    copy = pltpu.make_async_copy(field_ref.at[:, :, tile0 * LANES : tile1 * LANES], raw_ref, sem.at[0])
     copy.start()
+    brought = STEPS * (parts[0][1] - parts[0][2])
+    for j in range(tile0, tile1):
+        at = slice(j * LANES, (j + 1) * LANES)
+        for side in range(2):
+            for r in range(STEPS):
+                line = brought + r * (cols // LANES) + j
+                wide_ref[side * (total - STEPS) + r, :, at] = edges[side - 2][line : line + 1, :]
+        for r in range(rows):
+            wide_ref[STEPS + r, :, at] = ids_ref[r : r + 1, at].astype(F32)
 
     level, pick, steep = runs_ref[0:LEVELS], runs_ref[LEVELS : LEVELS + 1], runs_ref[LEVELS + 1 : LEVELS + 2]
     table = 0.03 * jnp.exp(level * jnp.log(F32(1.35)))
@@ -106,7 +118,7 @@
         both = both - piece
     pieces.append(jnp.zeros_like(both))
     tables = jnp.concatenate(pieces, axis=0).astype(BF16)
-    klass = lax.broadcasted_iota(jnp.int32, (4 * LEVELS, LANES), 0) % LEVELS
+    klass = (lax.broadcasted_iota(jnp.int32, (4 * LEVELS, LANES), 0) % LEVELS).astype(F32)
     pick8 = jnp.broadcast_to(pick, (SUB, LANES))
     has_top, has_bottom = ends_ref[0], ends_ref[1]
     zeros = jnp.zeros((SUB, LANES), F32)
@@ -116,7 +128,7 @@
 
     def coefficients(r, carry):
         valid = inside(r)
-        ids = ids_ref[r]
+        ids = wide_ref[r]
         for j in range(tile0, tile1):
             here = jnp.broadcast_to(ids[:, j * LANES : (j + 1) * LANES], klass.shape)
             onehot = jnp.where(here == klass, valid, 0.0)
@@ -194,16 +206,21 @@
 
     result = u0_ref if STEPS % 2 == 0 else u1_ref
     per_block = rows // len(outs)
-    for offset, out_ref in enumerate(outs):
+    done = []
+    for offset in list(range(1, len(outs))) + [0]:
         row = STEPS + (grp_ref[0] ^ offset) * per_block
         for i in range(per_block):
             for j in range(own // LANES):
                 p = SUB + chunk * own + j * LANES - low
                 at = i * own + j * LANES
-                out_ref[:, at : at + LANES] = jnp.transpose(result[row + i, p : p + LANES, :])
-
-
-def diffuse(chunk, chunks, start_field, edges, ids_wide, run_rows, ends, grp, blocks):
+                made_ref[offset, :, at : at + LANES] = jnp.transpose(result[row + i, p : p + LANES, :])
+        done.append(pltpu.make_async_copy(made_ref.at[offset], outs[offset], sem.at[1 + offset]))
+        done[-1].start()
+    for sent_out in done:
+        sent_out.wait()
+
+
+def diffuse(chunk, chunks, start_field, edges, ids, run_rows, ends, grp, blocks):
     runs, rows, cols = start_field.shape
     total = rows + 2 * STEPS
     low, high, _ = spans(cols, chunks)[chunk]
@@ -215,7 +232,7 @@
     return pl.pallas_call(
         functools.partial(diffuse_kernel, chunk, chunks),
         in_specs=[SCALARS, SCALARS, ANY, SPACE, SPACE] + [SPACE] * len(edges),
-        out_specs=[SPACE] * blocks,
+        out_specs=[ANY] * blocks,
         out_shape=[jax.ShapeDtypeStruct((runs, rows * own // blocks), F32)] * blocks,
         scratch_shapes=[
             pltpu.VMEM((runs, rows, tiles * LANES), F32),
@@ -226,11 +243,13 @@
             pltpu.VMEM((total, width, runs), F32),
             pltpu.VMEM((width + 2 * SUB, runs), F32),
             pltpu.VMEM((width, runs), F32),
-            pltpu.SemaphoreType.DMA,
+            pltpu.VMEM((total, 1, cols), F32),
+            pltpu.VMEM((blocks, runs, rows * own // blocks), F32),
+            pltpu.SemaphoreType.DMA((blocks + 1,)),
         ],
         cost_estimate=cost(100 * runs * total * width, 12 * runs * total * width),
         name="diffuse",
-    )(ends, grp, start_field, ids_wide, run_rows, *edges)
+    )(ends, grp, start_field, ids, run_rows, *edges)
 
 
 PITCH = 80
@@ -383,7 +402,11 @@
     total = jnp.zeros((1, own), F32)
     for offset, target_ref in enumerate(targets):
         at = pl.ds(pl.multiple_of((grp_ref[0] ^ offset) * per_source, per_source), per_source)
-        error = guess_ref[at, :] - target_ref[...]
+        if offset:
+            target = target_ref[:, pl.ds(pl.multiple_of(step * own, own), own)]
+        else:
+            target = target_ref[...]
+        error = guess_ref[at, :] - target
         misfit_ref[at, :] = error.astype(BF16)
         slope = (error * scale).astype(BF16)
         slope_ref[at, :] = slope
@@ -432,7 +455,7 @@
     last, has_before = chunk == chunks - 1, before is not None
     strip = lambda i: (0, i * chunks + chunk)
     in_specs = [SCALARS, pl.BlockSpec((runs, own), strip)]
-    in_specs += [pl.BlockSpec((per_source, own), lambda i: (0, i))] * sources
+    in_specs += [pl.BlockSpec((per_source, own), lambda i: (0, i))] + [SPACE] * (sources - 1)
     in_specs += [pl.BlockSpec((hid, own), strip), pl.BlockSpec((1, own), strip), ANY, SPACE]
     args = [grp, guess, *targets, weight, bias, gain_t, feats]
     if not last:
@@ -587,7 +610,7 @@
         top, bottom = packed[2 * c], packed[2 * c + 1]
         above = lax.ppermute(bottom, "tile", up)
         below = lax.ppermute(top, "tile", down)
-        edges.append((above, below))
+        edges.append((in_vmem(above), in_vmem(below)))
 
     run_rows = jnp.concatenate(
         [
@@ -600,16 +623,6 @@
     )
     run_rows_here = lax.dynamic_slice_in_dim(run_rows, first_run, local_runs, 1)
     ends = jnp.stack([(tile > 0).astype(F32), (tile < n_tile - 1).astype(F32)])
-    brought = STEPS * (parts[0][1] - parts[0][2])
-    ids_wide = jnp.concatenate(
-        [
-            edges[0][0][brought:].reshape(STEPS, cols).astype(jnp.int32),
-            class_ids,
-            edges[0][1][brought:].reshape(STEPS, cols).astype(jnp.int32),
-        ],
-        axis=0,
-    )[:, None, :]
-
     hidden, hidden_t, gain_t, project = hidden_units(run_rows, input_layer)
     bias_row = output_bias[None, :]
     guess = predict(hidden, output_layer, bias_row)
@@ -619,11 +632,11 @@
     scale = 2.0 / runs_total
     grp = lax.axis_index("grp").astype(jnp.int32)[None]
     for c in range(chunks):
-        snaps = diffuse(c, chunks, start_field, edges, ids_wide, run_rows_here, ends, grp, n_grp)
+        snaps = diffuse(c, chunks, start_field, edges, class_ids, run_rows_here, ends, grp, n_grp)
         targets = [snaps[0]]
         for offset in range(1, n_grp):
             pairs = [(i, i ^ offset) for i in range(n_grp)]
-            targets.append(lax.ppermute(snaps[offset], "grp", pairs))
+            targets.append(in_vmem(lax.ppermute(snaps[offset], "grp", pairs)))
         before = state
         state = learn(
             c, chunks, cols, grp, guess, targets, output_layer, bias_row,
@@ -654,6 +667,4 @@
     )
     out_specs = (P(None, ("grp", "tile")), P(None, ("grp", "tile")), P(("grp", "tile")), P())
 
-    return jax.shard_map(
-        on_device, mesh=mesh, in_specs=in_specs, out_specs=out_specs, check_vma=False
-    )
+    return jax.shard_map(on_device, mesh=mesh, in_specs=in_specs, out_specs=out_specs, check_vma=False)

time: 179 us -> 174 us (0.972)
  local copies, waits for them, and re-layouts: 6.03 us -> 3.54 us
  Pallas kernels: 84.9 us -> 82.6 us
where the time goes in v3:
time: 174 us
  Pallas kernels  82.6 us (47%)
  waiting for transfers between devices  55.7 us (32%)
  starting transfers between devices  28.4 us (16%)
  local copies, waits for them, and re-layouts  3.54 us (2%)
  other arithmetic  2.66 us (2%)
    ppermute x2, waiting for transfers between devices, on_device(): above = lax.ppermute(bottom, 'tile', up)  34.2 us
    pallas_call x2, Pallas kernels, diffuse(): pl.pallas_call(functools.partial(diffuse_kernel, chunk, chunks), in_specs...  29.9 us
    pallas_call x2, Pallas kernels, learn(): pl.pallas_call(functools.partial(learn_kernel, last, has_before, scale, s...  21 us
    ppermute x3, waiting for transfers between devices, sum_over_devices(): x = x + lax.ppermute(x, 'tile', [(i, i ^ bit) for i in range(tile)])  11.3 us
    pallas_call x1, Pallas kernels, predict(): pl.pallas_call(predict_kernel, grid=(cells // block,), in_specs=[pl.Block...  9.29 us
    ppermute x2, starting transfers between devices, on_device(): above = lax.ppermute(bottom, 'tile', up)  9.23 us
    ppermute x3, starting transfers between devices, sum_over_devices(): x = x + lax.ppermute(x, 'tile', [(i, i ^ bit) for i in range(tile)])  9.2 us
    pallas_call x2, Pallas kernels, update(): pl.pallas_call(update_kernel, grid=(count,), in_specs=[pl.BlockSpec((hid,...  8.95 us
  transfers between devices with their start and end apart: 17, of which 9 were waited for; matrix products, arithmetic and copies ran while one was open for 1% of the time, Pallas kernels for 29%

profile of v3, /device:TPU:0, one launch (start us, length us, event | category | flops | bytes accessed | tf_op | source)
XLA Modules:
  0.0 173.8 jit_solution(16654942665741632448)
XLA Ops:
  0.7 5.0 %pack_edges.1 = (f32[1072,128]{1,0:T(8,128)}, f32[1072,128]{1,0:T(8,128)}, f32[992,128]{1,0:T(8,128)}, f32[992,128]{1,0:T(8,128)}) custom-call(f32[128,16,512]{2,1,0:T(8,128)} %field_ref.5, s32[16,512]{1,0:T(8,128)} %ids_ref.5), custom_call_target="tpu_custom_call" | custom-call | bytes 6291456 | tf_op jit(solution)/shard_map/pack_edges/pallas_call | solution.py:75
  5.6 4.9 %collective-permute-start.2 = (f32[1072,128]{1,0:T(8,128)}, f32[1072,128]{1,0:T(8,128)S(1)}, u32[]{:S(2)}, u32[]{:S(2)}) collective-permute-start(f32[1072,128]{1,0:T(8,128)} %get-tuple-element.31), channel_id=1, source_target_pairs={{0,1},{1,2},{2,3},{3,4},{4,5},{5,6},{6,7},{8,9},{9,10},{10,11},{11... | collective-permute-start | bytes 1646600 | tf_op jit(solution)/shard_map/ppermute | solution.py:611
  10.6 1.3 collective-permute-start.3
  13.3 21.0 %collective-permute-done.2.refs_2_.refs_0_ = f32[1072,128]{1,0:T(8,128)S(1)} collective-permute-done((f32[1072,128]{1,0:T(8,128)}, f32[1072,128]{1,0:T(8,128)S(1)}, u32[]{:S(2)}, u32[]{:S(2)}) %collective-permute-start.2) | collective-permute-done | bytes 548896 | tf_op jit(solution)/shard_map/ppermute | solution.py:611
  34.3 14.9 %diffuse.3 = (f32[128,1024]{1,0:T(8,128)}, f32[128,1024]{1,0:T(8,128)}, f32[128,1024]{1,0:T(8,128)}, f32[128,1024]{1,0:T(8,128)}) custom-call(f32[2]{0:T(128)} %add_convert_fusion.ends_ref, s32[1]{0:T(128)} %bitcast.grp_ref.refs_0_, f32[128,16,512]{2,1,0:T(8,128)} %field_ref.5, s32[16,512]{1,0:T(8,128)} %ids_ref.5, ...), custom_call_target="tpu_custom_call" | custom-call | flops 81100800 | bytes 9732096 | tf_op jit(solution)/shard_map/diffuse/pallas_call | solution.py:232
  49.3 4.3 %collective-permute-start = (f32[992,128]{1,0:T(8,128)}, f32[992,128]{1,0:T(8,128)S(1)}, u32[]{:S(2)}, u32[]{:S(2)}) collective-permute-start(f32[992,128]{1,0:T(8,128)} %get-tuple-element.29), channel_id=1, source_target_pairs={{0,1},{1,2},{2,3},{3,4},{4,5},{5,6},{6,7},{8,9},{9,10},{10,11},{11... | collective-permute-start | bytes 1523720 | tf_op jit(solution)/shard_map/ppermute | solution.py:611
  53.6 1.5 collective-permute-start.1
  55.1 1.6 collective-permute-start.8
  56.7 6.3 %hidden_units.1 = (bf16[512,2048]{1,0:T(8,128)(2,1)}, bf16[2048,512]{1,0:T(8,128)(2,1)}, f32[2048,512]{1,0:T(8,128)}, bf16[512,128]{1,0:T(8,128)(2,1)}) custom-call(f32[16,512]{1,0:T(8,128)} %copy-done.2, f32[69,2048]{1,0:T(8,128)} %layer_ref.3), custom_call_target="tpu_custom_call" | custom-call | flops 1073741824 | bytes 10485760 | tf_op jit(solution)/shard_map/hidden_units/pallas_call | solution.py:323
  63.0 13.2 %collective-permute-done.refs_0_ = f32[992,128]{1,0:T(8,128)S(1)} collective-permute-done((f32[992,128]{1,0:T(8,128)}, f32[992,128]{1,0:T(8,128)S(1)}, u32[]{:S(2)}, u32[]{:S(2)}) %collective-permute-start) | collective-permute-done | bytes 507936 | tf_op jit(solution)/shard_map/ppermute | solution.py:611
  76.2 15.0 %diffuse.2 = (f32[128,1024]{1,0:T(8,128)}, f32[128,1024]{1,0:T(8,128)}, f32[128,1024]{1,0:T(8,128)}, f32[128,1024]{1,0:T(8,128)}) custom-call(f32[2]{0:T(128)} %add_convert_fusion.ends_ref, s32[1]{0:T(128)} %bitcast.grp_ref.refs_0_, f32[128,16,512]{2,1,0:T(8,128)} %field_ref.5, s32[16,512]{1,0:T(8,128)} %ids_ref.5, ...), custom_call_target="tpu_custom_call" | custom-call | flops 81100800 | bytes 9732096 | tf_op jit(solution)/shard_map/diffuse/pallas_call | solution.py:232
  91.3 1.6 collective-permute-start.5
  93.2 9.3 %predict.1.refs_1_ = f32[512,2048]{1,0:T(8,128)} custom-call(bf16[512,2048]{1,0:T(8,128)(2,1)} %get-tuple-element.28.hidden_ref, bf16[2048,2048]{1,0:T(8,128)(2,1)} %weight_ref.5, f32[1,2048]{1,0:T(1,128)} %bitcast.14), custom_call_target="tpu_custom_call" | custom-call | flops 4294967296 | bytes 12582912 | tf_op jit(solution)/shard_map/predict/pallas_call | solution.py:362
  103.3 1.0 copy-done.1
  104.3 11.7 %learn.2 = (bf16[512,2048]{1,0:T(8,128)(2,1)}, f32[1,2048]{1,0:T(1,128)}, f32[2048,128]{1,0:T(8,128)}, bf16[2048,2048]{1,0:T(8,128)(2,1)}) custom-call(s32[1]{0:T(128)} %bitcast.grp_ref.refs_0_, f32[512,2048]{1,0:T(8,128)} %predict.1.refs_1_, f32[128,1024]{1,0:T(8,128)} %get-tuple-element.39.refs_2_, f32[128,1024]{1,0:T(8,128)S(1)} %collective-permute-done.7.refs_3_, ...), custom_call_target="tpu_custom_call" | custom-call | flops 4831838208 | bytes 14680064 | tf_op jit(solution)/shard_map/learn/pallas_call | solution.py:484
  116.6 9.4 %learn.3 = (bf16[512,2048]{1,0:T(8,128)(2,1)}, f32[1,2048]{1,0:T(1,128)}, f32[16,72,128]{2,1,0:T(8,128)}, bf16[512,1024]{1,0:T(8,128)(2,1)}) custom-call(s32[1]{0:T(128)} %bitcast.grp_ref.refs_0_, f32[512,2048]{1,0:T(8,128)} %predict.1.refs_1_, f32[128,1024]{1,0:T(8,128)} %get-tuple-element.33.refs_2_, ...), custom_call_target="tpu_custom_call", output_to_operand_aliasing={{0}: (10, {}), {1}: (11, {})} | custom-call | flops 2684354560 | bytes 10485760 | tf_op jit(solution)/shard_map/learn/pallas_call | solution.py:484
  126.0 1.0 constant_dynamic-slice_fusion.1
  127.4 1.2 collective-permute-done.10
  128.7 1.0 dynamic-slice_add_fusion
  129.7 1.6 collective-permute-start.11
  131.2 4.6 %collective-permute-done.11 = f32[288,128]{1,0:T(8,128)S(1)} collective-permute-done((f32[288,128]{1,0:T(8,128)S(1)}, f32[288,128]{1,0:T(8,128)S(1)}, u32[]{:S(2)}, u32[]{:S(2)}) %collective-permute-start.11) | collective-permute-done | bytes 147488 | tf_op jit(solution)/shard_map/ppermute | solution.py:570
  135.9 2.4 %collective-permute-start.12 = (f32[288,128]{1,0:T(8,128)S(1)}, f32[288,128]{1,0:T(8,128)S(1)}, u32[]{:S(2)}, u32[]{:S(2)}) collective-permute-start(f32[288,128]{1,0:T(8,128)S(1)} %dynamic-slice_add_fusion.1), channel_id=1, source_target_pairs={{0,1},{1,0},{2,3},{3,2},{4,5},{5,4},{6,7},{7,6},{8,9},{9,8},{10,11... | collective-permute-start | bytes 442376 | tf_op jit(solution)/shard_map/ppermute | solution.py:587
  138.3 3.5 %collective-permute-done.12 = f32[288,128]{1,0:T(8,128)S(1)} collective-permute-done((f32[288,128]{1,0:T(8,128)S(1)}, f32[288,128]{1,0:T(8,128)S(1)}, u32[]{:S(2)}, u32[]{:S(2)}) %collective-permute-start.12) | collective-permute-done | bytes 147488 | tf_op jit(solution)/shard_map/ppermute | solution.py:587
  141.9 3.7 %collective-permute-start.13 = (f32[288,128]{1,0:T(8,128)S(1)}, f32[288,128]{1,0:T(8,128)S(1)}, u32[]{:S(2)}, u32[]{:S(2)}) collective-permute-start(f32[288,128]{1,0:T(8,128)S(1)} %add.25), channel_id=1, source_target_pairs={{0,2},{1,3},{2,0},{3,1},{4,6},{5,7},{6,4},{7,5},{8,10},{9,11},{10,... | collective-permute-start | bytes 442376 | tf_op jit(solution)/shard_map/ppermute | solution.py:587
  145.5 3.1 %collective-permute-done.13 = f32[288,128]{1,0:T(8,128)S(1)} collective-permute-done((f32[288,128]{1,0:T(8,128)S(1)}, f32[288,128]{1,0:T(8,128)S(1)}, u32[]{:S(2)}, u32[]{:S(2)}) %collective-permute-start.13) | collective-permute-done | bytes 147488 | tf_op jit(solution)/shard_map/ppermute | solution.py:587
  148.7 3.1 %collective-permute-start.14 = (f32[288,128]{1,0:T(8,128)S(1)}, f32[288,128]{1,0:T(8,128)S(1)}, u32[]{:S(2)}, u32[]{:S(2)}) collective-permute-start(f32[288,128]{1,0:T(8,128)S(1)} %add.26), channel_id=1, source_target_pairs={{0,4},{1,5},{2,6},{3,7},{4,0},{5,1},{6,2},{7,3},{8,12},{9,13},{10,... | collective-permute-start | bytes 442376 | tf_op jit(solution)/shard_map/ppermute | solution.py:587
  151.8 4.7 %collective-permute-done.14 = f32[288,128]{1,0:T(8,128)S(1)} collective-permute-done((f32[288,128]{1,0:T(8,128)S(1)}, f32[288,128]{1,0:T(8,128)S(1)}, u32[]{:S(2)}, u32[]{:S(2)}) %collective-permute-start.14) | collective-permute-done | bytes 147488 | tf_op jit(solution)/shard_map/ppermute | solution.py:587
  156.5 1.6 collective-permute-start.15
  158.1 3.7 %collective-permute-done.15 = f32[288,128]{1,0:T(8,128)S(1)} collective-permute-done((f32[288,128]{1,0:T(8,128)S(1)}, f32[288,128]{1,0:T(8,128)S(1)}, u32[]{:S(2)}, u32[]{:S(2)}) %collective-permute-start.15) | collective-permute-done | bytes 147488 | tf_op jit(solution)/shard_map/ppermute | solution.py:576
  161.8 4.5 %update.2._ = bf16[2048,2048]{1,0:T(8,128)(2,1)} custom-call(bf16[2048,512]{1,0:T(8,128)(2,1)} %get-tuple-element.43.refs_10_.hidden_t_ref, bf16[512,1024]{1,0:T(8,128)(2,1)} %get-tuple-element.48.slope_ref, bf16[2048,2048]{1,0:T(8,128)(2,1)} %weight_ref.5, bf16[2048,2048]{1,0:T(8,128)(2,1)} %get-tuple-element.49._), custom_call_target="tpu_custom_call", output_to_operand_aliasing={{}: (3, {})} | custom-call | flops 1073741824 | bytes 5242880 | tf_op jit(solution)/shard_map/update/pallas_call | solution.py:522
  166.3 4.5 %update.3 = bf16[2048,2048]{1,0:T(8,128)(2,1)} custom-call(bf16[2048,512]{1,0:T(8,128)(2,1)} %get-tuple-element.43.refs_10_.hidden_t_ref, bf16[512,1024]{1,0:T(8,128)(2,1)} %get-tuple-element.48.slope_ref, bf16[2048,2048]{1,0:T(8,128)(2,1)} %weight_ref.5, bf16[2048,2048]{1,0:T(8,128)(2,1)} %update.2._), custom_call_target="tpu_custom_call", output_to_operand_aliasing={{}: (3, {})} | custom-call | flops 1073741824 | bytes 5242880 | tf_op jit(solution)/shard_map/update/pallas_call | solution.py:522
  171.7 2.1 %finish.1 = f32[69,2048]{1,0:T(8,128)} custom-call(f32[16,72,128]{2,1,0:T(8,128)} %bitcast.11, f32[69,2048]{1,0:T(8,128)} %layer_ref.3), custom_call_target="tpu_custom_call" | custom-call | flops 423936 | bytes 1695744 | tf_op jit(solution)/shard_map/finish/pallas_call | solution.py:550
  (40 shorter events, 4.9 us)
Async XLA Ops:
  0.6 11.2 %copy-start.4 = (s32[512]{0:T(512)S(1)}, s32[512]{0:T(512)}, u32[]{:S(2)}) copy-start(s32[512]{0:T(512)} %param.12) | copy-start | bytes 6148
  0.6 11.9 %copy-start.3 = (s32[512,8]{0,1:T(8,128)S(1)}, s32[512,8]{0,1:T(8,128)}, u32[]{:S(2)}) copy-start(s32[512,8]{0,1:T(8,128)} %param.10) | copy-start | bytes 49156
  0.7 11.9 %copy-start.5 = (f32[512]{0:T(512)S(1)}, f32[512]{0:T(512)}, u32[]{:S(2)}) copy-start(f32[512]{0:T(512)} %param.11) | copy-start | bytes 6148
  5.6 28.7 %collective-permute-start.2 = (f32[1072,128]{1,0:T(8,128)}, f32[1072,128]{1,0:T(8,128)S(1)}, u32[]{:S(2)}, u32[]{:S(2)}) collective-permute-start(f32[1072,128]{1,0:T(8,128)} %get-tuple-element.31), channel_id=1, source_target_pairs={{0,1},{1,2},{2,3},{3,4},{4,5},{5,6},{6,7},{8,9},{9,10},{10,11},{11... | collective-permute-start | bytes 1646600 | tf_op jit(solution)/shard_map/ppermute | solution.py:611
  10.6 23.7 %collective-permute-start.3 = (f32[1072,128]{1,0:T(8,128)}, f32[1072,128]{1,0:T(8,128)S(1)}, u32[]{:S(2)}, u32[]{:S(2)}) collective-permute-start(f32[1072,128]{1,0:T(8,128)} %get-tuple-element.32), channel_id=1, source_target_pairs={{1,0},{2,1},{3,2},{4,3},{5,4},{6,5},{7,6},{9,8},{10,9},{11,10},{12... | collective-permute-start | bytes 1646600 | tf_op jit(solution)/shard_map/ppermute | solution.py:612
  12.7 44.0 %copy-start.2 = (f32[16,512]{1,0:T(8,128)}, f32[16,512]{1,0:T(8,128)S(1)}, u32[]{:S(2)}) copy-start(f32[16,512]{1,0:T(8,128)S(1)} %maximum_maximum_fusion.runs_ref) | copy-start | bytes 98308
  49.2 43.6 %collective-permute-start.7 = (f32[128,1024]{1,0:T(8,128)}, f32[128,1024]{1,0:T(8,128)S(1)}, u32[]{:S(2)}, u32[]{:S(2)}) collective-permute-start(f32[128,1024]{1,0:T(8,128)} %get-tuple-element.40), channel_id=1, source_target_pairs={{0,8},{8,0},{16,24},{24,16},{1,9},{9,1},{17,25},{25,17},{2,10},{10... | collective-permute-start | bytes 1572872 | tf_op jit(solution)/shard_map/ppermute | solution.py:639
  49.3 27.0 %collective-permute-start = (f32[992,128]{1,0:T(8,128)}, f32[992,128]{1,0:T(8,128)S(1)}, u32[]{:S(2)}, u32[]{:S(2)}) collective-permute-start(f32[992,128]{1,0:T(8,128)} %get-tuple-element.29), channel_id=1, source_target_pairs={{0,1},{1,2},{2,3},{3,4},{4,5},{5,6},{6,7},{8,9},{9,10},{10,11},{11... | collective-permute-start | bytes 1523720 | tf_op jit(solution)/shard_map/ppermute | solution.py:611
  53.6 22.6 %collective-permute-start.1 = (f32[992,128]{1,0:T(8,128)}, f32[992,128]{1,0:T(8,128)S(1)}, u32[]{:S(2)}, u32[]{:S(2)}) collective-permute-start(f32[992,128]{1,0:T(8,128)} %get-tuple-element.30), channel_id=1, source_target_pairs={{1,0},{2,1},{3,2},{4,3},{5,4},{6,5},{7,6},{9,8},{10,9},{11,10},{12... | collective-permute-start | bytes 1523720 | tf_op jit(solution)/shard_map/ppermute | solution.py:612
  55.1 47.4 %collective-permute-start.8 = (f32[128,1024]{1,0:T(8,128)}, f32[128,1024]{1,0:T(8,128)S(1)}, u32[]{:S(2)}, u32[]{:S(2)}) collective-permute-start(f32[128,1024]{1,0:T(8,128)} %get-tuple-element.41), channel_id=1, source_target_pairs={{0,16},{8,24},{16,0},{24,8},{1,17},{9,25},{17,1},{25,9},{2,18},{10... | collective-permute-start | bytes 1572872 | tf_op jit(solution)/shard_map/ppermute | solution.py:639
  56.6 46.6 %collective-permute-start.9 = (f32[128,1024]{1,0:T(8,128)}, f32[128,1024]{1,0:T(8,128)}, u32[]{:S(2)}, u32[]{:S(2)}) collective-permute-start(f32[128,1024]{1,0:T(8,128)} %get-tuple-element.42), channel_id=1, source_target_pairs={{0,24},{8,16},{16,8},{24,0},{1,25},{9,17},{17,9},{25,1},{2,26},{10... | collective-permute-start | bytes 1572872 | tf_op jit(solution)/shard_map/ppermute | solution.py:639
  91.2 24.7 %collective-permute-start.4 = (f32[128,1024]{1,0:T(8,128)}, f32[128,1024]{1,0:T(8,128)S(1)}, u32[]{:S(2)}, u32[]{:S(2)}) collective-permute-start(f32[128,1024]{1,0:T(8,128)} %get-tuple-element.34), channel_id=1, source_target_pairs={{0,8},{8,0},{16,24},{24,16},{1,9},{9,1},{17,25},{25,17},{2,10},{10... | collective-permute-start | bytes 1572872 | tf_op jit(solution)/shard_map/ppermute | solution.py:639
  91.3 24.7 %collective-permute-start.5 = (f32[128,1024]{1,0:T(8,128)}, f32[128,1024]{1,0:T(8,128)S(1)}, u32[]{:S(2)}, u32[]{:S(2)}) collective-permute-start(f32[128,1024]{1,0:T(8,128)} %get-tuple-element.35), channel_id=1, source_target_pairs={{0,16},{8,24},{16,0},{24,8},{1,17},{9,25},{17,1},{25,9},{2,18},{10... | collective-permute-start | bytes 1572872 | tf_op jit(solution)/shard_map/ppermute | solution.py:639
  92.9 23.8 %collective-permute-start.6 = (f32[128,1024]{1,0:T(8,128)}, f32[128,1024]{1,0:T(8,128)}, u32[]{:S(2)}, u32[]{:S(2)}) collective-permute-start(f32[128,1024]{1,0:T(8,128)} %get-tuple-element.36), channel_id=1, source_target_pairs={{0,24},{8,16},{16,8},{24,0},{1,25},{9,17},{17,9},{25,1},{2,26},{10... | collective-permute-start | bytes 1572872 | tf_op jit(solution)/shard_map/ppermute | solution.py:639
  102.5 0.8 copy-start
  103.3 1.0 copy-start.1
  127.0 1.6 collective-permute-start.10
  129.7 6.2 %collective-permute-start.11 = (f32[288,128]{1,0:T(8,128)S(1)}, f32[288,128]{1,0:T(8,128)S(1)}, u32[]{:S(2)}, u32[]{:S(2)}) collective-permute-start(f32[288,128]{1,0:T(8,128)S(1)} %constant_dynamic-slice_fusion), channel_id=1, source_target_pairs={{0,16},{8,24},{16,0},{24,8},{1,17},{9,25},{17,1},{25,9},{2,18},{10... | collective-permute-start | bytes 442376 | tf_op jit(solution)/shard_map/ppermute | solution.py:570
  135.9 6.0 %collective-permute-start.12 = (f32[288,128]{1,0:T(8,128)S(1)}, f32[288,128]{1,0:T(8,128)S(1)}, u32[]{:S(2)}, u32[]{:S(2)}) collective-permute-start(f32[288,128]{1,0:T(8,128)S(1)} %dynamic-slice_add_fusion.1), channel_id=1, source_target_pairs={{0,1},{1,0},{2,3},{3,2},{4,5},{5,4},{6,7},{7,6},{8,9},{9,8},{10,11... | collective-permute-start | bytes 442376 | tf_op jit(solution)/shard_map/ppermute | solution.py:587
  141.9 6.8 %collective-permute-start.13 = (f32[288,128]{1,0:T(8,128)S(1)}, f32[288,128]{1,0:T(8,128)S(1)}, u32[]{:S(2)}, u32[]{:S(2)}) collective-permute-start(f32[288,128]{1,0:T(8,128)S(1)} %add.25), channel_id=1, source_target_pairs={{0,2},{1,3},{2,0},{3,1},{4,6},{5,7},{6,4},{7,5},{8,10},{9,11},{10,... | collective-permute-start | bytes 442376 | tf_op jit(solution)/shard_map/ppermute | solution.py:587
  148.7 7.8 %collective-permute-start.14 = (f32[288,128]{1,0:T(8,128)S(1)}, f32[288,128]{1,0:T(8,128)S(1)}, u32[]{:S(2)}, u32[]{:S(2)}) collective-permute-start(f32[288,128]{1,0:T(8,128)S(1)} %add.26), channel_id=1, source_target_pairs={{0,4},{1,5},{2,6},{3,7},{4,0},{5,1},{6,2},{7,3},{8,12},{9,13},{10,... | collective-permute-start | bytes 442376 | tf_op jit(solution)/shard_map/ppermute | solution.py:587
  156.5 5.2 %collective-permute-start.15 = (f32[288,128]{1,0:T(8,128)S(1)}, f32[288,128]{1,0:T(8,128)S(1)}, u32[]{:S(2)}, u32[]{:S(2)}) collective-permute-start(f32[288,128]{1,0:T(8,128)S(1)} %add.27), channel_id=1, source_target_pairs={{0,16},{8,24},{16,0},{24,8},{1,17},{9,25},{17,1},{25,9},{2,18},{10... | collective-permute-start | bytes 442376 | tf_op jit(solution)/shard_map/ppermute | solution.py:576
  161.7 9.0 %collective-permute-start.16 = (f32[576,128]{1,0:T(8,128)S(1)}, f32[576,128]{1,0:T(8,128)S(1)}, u32[]{:S(2)}, u32[]{:S(2)}) collective-permute-start(f32[576,128]{1,0:T(8,128)S(1)} %maximum_select_fusion.1), channel_id=1, source_target_pairs={{0,8},{8,0},{16,24},{24,16},{1,9},{9,1},{17,25},{25,17},{2,10},{10... | collective-permute-start | bytes 884744 | tf_op jit(solution)/shard_map/ppermute | solution.py:576

commit v4 on v3

--- a/solution.py
+++ b/solution.py
@@ -43,45 +43,52 @@
     return out
 
 
-def pack_kernel(parts, field_ref, ids_ref, *outs):
+def pack_kernel(chunk, part, field_ref, ids_ref, *outs):
     rows, cols = ids_ref.shape
-    for j in range(cols // LANES):
-
-        @pl.when(pl.program_id(0) == j)
+    _, high, sent = part
+    for j in range(sent // LANES, -(-high // LANES)):
+
+        @pl.when(pl.program_id(0) == j - sent // LANES)
         def _(j=j):
+            first, last = max(sent, j * LANES), min(high, (j + 1) * LANES)
             for side in range(2):
                 for r in range(STEPS):
                     row = r if side == 0 else rows - STEPS + r
                     tile = jnp.transpose(field_ref[:, row, :])
-                    for c, (_, high, sent) in enumerate(parts):
-                        first, last = max(sent, j * LANES), min(high, (j + 1) * LANES)
-                        if first < last:
-                            at = r * (high - sent) + first - sent
-                            outs[2 * c + side][at : at + last - first, :] = tile[
-                                first - j * LANES : last - j * LANES, :
-                            ]
-                    at = STEPS * (parts[0][1] - parts[0][2]) + r * (cols // LANES) + j
-                    outs[side][at : at + 1, :] = ids_ref[
-                        row : row + 1, j * LANES : (j + 1) * LANES
-                    ].astype(F32)
-
-
-def pack_edges(start_field, ids, parts):
+                    at = r * (high - sent) + first - sent
+                    outs[side][at : at + last - first, :] = tile[
+                        first - j * LANES : last - j * LANES, :
+                    ]
+
+    @pl.when(pl.program_id(0) == 0)
+    def _():
+        if chunk == 0:
+            for side in range(2):
+                for r in range(STEPS):
+                    row = r if side == 0 else rows - STEPS + r
+                    for j in range(cols // LANES):
+                        at = STEPS * (high - sent) + r * (cols // LANES) + j
+                        outs[side][at : at + 1, :] = ids_ref[
+                            row : row + 1, j * LANES : (j + 1) * LANES
+                        ].astype(F32)
+
+
+def pack_edges(chunk, start_field, ids, parts):
     runs, rows, cols = start_field.shape
-    shapes = []
-    for c, (_, high, sent) in enumerate(parts):
-        extra = STEPS * cols // LANES if c == 0 else 0
-        shapes += [jax.ShapeDtypeStruct((STEPS * (high - sent) + extra, runs), F32)] * 2
+    _, high, sent = parts[chunk]
+    extra = STEPS * cols // LANES if chunk == 0 else 0
+    shapes = [jax.ShapeDtypeStruct((STEPS * (high - sent) + extra, runs), F32)] * 2
+    tile0, tile1 = sent // LANES, -(-high // LANES)
     return pl.pallas_call(
-        functools.partial(pack_kernel, parts),
-        grid=(cols // LANES,),
+        functools.partial(pack_kernel, chunk, parts[chunk]),
+        grid=(tile1 - tile0,),
         in_specs=[
-            pl.BlockSpec((runs, rows, LANES), lambda j: (0, 0, j)),
+            pl.BlockSpec((runs, rows, LANES), lambda j: (0, 0, tile0 + j)),
             pl.BlockSpec((rows, cols), lambda j: (0, 0)),
         ],
         out_specs=[pl.BlockSpec(x.shape, lambda j: (0, 0)) for x in shapes],
         out_shape=shapes,
-        cost_estimate=cost(0, 6 * runs * rows * cols),
+        cost_estimate=cost(0, 6 * runs * rows * (high - sent)),
         name="pack_edges",
     )(start_field, ids)
 
@@ -604,10 +611,9 @@
 
     up = [(i, i + 1) for i in range(n_tile - 1)]
     down = [(j, i) for i, j in up]
-    packed = pack_edges(start_field, class_ids, parts)
     edges = []
     for c in range(chunks):
-        top, bottom = packed[2 * c], packed[2 * c + 1]
+        top, bottom = pack_edges(c, start_field, class_ids, parts)
         above = lax.ppermute(bottom, "tile", up)
         below = lax.ppermute(top, "tile", down)
         edges.append((in_vmem(above), in_vmem(below)))
@@ -650,7 +656,7 @@
             first, past - first, chunks, cols, hidden_t, slope, output_layer, output_next
         )
     total = sum_over_devices(partial.reshape(-1, LANES)).reshape(partial.shape)
-    input_next = finish(total, input_layer)
+    input_next = finish(in_vmem(total), in_vmem(input_layer))
     return misfit, output_next, bias_next.reshape(-1), input_next
 
 

time: 174 us -> 175 us (level)
    pallas_call x1 -> x2, Pallas kernels: 4.97 us -> 7.06 us  [pack_edges(): pl.pallas_call(functools.partial(pack_kernel, chunk, parts[chunk]), grid=...]
  transfers between devices with their start and end apart: 17 -> 17, of which waited for: 9 -> 9; matrix products, arithmetic and copies ran while one was open for 1% -> 1% of each run, Pallas kernels for 29% -> 31%
where the time goes in v4:
time: 175 us; the launch traced here: 174 us
  Pallas kernels  83.5 us (48%)
  waiting for transfers between devices  55.8 us (32%)
  starting transfers between devices  28.4 us (16%)
  local copies, waits for them, and re-layouts  3.55 us (2%)
  other arithmetic  1.79 us (1%)
    ppermute x2, waiting for transfers between devices, on_device(): above = lax.ppermute(bottom, 'tile', up)  34.3 us
    pallas_call x2, Pallas kernels, diffuse(): pl.pallas_call(functools.partial(diffuse_kernel, chunk, chunks), in_specs...  29.9 us
    pallas_call x2, Pallas kernels, learn(): pl.pallas_call(functools.partial(learn_kernel, last, has_before, scale, s...  21 us
    ppermute x3, waiting for transfers between devices, sum_over_devices(): x = x + lax.ppermute(x, 'tile', [(i, i ^ bit) for i in range(tile)])  11.3 us
    pallas_call x1, Pallas kernels, predict(): pl.pallas_call(predict_kernel, grid=(cells // block,), in_specs=[pl.Block...  9.23 us
    ppermute x2, starting transfers between devices, on_device(): above = lax.ppermute(bottom, 'tile', up)  9.22 us
    ppermute x3, starting transfers between devices, sum_over_devices(): x = x + lax.ppermute(x, 'tile', [(i, i ^ bit) for i in range(tile)])  9.22 us
    pallas_call x2, Pallas kernels, update(): pl.pallas_call(update_kernel, grid=(count,), in_specs=[pl.BlockSpec((hid,...  9.02 us
  transfers between devices with their start and end apart: 17, of which 9 were waited for; matrix products, arithmetic and copies ran while one was open for 1% of the time, Pallas kernels for 31%

profile of v4, /device:TPU:0, one launch (start us, length us, event | category | flops | bytes accessed | tf_op | source)
XLA Modules:
  0.0 173.9 jit_solution(983948523091836583)
XLA Ops:
  0.7 4.1 %pack_edges.3 = (f32[1072,128]{1,0:T(8,128)}, f32[1072,128]{1,0:T(8,128)}) custom-call(f32[128,16,512]{2,1,0:T(8,128)} %field_ref.7, s32[16,512]{1,0:T(8,128)} %ids_ref.7), custom_call_target="tpu_custom_call" | custom-call | bytes 3244032 | tf_op jit(solution)/shard_map/pack_edges/pallas_call | solution.py:82
  4.8 4.9 %collective-permute-start.2 = (f32[1072,128]{1,0:T(8,128)}, f32[1072,128]{1,0:T(8,128)S(1)}, u32[]{:S(2)}, u32[]{:S(2)}) collective-permute-start(f32[1072,128]{1,0:T(8,128)} %get-tuple-element.31), channel_id=1, source_target_pairs={{0,1},{1,2},{2,3},{3,4},{4,5},{5,6},{6,7},{8,9},{9,10},{10,11},{11... | collective-permute-start | bytes 1646600 | tf_op jit(solution)/shard_map/ppermute | solution.py:617
  9.7 1.3 collective-permute-start.3
  12.4 21.0 %collective-permute-done.2.refs_2_.refs_0_ = f32[1072,128]{1,0:T(8,128)S(1)} collective-permute-done((f32[1072,128]{1,0:T(8,128)}, f32[1072,128]{1,0:T(8,128)S(1)}, u32[]{:S(2)}, u32[]{:S(2)}) %collective-permute-start.2) | collective-permute-done | bytes 548896 | tf_op jit(solution)/shard_map/ppermute | solution.py:617
  33.5 14.9 %diffuse.3 = (f32[128,1024]{1,0:T(8,128)}, f32[128,1024]{1,0:T(8,128)}, f32[128,1024]{1,0:T(8,128)}, f32[128,1024]{1,0:T(8,128)}) custom-call(f32[2]{0:T(128)} %add_convert_fusion.ends_ref, s32[1]{0:T(128)} %bitcast.grp_ref.refs_0_, f32[128,16,512]{2,1,0:T(8,128)} %field_ref.7, s32[16,512]{1,0:T(8,128)} %ids_ref.7, ...), custom_call_target="tpu_custom_call" | custom-call | flops 81100800 | bytes 9732096 | tf_op jit(solution)/shard_map/diffuse/pallas_call | solution.py:239
  48.5 2.9 %pack_edges.2 = (f32[992,128]{1,0:T(8,128)}, f32[992,128]{1,0:T(8,128)}) custom-call(f32[128,16,512]{2,1,0:T(8,128)} %field_ref.7, s32[16,512]{1,0:T(8,128)} %ids_ref.7), custom_call_target="tpu_custom_call" | custom-call | bytes 3047424 | tf_op jit(solution)/shard_map/pack_edges/pallas_call | solution.py:82
  51.4 4.3 %collective-permute-start = (f32[992,128]{1,0:T(8,128)}, f32[992,128]{1,0:T(8,128)S(1)}, u32[]{:S(2)}, u32[]{:S(2)}) collective-permute-start(f32[992,128]{1,0:T(8,128)} %get-tuple-element.29), channel_id=1, source_target_pairs={{0,1},{1,2},{2,3},{3,4},{4,5},{5,6},{6,7},{8,9},{9,10},{10,11},{11... | collective-permute-start | bytes 1523720 | tf_op jit(solution)/shard_map/ppermute | solution.py:617
  55.7 1.5 collective-permute-start.1
  57.2 1.6 collective-permute-start.8
  58.8 6.3 %hidden_units.1 = (bf16[512,2048]{1,0:T(8,128)(2,1)}, bf16[2048,512]{1,0:T(8,128)(2,1)}, f32[2048,512]{1,0:T(8,128)}, bf16[512,128]{1,0:T(8,128)(2,1)}) custom-call(f32[16,512]{1,0:T(8,128)} %copy-done.3, f32[69,2048]{1,0:T(8,128)} %layer_ref.3), custom_call_target="tpu_custom_call" | custom-call | flops 1073741824 | bytes 10485760 | tf_op jit(solution)/shard_map/hidden_units/pallas_call | solution.py:330
  65.1 13.2 %collective-permute-done.refs_0_ = f32[992,128]{1,0:T(8,128)S(1)} collective-permute-done((f32[992,128]{1,0:T(8,128)}, f32[992,128]{1,0:T(8,128)S(1)}, u32[]{:S(2)}, u32[]{:S(2)}) %collective-permute-start) | collective-permute-done | bytes 507936 | tf_op jit(solution)/shard_map/ppermute | solution.py:617
  78.4 15.0 %diffuse.2 = (f32[128,1024]{1,0:T(8,128)}, f32[128,1024]{1,0:T(8,128)}, f32[128,1024]{1,0:T(8,128)}, f32[128,1024]{1,0:T(8,128)}) custom-call(f32[2]{0:T(128)} %add_convert_fusion.ends_ref, s32[1]{0:T(128)} %bitcast.grp_ref.refs_0_, f32[128,16,512]{2,1,0:T(8,128)} %field_ref.7, s32[16,512]{1,0:T(8,128)} %ids_ref.7, ...), custom_call_target="tpu_custom_call" | custom-call | flops 81100800 | bytes 9732096 | tf_op jit(solution)/shard_map/diffuse/pallas_call | solution.py:239
  93.4 1.6 collective-permute-start.5
  95.3 9.2 %predict.1.refs_1_ = f32[512,2048]{1,0:T(8,128)} custom-call(bf16[512,2048]{1,0:T(8,128)(2,1)} %get-tuple-element.28.hidden_ref, bf16[2048,2048]{1,0:T(8,128)(2,1)} %weight_ref.5, f32[1,2048]{1,0:T(1,128)} %bitcast.14), custom_call_target="tpu_custom_call" | custom-call | flops 4294967296 | bytes 12582912 | tf_op jit(solution)/shard_map/predict/pallas_call | solution.py:369
  105.3 1.0 copy-done.2
  106.3 11.7 %learn.2 = (bf16[512,2048]{1,0:T(8,128)(2,1)}, f32[1,2048]{1,0:T(1,128)}, f32[2048,128]{1,0:T(8,128)}, bf16[2048,2048]{1,0:T(8,128)(2,1)}) custom-call(s32[1]{0:T(128)} %bitcast.grp_ref.refs_0_, f32[512,2048]{1,0:T(8,128)} %predict.1.refs_1_, f32[128,1024]{1,0:T(8,128)} %get-tuple-element.39.refs_2_, f32[128,1024]{1,0:T(8,128)S(1)} %collective-permute-done.7.refs_3_, ...), custom_call_target="tpu_custom_call" | custom-call | flops 4831838208 | bytes 14680064 | tf_op jit(solution)/shard_map/learn/pallas_call | solution.py:491
  118.8 9.4 %learn.3 = (bf16[512,2048]{1,0:T(8,128)(2,1)}, f32[1,2048]{1,0:T(1,128)}, f32[16,72,128]{2,1,0:T(8,128)}, bf16[512,1024]{1,0:T(8,128)(2,1)}) custom-call(s32[1]{0:T(128)} %bitcast.grp_ref.refs_0_, f32[512,2048]{1,0:T(8,128)} %predict.1.refs_1_, f32[128,1024]{1,0:T(8,128)} %get-tuple-element.33.refs_2_, ...), custom_call_target="tpu_custom_call", output_to_operand_aliasing={{0}: (10, {}), {1}: (11, {})} | custom-call | flops 2684354560 | bytes 10485760 | tf_op jit(solution)/shard_map/learn/pallas_call | solution.py:491
  128.1 1.0 constant_dynamic-slice_fusion.1
  129.6 1.2 collective-permute-done.10
  130.8 1.0 dynamic-slice_add_fusion
  131.8 1.6 collective-permute-start.11
  133.4 4.6 %collective-permute-done.11 = f32[288,128]{1,0:T(8,128)S(1)} collective-permute-done((f32[288,128]{1,0:T(8,128)S(1)}, f32[288,128]{1,0:T(8,128)S(1)}, u32[]{:S(2)}, u32[]{:S(2)}) %collective-permute-start.11) | collective-permute-done | bytes 147488 | tf_op jit(solution)/shard_map/ppermute | solution.py:577
  138.0 2.4 %collective-permute-start.12 = (f32[288,128]{1,0:T(8,128)S(1)}, f32[288,128]{1,0:T(8,128)S(1)}, u32[]{:S(2)}, u32[]{:S(2)}) collective-permute-start(f32[288,128]{1,0:T(8,128)S(1)} %dynamic-slice_add_fusion.1), channel_id=1, source_target_pairs={{0,1},{1,0},{2,3},{3,2},{4,5},{5,4},{6,7},{7,6},{8,9},{9,8},{10,11... | collective-permute-start | bytes 442376 | tf_op jit(solution)/shard_map/ppermute | solution.py:594
  140.4 3.5 %collective-permute-done.12 = f32[288,128]{1,0:T(8,128)S(1)} collective-permute-done((f32[288,128]{1,0:T(8,128)S(1)}, f32[288,128]{1,0:T(8,128)S(1)}, u32[]{:S(2)}, u32[]{:S(2)}) %collective-permute-start.12) | collective-permute-done | bytes 147488 | tf_op jit(solution)/shard_map/ppermute | solution.py:594
  144.0 3.7 %collective-permute-start.13 = (f32[288,128]{1,0:T(8,128)S(1)}, f32[288,128]{1,0:T(8,128)S(1)}, u32[]{:S(2)}, u32[]{:S(2)}) collective-permute-start(f32[288,128]{1,0:T(8,128)S(1)} %add.25), channel_id=1, source_target_pairs={{0,2},{1,3},{2,0},{3,1},{4,6},{5,7},{6,4},{7,5},{8,10},{9,11},{10,... | collective-permute-start | bytes 442376 | tf_op jit(solution)/shard_map/ppermute | solution.py:594
  147.7 3.1 %collective-permute-done.13 = f32[288,128]{1,0:T(8,128)S(1)} collective-permute-done((f32[288,128]{1,0:T(8,128)S(1)}, f32[288,128]{1,0:T(8,128)S(1)}, u32[]{:S(2)}, u32[]{:S(2)}) %collective-permute-start.13) | collective-permute-done | bytes 147488 | tf_op jit(solution)/shard_map/ppermute | solution.py:594
  150.8 3.1 %collective-permute-start.14 = (f32[288,128]{1,0:T(8,128)S(1)}, f32[288,128]{1,0:T(8,128)S(1)}, u32[]{:S(2)}, u32[]{:S(2)}) collective-permute-start(f32[288,128]{1,0:T(8,128)S(1)} %add.26), channel_id=1, source_target_pairs={{0,4},{1,5},{2,6},{3,7},{4,0},{5,1},{6,2},{7,3},{8,12},{9,13},{10,... | collective-permute-start | bytes 442376 | tf_op jit(solution)/shard_map/ppermute | solution.py:594
  153.9 4.7 %collective-permute-done.14 = f32[288,128]{1,0:T(8,128)S(1)} collective-permute-done((f32[288,128]{1,0:T(8,128)S(1)}, f32[288,128]{1,0:T(8,128)S(1)}, u32[]{:S(2)}, u32[]{:S(2)}) %collective-permute-start.14) | collective-permute-done | bytes 147488 | tf_op jit(solution)/shard_map/ppermute | solution.py:594
  158.6 1.6 collective-permute-start.15
  160.2 3.7 %collective-permute-done.15 = f32[288,128]{1,0:T(8,128)S(1)} collective-permute-done((f32[288,128]{1,0:T(8,128)S(1)}, f32[288,128]{1,0:T(8,128)S(1)}, u32[]{:S(2)}, u32[]{:S(2)}) %collective-permute-start.15) | collective-permute-done | bytes 147488 | tf_op jit(solution)/shard_map/ppermute | solution.py:583
  163.9 4.5 %update.2._ = bf16[2048,2048]{1,0:T(8,128)(2,1)} custom-call(bf16[2048,512]{1,0:T(8,128)(2,1)} %get-tuple-element.43.refs_10_.hidden_t_ref, bf16[512,1024]{1,0:T(8,128)(2,1)} %get-tuple-element.48.slope_ref, bf16[2048,2048]{1,0:T(8,128)(2,1)} %weight_ref.5, bf16[2048,2048]{1,0:T(8,128)(2,1)} %get-tuple-element.49._), custom_call_target="tpu_custom_call", output_to_operand_aliasing={{}: (3, {})} | custom-call | flops 1073741824 | bytes 5242880 | tf_op jit(solution)/shard_map/update/pallas_call | solution.py:529
  168.4 4.5 %update.3 = bf16[2048,2048]{1,0:T(8,128)(2,1)} custom-call(bf16[2048,512]{1,0:T(8,128)(2,1)} %get-tuple-element.43.refs_10_.hidden_t_ref, bf16[512,1024]{1,0:T(8,128)(2,1)} %get-tuple-element.48.slope_ref, bf16[2048,2048]{1,0:T(8,128)(2,1)} %weight_ref.5, bf16[2048,2048]{1,0:T(8,128)(2,1)} %update.2._), custom_call_target="tpu_custom_call", output_to_operand_aliasing={{}: (3, {})} | custom-call | flops 1073741824 | bytes 5242880 | tf_op jit(solution)/shard_map/update/pallas_call | solution.py:529
  (43 shorter events, 4.9 us)
Async XLA Ops:
  0.6 10.4 %copy-start.5 = (s32[512]{0:T(512)S(1)}, s32[512]{0:T(512)}, u32[]{:S(2)}) copy-start(s32[512]{0:T(512)} %param.12) | copy-start | bytes 6148
  0.6 11.1 %copy-start.4 = (s32[512,8]{0,1:T(8,128)S(1)}, s32[512,8]{0,1:T(8,128)}, u32[]{:S(2)}) copy-start(s32[512,8]{0,1:T(8,128)} %param.10) | copy-start | bytes 49156
  0.7 11.1 %copy-start.6 = (f32[512]{0:T(512)S(1)}, f32[512]{0:T(512)}, u32[]{:S(2)}) copy-start(f32[512]{0:T(512)} %param.11) | copy-start | bytes 6148
  4.8 28.7 %collective-permute-start.2 = (f32[1072,128]{1,0:T(8,128)}, f32[1072,128]{1,0:T(8,128)S(1)}, u32[]{:S(2)}, u32[]{:S(2)}) collective-permute-start(f32[1072,128]{1,0:T(8,128)} %get-tuple-element.31), channel_id=1, source_target_pairs={{0,1},{1,2},{2,3},{3,4},{4,5},{5,6},{6,7},{8,9},{9,10},{10,11},{11... | collective-permute-start | bytes 1646600 | tf_op jit(solution)/shard_map/ppermute | solution.py:617
  9.7 23.7 %collective-permute-start.3 = (f32[1072,128]{1,0:T(8,128)}, f32[1072,128]{1,0:T(8,128)S(1)}, u32[]{:S(2)}, u32[]{:S(2)}) collective-permute-start(f32[1072,128]{1,0:T(8,128)} %get-tuple-element.32), channel_id=1, source_target_pairs={{1,0},{2,1},{3,2},{4,3},{5,4},{6,5},{7,6},{9,8},{10,9},{11,10},{12... | collective-permute-start | bytes 1646600 | tf_op jit(solution)/shard_map/ppermute | solution.py:618
  11.8 39.6 %copy-start.3 = (f32[16,512]{1,0:T(8,128)}, f32[16,512]{1,0:T(8,128)S(1)}, u32[]{:S(2)}) copy-start(f32[16,512]{1,0:T(8,128)S(1)} %maximum_maximum_fusion.runs_ref) | copy-start | bytes 98308
  48.4 46.6 %collective-permute-start.7 = (f32[128,1024]{1,0:T(8,128)}, f32[128,1024]{1,0:T(8,128)S(1)}, u32[]{:S(2)}, u32[]{:S(2)}) collective-permute-start(f32[128,1024]{1,0:T(8,128)} %get-tuple-element.40), channel_id=1, source_target_pairs={{0,8},{8,0},{16,24},{24,16},{1,9},{9,1},{17,25},{25,17},{2,10},{10... | collective-permute-start | bytes 1572872 | tf_op jit(solution)/shard_map/ppermute | solution.py:645
  51.4 26.9 %collective-permute-start = (f32[992,128]{1,0:T(8,128)}, f32[992,128]{1,0:T(8,128)S(1)}, u32[]{:S(2)}, u32[]{:S(2)}) collective-permute-start(f32[992,128]{1,0:T(8,128)} %get-tuple-element.29), channel_id=1, source_target_pairs={{0,1},{1,2},{2,3},{3,4},{4,5},{5,6},{6,7},{8,9},{9,10},{10,11},{11... | collective-permute-start | bytes 1523720 | tf_op jit(solution)/shard_map/ppermute | solution.py:617
  55.7 22.6 %collective-permute-start.1 = (f32[992,128]{1,0:T(8,128)}, f32[992,128]{1,0:T(8,128)S(1)}, u32[]{:S(2)}, u32[]{:S(2)}) collective-permute-start(f32[992,128]{1,0:T(8,128)} %get-tuple-element.30), channel_id=1, source_target_pairs={{1,0},{2,1},{3,2},{4,3},{5,4},{6,5},{7,6},{9,8},{10,9},{11,10},{12... | collective-permute-start | bytes 1523720 | tf_op jit(solution)/shard_map/ppermute | solution.py:618
  57.2 47.3 %collective-permute-start.8 = (f32[128,1024]{1,0:T(8,128)}, f32[128,1024]{1,0:T(8,128)S(1)}, u32[]{:S(2)}, u32[]{:S(2)}) collective-permute-start(f32[128,1024]{1,0:T(8,128)} %get-tuple-element.41), channel_id=1, source_target_pairs={{0,16},{8,24},{16,0},{24,8},{1,17},{9,25},{17,1},{25,9},{2,18},{10... | collective-permute-start | bytes 1572872 | tf_op jit(solution)/shard_map/ppermute | solution.py:645
  58.8 46.5 %collective-permute-start.9 = (f32[128,1024]{1,0:T(8,128)}, f32[128,1024]{1,0:T(8,128)}, u32[]{:S(2)}, u32[]{:S(2)}) collective-permute-start(f32[128,1024]{1,0:T(8,128)} %get-tuple-element.42), channel_id=1, source_target_pairs={{0,24},{8,16},{16,8},{24,0},{1,25},{9,17},{17,9},{25,1},{2,26},{10... | collective-permute-start | bytes 1572872 | tf_op jit(solution)/shard_map/ppermute | solution.py:645
  93.3 24.7 %collective-permute-start.4 = (f32[128,1024]{1,0:T(8,128)}, f32[128,1024]{1,0:T(8,128)S(1)}, u32[]{:S(2)}, u32[]{:S(2)}) collective-permute-start(f32[128,1024]{1,0:T(8,128)} %get-tuple-element.34), channel_id=1, source_target_pairs={{0,8},{8,0},{16,24},{24,16},{1,9},{9,1},{17,25},{25,17},{2,10},{10... | collective-permute-start | bytes 1572872 | tf_op jit(solution)/shard_map/ppermute | solution.py:645
  93.4 24.6 %collective-permute-start.5 = (f32[128,1024]{1,0:T(8,128)}, f32[128,1024]{1,0:T(8,128)S(1)}, u32[]{:S(2)}, u32[]{:S(2)}) collective-permute-start(f32[128,1024]{1,0:T(8,128)} %get-tuple-element.35), channel_id=1, source_target_pairs={{0,16},{8,24},{16,0},{24,8},{1,17},{9,25},{17,1},{25,9},{2,18},{10... | collective-permute-start | bytes 1572872 | tf_op jit(solution)/shard_map/ppermute | solution.py:645
  95.0 23.8 %collective-permute-start.6 = (f32[128,1024]{1,0:T(8,128)}, f32[128,1024]{1,0:T(8,128)}, u32[]{:S(2)}, u32[]{:S(2)}) collective-permute-start(f32[128,1024]{1,0:T(8,128)} %get-tuple-element.36), channel_id=1, source_target_pairs={{0,24},{8,16},{16,8},{24,0},{1,25},{9,17},{17,9},{25,1},{2,26},{10... | collective-permute-start | bytes 1572872 | tf_op jit(solution)/shard_map/ppermute | solution.py:645
  104.5 0.8 copy-start.1
  105.3 1.0 copy-start.2
  129.1 1.6 collective-permute-start.10
  131.8 6.2 %collective-permute-start.11 = (f32[288,128]{1,0:T(8,128)S(1)}, f32[288,128]{1,0:T(8,128)S(1)}, u32[]{:S(2)}, u32[]{:S(2)}) collective-permute-start(f32[288,128]{1,0:T(8,128)S(1)} %constant_dynamic-slice_fusion), channel_id=1, source_target_pairs={{0,16},{8,24},{16,0},{24,8},{1,17},{9,25},{17,1},{25,9},{2,18},{10... | collective-permute-start | bytes 442376 | tf_op jit(solution)/shard_map/ppermute | solution.py:577
  138.0 6.0 %collective-permute-start.12 = (f32[288,128]{1,0:T(8,128)S(1)}, f32[288,128]{1,0:T(8,128)S(1)}, u32[]{:S(2)}, u32[]{:S(2)}) collective-permute-start(f32[288,128]{1,0:T(8,128)S(1)} %dynamic-slice_add_fusion.1), channel_id=1, source_target_pairs={{0,1},{1,0},{2,3},{3,2},{4,5},{5,4},{6,7},{7,6},{8,9},{9,8},{10,11... | collective-permute-start | bytes 442376 | tf_op jit(solution)/shard_map/ppermute | solution.py:594
  144.0 6.8 %collective-permute-start.13 = (f32[288,128]{1,0:T(8,128)S(1)}, f32[288,128]{1,0:T(8,128)S(1)}, u32[]{:S(2)}, u32[]{:S(2)}) collective-permute-start(f32[288,128]{1,0:T(8,128)S(1)} %add.25), channel_id=1, source_target_pairs={{0,2},{1,3},{2,0},{3,1},{4,6},{5,7},{6,4},{7,5},{8,10},{9,11},{10,... | collective-permute-start | bytes 442376 | tf_op jit(solution)/shard_map/ppermute | solution.py:594
  150.8 7.8 %collective-permute-start.14 = (f32[288,128]{1,0:T(8,128)S(1)}, f32[288,128]{1,0:T(8,128)S(1)}, u32[]{:S(2)}, u32[]{:S(2)}) collective-permute-start(f32[288,128]{1,0:T(8,128)S(1)} %add.26), channel_id=1, source_target_pairs={{0,4},{1,5},{2,6},{3,7},{4,0},{5,1},{6,2},{7,3},{8,12},{9,13},{10,... | collective-permute-start | bytes 442376 | tf_op jit(solution)/shard_map/ppermute | solution.py:594
  158.6 5.2 %collective-permute-start.15 = (f32[288,128]{1,0:T(8,128)S(1)}, f32[288,128]{1,0:T(8,128)S(1)}, u32[]{:S(2)}, u32[]{:S(2)}) collective-permute-start(f32[288,128]{1,0:T(8,128)S(1)} %add.27), channel_id=1, source_target_pairs={{0,16},{8,24},{16,0},{24,8},{1,17},{9,25},{17,1},{25,9},{2,18},{10... | collective-permute-start | bytes 442376 | tf_op jit(solution)/shard_map/ppermute | solution.py:583
  163.9 9.1 %collective-permute-start.16 = (f32[576,128]{1,0:T(8,128)S(1)}, f32[576,128]{1,0:T(8,128)S(1)}, u32[]{:S(2)}, u32[]{:S(2)}) collective-permute-start(f32[576,128]{1,0:T(8,128)S(1)} %maximum_select_fusion.1), channel_id=1, source_target_pairs={{0,8},{8,0},{16,24},{24,16},{1,9},{9,1},{17,25},{25,17},{2,10},{10... | collective-permute-start | bytes 884744 | tf_op jit(solution)/shard_map/ppermute | solution.py:583
  168.4 4.6 %copy-start = (f32[69,2048]{1,0:T(8,128)S(1)}, f32[69,2048]{1,0:T(8,128)}, u32[]{:S(2)}) copy-start(f32[69,2048]{1,0:T(8,128)} %layer_ref.3) | copy-start | bytes 1695748

commit v5 on v4

--- a/solution.py
+++ b/solution.py
@@ -93,7 +93,7 @@
     )(start_field, ids)
 
 
-def diffuse_kernel(chunk, chunks, ends_ref, grp_ref, field_ref, ids_ref, runs_ref, *refs):
+def diffuse_kernel(chunk, chunks, n_tile, tile_ref, grp_ref, field_ref, ids_ref, runs_ref, *refs):
     edges, outs = refs[: 2 + 2 * (chunk > 0)], refs[2 + 2 * (chunk > 0) : -11]
     raw_ref, u0_ref, u1_ref, d_ref, a_ref, b_ref, fx_ref, v_ref, wide_ref, made_ref, sem = refs[-11:]
     rows, cols = ids_ref.shape
@@ -115,7 +115,12 @@
         for r in range(rows):
             wide_ref[STEPS + r, :, at] = ids_ref[r : r + 1, at].astype(F32)
 
-    level, pick, steep = runs_ref[0:LEVELS], runs_ref[LEVELS : LEVELS + 1], runs_ref[LEVELS + 1 : LEVELS + 2]
+    mine = pl.ds(pl.multiple_of(grp_ref[0] * LANES, LANES), LANES)
+    level, pick, steep = (
+        runs_ref[0:LEVELS, mine],
+        runs_ref[LEVELS : LEVELS + 1, mine],
+        runs_ref[LEVELS + 1 : LEVELS + 2, mine],
+    )
     table = 0.03 * jnp.exp(level * jnp.log(F32(1.35)))
     both = jnp.concatenate([table * (0.5 * steep), table * (0.5 * (1.0 - steep))], axis=1)
     pieces = []
@@ -127,7 +132,8 @@
     tables = jnp.concatenate(pieces, axis=0).astype(BF16)
     klass = (lax.broadcasted_iota(jnp.int32, (4 * LEVELS, LANES), 0) % LEVELS).astype(F32)
     pick8 = jnp.broadcast_to(pick, (SUB, LANES))
-    has_top, has_bottom = ends_ref[0], ends_ref[1]
+    has_top = jnp.where(tile_ref[0] > 0, F32(1.0), F32(0.0))
+    has_bottom = jnp.where(tile_ref[0] < n_tile - 1, F32(1.0), F32(0.0))
     zeros = jnp.zeros((SUB, LANES), F32)
 
     def inside(r):
@@ -227,7 +233,7 @@
         sent_out.wait()
 
 
-def diffuse(chunk, chunks, start_field, edges, ids, run_rows, ends, grp, blocks):
+def diffuse(chunk, chunks, start_field, edges, ids, run_rows, tile, n_tile, grp, blocks):
     runs, rows, cols = start_field.shape
     total = rows + 2 * STEPS
     low, high, _ = spans(cols, chunks)[chunk]
@@ -237,7 +243,7 @@
     edges = list(edges[chunk]) + (list(edges[chunk - 1]) if chunk else [])
     state = pltpu.VMEM((total, width + 2 * SUB, runs), F32)
     return pl.pallas_call(
-        functools.partial(diffuse_kernel, chunk, chunks),
+        functools.partial(diffuse_kernel, chunk, chunks, n_tile),
         in_specs=[SCALARS, SCALARS, ANY, SPACE, SPACE] + [SPACE] * len(edges),
         out_specs=[ANY] * blocks,
         out_shape=[jax.ShapeDtypeStruct((runs, rows * own // blocks), F32)] * blocks,
@@ -256,7 +262,7 @@
         ],
         cost_estimate=cost(100 * runs * total * width, 12 * runs * total * width),
         name="diffuse",
-    )(ends, grp, start_field, ids, run_rows, *edges)
+    )(tile, grp, start_field, ids, run_rows, *edges)
 
 
 PITCH = 80
@@ -363,20 +369,22 @@
     )
 
 
-def predict(hidden, weight, bias, block=512):
+def predict(chunk, chunks, cols, hidden, weight, bias):
     runs, hid = hidden.shape
-    cells = weight.shape[1]
+    own = cols // chunks
+    mine = weight.shape[1] // chunks
+    strip = lambda i: (0, i * chunks + chunk)
     return pl.pallas_call(
         predict_kernel,
-        grid=(cells // block,),
+        grid=(mine // own,),
         in_specs=[
             pl.BlockSpec((runs, hid), lambda i: (0, 0)),
-            pl.BlockSpec((hid, block), lambda i: (0, i)),
-            pl.BlockSpec((1, block), lambda i: (0, i)),
-        ],
-        out_specs=pl.BlockSpec((runs, block), lambda i: (0, i)),
-        out_shape=jax.ShapeDtypeStruct((runs, cells), F32),
-        cost_estimate=cost(2 * runs * hid * cells, 2 * hid * cells + 4 * runs * cells),
+            pl.BlockSpec((hid, own), strip),
+            pl.BlockSpec((1, own), strip),
+        ],
+        out_specs=pl.BlockSpec((runs, own), lambda i: (0, i)),
+        out_shape=jax.ShapeDtypeStruct((runs, mine), F32),
+        cost_estimate=cost(2 * runs * hid * mine, 2 * hid * mine + 4 * runs * mine),
         name="predict",
     )(hidden, weight, bias)
 
@@ -391,6 +399,8 @@
     if has_before:
         acc_in_any, refs = refs[2], refs[3 + (not last) :]
     misfit_ref, bias_out_ref, acc_ref, extra_ref = refs[:4]
+    if last:
+        sent_ref, refs = refs[4], refs[1:]
     back_ref, gain_ref, sem, acc_in_ref = refs[4:8]
     slope_ref = extra_ref if last else refs[8]
     step, steps = pl.program_id(0), pl.num_programs(0)
@@ -447,8 +457,16 @@
                 acc = acc + acc_in_ref[at, :]
             if last:
                 for t in range(0, BLOCK, LANES):
-                    turned = jnp.transpose(acc[t : t + LANES, :])
-                    acc_ref[(h + t) // LANES] = turned[: acc_ref.shape[1], :]
+                    turned = jnp.transpose(acc[t : t + LANES, :])[: acc_ref.shape[1], :]
+                    half, place = divmod((h + t) // LANES, acc_ref.shape[0])
+
+                    @pl.when((grp_ref[0] & 1) == half)
+                    def _(turned=turned, place=place):
+                        acc_ref[place] = turned
+
+                    @pl.when((grp_ref[0] & 1) != half)
+                    def _(turned=turned, place=place):
+                        sent_ref[place] = turned
             else:
                 acc_ref[at, :] = acc
 
@@ -461,7 +479,7 @@
     own = cols // chunks
     last, has_before = chunk == chunks - 1, before is not None
     strip = lambda i: (0, i * chunks + chunk)
-    in_specs = [SCALARS, pl.BlockSpec((runs, own), strip)]
+    in_specs = [SCALARS, pl.BlockSpec((runs, own), lambda i: (0, i))]
     in_specs += [pl.BlockSpec((per_source, own), lambda i: (0, i))] + [SPACE] * (sources - 1)
     in_specs += [pl.BlockSpec((hid, own), strip), pl.BlockSpec((1, own), strip), ANY, SPACE]
     args = [grp, guess, *targets, weight, bias, gain_t, feats]
@@ -477,7 +495,9 @@
             aliases[len(args)] = 3
             in_specs.append(ANY)
             args.append(before[3])
-    acc_shape = (hid // LANES, kept, LANES) if last else (hid, LANES)
+    acc_shape = (hid // LANES // 2, kept, LANES) if last else (hid, LANES)
+    acc_spec = pl.BlockSpec(acc_shape, lambda i: (0,) * len(acc_shape))
+    more = 1 if last else 0
     extra = (runs, own, runs) if last else (hid, own, hid)
     scratch = [
         pltpu.VMEM((hid, runs), F32),
@@ -495,15 +515,17 @@
         out_specs=[
             pl.BlockSpec((runs, own), strip),
             pl.BlockSpec((1, own), strip),
-            pl.BlockSpec(acc_shape, lambda i: (0,) * len(acc_shape)),
+            acc_spec,
             pl.BlockSpec((extra[0], own), (lambda i: (0, i)) if last else strip),
-        ],
+        ]
+        + [acc_spec] * more,
         out_shape=[
             jax.ShapeDtypeStruct((runs, cells), BF16),
             jax.ShapeDtypeStruct((1, cells), F32),
             jax.ShapeDtypeStruct(acc_shape, F32),
             jax.ShapeDtypeStruct((runs, mine) if last else (hid, cells), BF16),
-        ],
+        ]
+        + [jax.ShapeDtypeStruct(acc_shape, F32)] * more,
         scratch_shapes=scratch,
         input_output_aliases=aliases,
         cost_estimate=cost(
@@ -586,9 +608,10 @@
     )
 
 
-def sum_over_devices(x):
+def sum_over_devices(x, sent):
     grp, tile = lax.axis_size("grp"), lax.axis_size("tile")
-    for bit in bits_of(grp):
+    x = x + lax.ppermute(sent, "grp", [(i, i ^ 1) for i in range(grp)])
+    for bit in bits_of(grp)[1:]:
         x = halve(x, "grp", bit)
     for bit in bits_of(tile):
         x = x + lax.ppermute(x, "tile", [(i, i ^ bit) for i in range(tile)])
@@ -600,14 +623,14 @@
 def on_device(
     start_field, class_ids, run_levels, steepness, step_pick, input_layer, output_layer, output_bias
 ):
-    local_runs, rows, cols = start_field.shape
+    _, rows, cols = start_field.shape
     n_grp, n_tile = lax.axis_size("grp"), lax.axis_size("tile")
-    tile = lax.axis_index("tile")
-    first_run = lax.axis_index("grp") * local_runs
+    tile = lax.axis_index("tile").astype(jnp.int32)[None]
+    grp = lax.axis_index("grp").astype(jnp.int32)[None]
     chunks = CHUNKS
     parts = spans(cols, chunks)
     runs_total, classes = run_levels.shape
-    n_feat, _ = input_layer.shape
+    n_feat, hid = input_layer.shape
 
     up = [(i, i + 1) for i in range(n_tile - 1)]
     down = [(j, i) for i, j in up]
@@ -627,35 +650,35 @@
         ],
         axis=0,
     )
-    run_rows_here = lax.dynamic_slice_in_dim(run_rows, first_run, local_runs, 1)
-    ends = jnp.stack([(tile > 0).astype(F32), (tile < n_tile - 1).astype(F32)])
     hidden, hidden_t, gain_t, project = hidden_units(run_rows, input_layer)
     bias_row = output_bias[None, :]
-    guess = predict(hidden, output_layer, bias_row)
+    guesses = []
+    for c in range(chunks):
+        guesses.append(predict(c, chunks, cols, hidden, output_layer, bias_row))
     kept = -(-(n_feat + 1) // SUB) * SUB
 
     state = None
     scale = 2.0 / runs_total
-    grp = lax.axis_index("grp").astype(jnp.int32)[None]
     for c in range(chunks):
-        snaps = diffuse(c, chunks, start_field, edges, class_ids, run_rows_here, ends, grp, n_grp)
+        snaps = diffuse(c, chunks, start_field, edges, class_ids, run_rows, tile, n_tile, grp, n_grp)
         targets = [snaps[0]]
         for offset in range(1, n_grp):
             pairs = [(i, i ^ offset) for i in range(n_grp)]
             targets.append(in_vmem(lax.ppermute(snaps[offset], "grp", pairs)))
         before = state
         state = learn(
-            c, chunks, cols, grp, guess, targets, output_layer, bias_row,
+            c, chunks, cols, grp, guesses[c], targets, output_layer, bias_row,
             gain_t, project, hidden_t, before, kept, scale,
         )
-    misfit, bias_next, partial, slope = state
+    misfit, bias_next, partial, slope, sent = state
     output_next, strips = before[3], rows // n_grp
     for part in range(UPDATES):
         first, past = part * strips // UPDATES, (part + 1) * strips // UPDATES
         output_next = update(
             first, past - first, chunks, cols, hidden_t, slope, output_layer, output_next
         )
-    total = sum_over_devices(partial.reshape(-1, LANES)).reshape(partial.shape)
+    total = sum_over_devices(partial.reshape(-1, LANES), sent.reshape(-1, LANES))
+    total = total.reshape(hid // LANES, kept, LANES)
     input_next = finish(in_vmem(total), in_vmem(input_layer))
     return misfit, output_next, bias_next.reshape(-1), input_next
 

time: 175 us -> 176 us (level)
  Pallas kernels: 83.5 us -> 89.1 us
  waiting for transfers between devices: 55.8 us -> 52.8 us
    ppermute x2, waiting for transfers between devices: 34.3 us -> 28.3 us  [on_device(): above = lax.ppermute(bottom, 'tile', up)]
    pallas_call x3 -> x4, Pallas kernels: 39.1 us -> 42.8 us  [the longest x2 29.8 us: diffuse(): pl.pallas_call(functools.partial(diffuse_kernel, chunk, chunks, n_tile),...]
    ppermute x6, waiting for transfers between devices: 0.73 us -> 3.42 us  [on_device(): targets.append(in_vmem(lax.ppermute(snaps[offset], 'grp', pairs)))]
    pallas_call x2, Pallas kernels: 21 us -> 23 us  [learn(): pl.pallas_call(functools.partial(learn_kernel, last, has_before, scale, s...]
    ppermute x2 -> x1, waiting for transfers between devices: 5.85 us -> 4.63 us  [halve(): return kept + lax.ppermute(sent, axis, [(i, i ^ bit) for i in range(size)])]
  transfers between devices with their start and end apart: 17 -> 17, of which waited for: 9 -> 9; matrix products, arithmetic and copies ran while one was open for 1% -> 0% of each run, Pallas kernels for 31% -> 33%
where the time goes in v5:
time: 176 us; the launch traced here: 175 us
  Pallas kernels  89.1 us (51%)
  waiting for transfers between devices  52.8 us (30%)
  starting transfers between devices  28.4 us (16%)
  local copies, waits for them, and re-layouts  1.95 us (1%)
  other arithmetic  1.81 us (1%)
    pallas_call x2, Pallas kernels, diffuse(): pl.pallas_call(functools.partial(diffuse_kernel, chunk, chunks, n_tile),...  29.8 us
    ppermute x2, waiting for transfers between devices, on_device(): above = lax.ppermute(bottom, 'tile', up)  28.3 us
    pallas_call x2, Pallas kernels, learn(): pl.pallas_call(functools.partial(learn_kernel, last, has_before, scale, s...  23 us
    pallas_call x2, Pallas kernels, predict(): pl.pallas_call(predict_kernel, grid=(mine // own,), in_specs=[pl.BlockSpe...  13 us
    ppermute x3, waiting for transfers between devices, sum_over_devices(): x = x + lax.ppermute(x, 'tile', [(i, i ^ bit) for i in range(tile)])  11.3 us
    ppermute x2, starting transfers between devices, on_device(): above = lax.ppermute(bottom, 'tile', up)  9.22 us
    ppermute x3, starting transfers between devices, sum_over_devices(): x = x + lax.ppermute(x, 'tile', [(i, i ^ bit) for i in range(tile)])  9.2 us
    pallas_call x2, Pallas kernels, update(): pl.pallas_call(update_kernel, grid=(count,), in_specs=[pl.BlockSpec((hid,...  9.02 us
  transfers between devices with their start and end apart: 17, of which 9 were waited for; matrix products, arithmetic and copies ran while one was open for 0% of the time, Pallas kernels for 33%

profile of v5, /device:TPU:0, one launch (start us, length us, event | category | flops | bytes accessed | tf_op | source)
XLA Modules:
  0.0 174.9 jit_solution(12503195123340096336)
XLA Ops:
  0.7 4.1 %pack_edges.3 = (f32[1072,128]{1,0:T(8,128)}, f32[1072,128]{1,0:T(8,128)}) custom-call(f32[128,16,512]{2,1,0:T(8,128)} %field_ref.7, s32[16,512]{1,0:T(8,128)} %ids_ref.7), custom_call_target="tpu_custom_call" | custom-call | bytes 3244032 | tf_op jit(solution)/shard_map/pack_edges/pallas_call | solution.py:82
  4.8 4.9 %collective-permute-start.2 = (f32[1072,128]{1,0:T(8,128)}, f32[1072,128]{1,0:T(8,128)S(1)}, u32[]{:S(2)}, u32[]{:S(2)}) collective-permute-start(f32[1072,128]{1,0:T(8,128)} %get-tuple-element.32), channel_id=1, source_target_pairs={{0,1},{1,2},{2,3},{3,4},{4,5},{5,6},{6,7},{8,9},{9,10},{10,11},{11... | collective-permute-start | bytes 1646600 | tf_op jit(solution)/shard_map/ppermute | solution.py:640
  9.7 1.3 collective-permute-start.3
  11.8 21.6 %collective-permute-done.2.refs_2_.refs_0_ = f32[1072,128]{1,0:T(8,128)S(1)} collective-permute-done((f32[1072,128]{1,0:T(8,128)}, f32[1072,128]{1,0:T(8,128)S(1)}, u32[]{:S(2)}, u32[]{:S(2)}) %collective-permute-start.2) | collective-permute-done | bytes 548896 | tf_op jit(solution)/shard_map/ppermute | solution.py:640
  33.5 14.9 %diffuse.3 = (f32[128,1024]{1,0:T(8,128)}, f32[128,1024]{1,0:T(8,128)}, f32[128,1024]{1,0:T(8,128)}, f32[128,1024]{1,0:T(8,128)}) custom-call(s32[1]{0:T(128)} %bitcast.5.tile_ref, s32[1]{0:T(128)} %bitcast.grp_ref.refs_0_, f32[128,16,512]{2,1,0:T(8,128)} %field_ref.7, s32[16,512]{1,0:T(8,128)} %ids_ref.7, f32[16,512]{1,0:T(8,128)} %maximum_maximum_fusion.runs_ref, ...), custom_call_target="tpu_custom_call" | custom-call | flops 81100800 | bytes 9732096 | tf_op jit(solution)/shard_map/diffuse/pallas_call | solution.py:245
  48.4 2.9 %pack_edges.2 = (f32[992,128]{1,0:T(8,128)}, f32[992,128]{1,0:T(8,128)}) custom-call(f32[128,16,512]{2,1,0:T(8,128)} %field_ref.7, s32[16,512]{1,0:T(8,128)} %ids_ref.7), custom_call_target="tpu_custom_call" | custom-call | bytes 3047424 | tf_op jit(solution)/shard_map/pack_edges/pallas_call | solution.py:82
  51.4 4.3 %collective-permute-start = (f32[992,128]{1,0:T(8,128)}, f32[992,128]{1,0:T(8,128)S(1)}, u32[]{:S(2)}, u32[]{:S(2)}) collective-permute-start(f32[992,128]{1,0:T(8,128)} %get-tuple-element.30), channel_id=1, source_target_pairs={{0,1},{1,2},{2,3},{3,4},{4,5},{5,6},{6,7},{8,9},{9,10},{10,11},{11... | collective-permute-start | bytes 1523720 | tf_op jit(solution)/shard_map/ppermute | solution.py:640
  55.7 1.5 collective-permute-start.1
  57.2 1.6 collective-permute-start.8
  58.8 6.3 %hidden_units.1 = (bf16[512,2048]{1,0:T(8,128)(2,1)}, bf16[2048,512]{1,0:T(8,128)(2,1)}, f32[2048,512]{1,0:T(8,128)}, bf16[512,128]{1,0:T(8,128)(2,1)}) custom-call(f32[16,512]{1,0:T(8,128)} %maximum_maximum_fusion.runs_ref, f32[69,2048]{1,0:T(8,128)} %layer_ref.3), custom_call_target="tpu_custom_call" | custom-call | flops 1073741824 | bytes 10485760 | tf_op jit(solution)/shard_map/hidden_units/pallas_call | solution.py:336
  65.1 6.5 %predict.3.refs_1_ = f32[512,1024]{1,0:T(8,128)} custom-call(bf16[512,2048]{1,0:T(8,128)(2,1)} %get-tuple-element.29.hidden_ref, bf16[2048,2048]{1,0:T(8,128)(2,1)} %weight_ref.7, f32[1,2048]{1,0:T(1,128)} %bitcast.13), custom_call_target="tpu_custom_call" | custom-call | flops 2147483648 | bytes 6291456 | tf_op jit(solution)/shard_map/predict/pallas_call | solution.py:377
  71.6 6.7 %collective-permute-done.refs_0_ = f32[992,128]{1,0:T(8,128)S(1)} collective-permute-done((f32[992,128]{1,0:T(8,128)}, f32[992,128]{1,0:T(8,128)S(1)}, u32[]{:S(2)}, u32[]{:S(2)}) %collective-permute-start) | collective-permute-done | bytes 507936 | tf_op jit(solution)/shard_map/ppermute | solution.py:640
  78.3 14.9 %diffuse.2 = (f32[128,1024]{1,0:T(8,128)}, f32[128,1024]{1,0:T(8,128)}, f32[128,1024]{1,0:T(8,128)}, f32[128,1024]{1,0:T(8,128)}) custom-call(s32[1]{0:T(128)} %bitcast.5.tile_ref, s32[1]{0:T(128)} %bitcast.grp_ref.refs_0_, f32[128,16,512]{2,1,0:T(8,128)} %field_ref.7, s32[16,512]{1,0:T(8,128)} %ids_ref.7, f32[16,512]{1,0:T(8,128)} %maximum_maximum_fusion.runs_ref, ...), custom_call_target="tpu_custom_call" | custom-call | flops 81100800 | bytes 9732096 | tf_op jit(solution)/shard_map/diffuse/pallas_call | solution.py:245
  93.3 1.6 collective-permute-start.5
  95.1 6.5 %predict.2.refs_1_ = f32[512,1024]{1,0:T(8,128)} custom-call(bf16[512,2048]{1,0:T(8,128)(2,1)} %get-tuple-element.29.hidden_ref, bf16[2048,2048]{1,0:T(8,128)(2,1)} %weight_ref.7, f32[1,2048]{1,0:T(1,128)} %bitcast.14), custom_call_target="tpu_custom_call" | custom-call | flops 2147483648 | bytes 6291456 | tf_op jit(solution)/shard_map/predict/pallas_call | solution.py:377
  102.4 1.0 copy-done.2
  103.4 11.7 %learn.2 = (bf16[512,2048]{1,0:T(8,128)(2,1)}, f32[1,2048]{1,0:T(1,128)}, f32[2048,128]{1,0:T(8,128)}, bf16[2048,2048]{1,0:T(8,128)(2,1)}) custom-call(s32[1]{0:T(128)} %bitcast.grp_ref.refs_0_, f32[512,1024]{1,0:T(8,128)} %predict.3.refs_1_, f32[128,1024]{1,0:T(8,128)} %get-tuple-element.40.refs_2_, f32[128,1024]{1,0:T(8,128)S(1)} %collective-permute-done.7.refs_3_, ...), custom_call_target="tpu_custom_call" | custom-call | flops 4831838208 | bytes 14680064 | tf_op jit(solution)/shard_map/learn/pallas_call | solution.py:511
  115.2 3.4 %collective-permute-done.6.refs_5_ = f32[128,1024]{1,0:T(8,128)} collective-permute-done((f32[128,1024]{1,0:T(8,128)}, f32[128,1024]{1,0:T(8,128)}, u32[]{:S(2)}, u32[]{:S(2)}) %collective-permute-start.6) | collective-permute-done | bytes 524320 | tf_op jit(solution)/shard_map/ppermute | solution.py:667
  118.6 11.3 %learn.3 = (bf16[512,2048]{1,0:T(8,128)(2,1)}, f32[1,2048]{1,0:T(1,128)}, f32[8,72,128]{2,1,0:T(8,128)}, bf16[512,1024]{1,0:T(8,128)(2,1)}, f32[8,72,128]{2,1,0:T(8,128)}) custom-call(s32[1]{0:T(128)} %bitcast.grp_ref.refs_0_, f32[512,1024]{1,0:T(8,128)} %predict.2.refs_1_, ...), custom_call_target="tpu_custom_call", output_to_operand_aliasing={{0}: (10, {}), {1}: (11, {})} | custom-call | flops 2684354560 | bytes 10485760 | tf_op jit(solution)/shard_map/learn/pallas_call | solution.py:511
  130.4 1.4 collective-permute-done.10
  132.8 1.6 collective-permute-start.11
  134.4 4.6 %collective-permute-done.11 = f32[288,128]{1,0:T(8,128)S(1)} collective-permute-done((f32[288,128]{1,0:T(8,128)S(1)}, f32[288,128]{1,0:T(8,128)S(1)}, u32[]{:S(2)}, u32[]{:S(2)}) %collective-permute-start.11) | collective-permute-done | bytes 147488 | tf_op jit(solution)/shard_map/ppermute | solution.py:599
  139.0 2.4 %collective-permute-start.12 = (f32[288,128]{1,0:T(8,128)S(1)}, f32[288,128]{1,0:T(8,128)S(1)}, u32[]{:S(2)}, u32[]{:S(2)}) collective-permute-start(f32[288,128]{1,0:T(8,128)S(1)} %dynamic-slice_add_fusion), channel_id=1, source_target_pairs={{0,1},{1,0},{2,3},{3,2},{4,5},{5,4},{6,7},{7,6},{8,9},{9,8},{10,11... | collective-permute-start | bytes 442376 | tf_op jit(solution)/shard_map/ppermute | solution.py:617
  141.5 3.5 %collective-permute-done.12 = f32[288,128]{1,0:T(8,128)S(1)} collective-permute-done((f32[288,128]{1,0:T(8,128)S(1)}, f32[288,128]{1,0:T(8,128)S(1)}, u32[]{:S(2)}, u32[]{:S(2)}) %collective-permute-start.12) | collective-permute-done | bytes 147488 | tf_op jit(solution)/shard_map/ppermute | solution.py:617
  145.0 3.7 %collective-permute-start.13 = (f32[288,128]{1,0:T(8,128)S(1)}, f32[288,128]{1,0:T(8,128)S(1)}, u32[]{:S(2)}, u32[]{:S(2)}) collective-permute-start(f32[288,128]{1,0:T(8,128)S(1)} %add.19), channel_id=1, source_target_pairs={{0,2},{1,3},{2,0},{3,1},{4,6},{5,7},{6,4},{7,5},{8,10},{9,11},{10,... | collective-permute-start | bytes 442376 | tf_op jit(solution)/shard_map/ppermute | solution.py:617
  148.7 3.1 %collective-permute-done.13 = f32[288,128]{1,0:T(8,128)S(1)} collective-permute-done((f32[288,128]{1,0:T(8,128)S(1)}, f32[288,128]{1,0:T(8,128)S(1)}, u32[]{:S(2)}, u32[]{:S(2)}) %collective-permute-start.13) | collective-permute-done | bytes 147488 | tf_op jit(solution)/shard_map/ppermute | solution.py:617
  151.8 3.1 %collective-permute-start.14 = (f32[288,128]{1,0:T(8,128)S(1)}, f32[288,128]{1,0:T(8,128)S(1)}, u32[]{:S(2)}, u32[]{:S(2)}) collective-permute-start(f32[288,128]{1,0:T(8,128)S(1)} %add.20), channel_id=1, source_target_pairs={{0,4},{1,5},{2,6},{3,7},{4,0},{5,1},{6,2},{7,3},{8,12},{9,13},{10,... | collective-permute-start | bytes 442376 | tf_op jit(solution)/shard_map/ppermute | solution.py:617
  154.9 4.7 %collective-permute-done.14 = f32[288,128]{1,0:T(8,128)S(1)} collective-permute-done((f32[288,128]{1,0:T(8,128)S(1)}, f32[288,128]{1,0:T(8,128)S(1)}, u32[]{:S(2)}, u32[]{:S(2)}) %collective-permute-start.14) | collective-permute-done | bytes 147488 | tf_op jit(solution)/shard_map/ppermute | solution.py:617
  159.6 1.6 collective-permute-start.15
  161.2 3.7 %collective-permute-done.15 = f32[288,128]{1,0:T(8,128)S(1)} collective-permute-done((f32[288,128]{1,0:T(8,128)S(1)}, f32[288,128]{1,0:T(8,128)S(1)}, u32[]{:S(2)}, u32[]{:S(2)}) %collective-permute-start.15) | collective-permute-done | bytes 147488 | tf_op jit(solution)/shard_map/ppermute | solution.py:605
  164.9 4.5 %update.2._ = bf16[2048,2048]{1,0:T(8,128)(2,1)} custom-call(bf16[2048,512]{1,0:T(8,128)(2,1)} %get-tuple-element.44.refs_10_.hidden_t_ref, bf16[512,1024]{1,0:T(8,128)(2,1)} %get-tuple-element.49.slope_ref, bf16[2048,2048]{1,0:T(8,128)(2,1)} %weight_ref.7, bf16[2048,2048]{1,0:T(8,128)(2,1)} %get-tuple-element.50._), custom_call_target="tpu_custom_call", output_to_operand_aliasing={{}: (3, {})} | custom-call | flops 1073741824 | bytes 5242880 | tf_op jit(solution)/shard_map/update/pallas_call | solution.py:551
  169.4 4.5 %update.3 = bf16[2048,2048]{1,0:T(8,128)(2,1)} custom-call(bf16[2048,512]{1,0:T(8,128)(2,1)} %get-tuple-element.44.refs_10_.hidden_t_ref, bf16[512,1024]{1,0:T(8,128)(2,1)} %get-tuple-element.49.slope_ref, bf16[2048,2048]{1,0:T(8,128)(2,1)} %weight_ref.7, bf16[2048,2048]{1,0:T(8,128)(2,1)} %update.2._), custom_call_target="tpu_custom_call", output_to_operand_aliasing={{}: (3, {})} | custom-call | flops 1073741824 | bytes 5242880 | tf_op jit(solution)/shard_map/update/pallas_call | solution.py:551
  (39 shorter events, 4.6 us)
Async XLA Ops:
  0.6 10.4 %copy-start.4 = (s32[512]{0:T(512)S(1)}, s32[512]{0:T(512)}, u32[]{:S(2)}) copy-start(s32[512]{0:T(512)} %param.12) | copy-start | bytes 6148
  0.6 10.5 %copy-start.3 = (s32[512,8]{0,1:T(8,128)S(1)}, s32[512,8]{0,1:T(8,128)}, u32[]{:S(2)}) copy-start(s32[512,8]{0,1:T(8,128)} %param.10) | copy-start | bytes 49156
  0.7 10.5 %copy-start.5 = (f32[512]{0:T(512)S(1)}, f32[512]{0:T(512)}, u32[]{:S(2)}) copy-start(f32[512]{0:T(512)} %param.11) | copy-start | bytes 6148
  4.8 28.7 %collective-permute-start.2 = (f32[1072,128]{1,0:T(8,128)}, f32[1072,128]{1,0:T(8,128)S(1)}, u32[]{:S(2)}, u32[]{:S(2)}) collective-permute-start(f32[1072,128]{1,0:T(8,128)} %get-tuple-element.32), channel_id=1, source_target_pairs={{0,1},{1,2},{2,3},{3,4},{4,5},{5,6},{6,7},{8,9},{9,10},{10,11},{11... | collective-permute-start | bytes 1646600 | tf_op jit(solution)/shard_map/ppermute | solution.py:640
  9.7 23.7 %collective-permute-start.3 = (f32[1072,128]{1,0:T(8,128)}, f32[1072,128]{1,0:T(8,128)S(1)}, u32[]{:S(2)}, u32[]{:S(2)}) collective-permute-start(f32[1072,128]{1,0:T(8,128)} %get-tuple-element.33), channel_id=1, source_target_pairs={{1,0},{2,1},{3,2},{4,3},{5,4},{6,5},{7,6},{9,8},{10,9},{11,10},{12... | collective-permute-start | bytes 1646600 | tf_op jit(solution)/shard_map/ppermute | solution.py:641
  48.4 46.5 %collective-permute-start.7 = (f32[128,1024]{1,0:T(8,128)}, f32[128,1024]{1,0:T(8,128)S(1)}, u32[]{:S(2)}, u32[]{:S(2)}) collective-permute-start(f32[128,1024]{1,0:T(8,128)} %get-tuple-element.41), channel_id=1, source_target_pairs={{0,8},{8,0},{16,24},{24,16},{1,9},{9,1},{17,25},{25,17},{2,10},{10... | collective-permute-start | bytes 1572872 | tf_op jit(solution)/shard_map/ppermute | solution.py:667
  51.4 26.9 %collective-permute-start = (f32[992,128]{1,0:T(8,128)}, f32[992,128]{1,0:T(8,128)S(1)}, u32[]{:S(2)}, u32[]{:S(2)}) collective-permute-start(f32[992,128]{1,0:T(8,128)} %get-tuple-element.30), channel_id=1, source_target_pairs={{0,1},{1,2},{2,3},{3,4},{4,5},{5,6},{6,7},{8,9},{9,10},{10,11},{11... | collective-permute-start | bytes 1523720 | tf_op jit(solution)/shard_map/ppermute | solution.py:640
  55.7 22.6 %collective-permute-start.1 = (f32[992,128]{1,0:T(8,128)}, f32[992,128]{1,0:T(8,128)S(1)}, u32[]{:S(2)}, u32[]{:S(2)}) collective-permute-start(f32[992,128]{1,0:T(8,128)} %get-tuple-element.31), channel_id=1, source_target_pairs={{1,0},{2,1},{3,2},{4,3},{5,4},{6,5},{7,6},{9,8},{10,9},{11,10},{12... | collective-permute-start | bytes 1523720 | tf_op jit(solution)/shard_map/ppermute | solution.py:641
  57.2 44.4 %collective-permute-start.8 = (f32[128,1024]{1,0:T(8,128)}, f32[128,1024]{1,0:T(8,128)S(1)}, u32[]{:S(2)}, u32[]{:S(2)}) collective-permute-start(f32[128,1024]{1,0:T(8,128)} %get-tuple-element.42), channel_id=1, source_target_pairs={{0,16},{8,24},{16,0},{24,8},{1,17},{9,25},{17,1},{25,9},{2,18},{10... | collective-permute-start | bytes 1572872 | tf_op jit(solution)/shard_map/ppermute | solution.py:667
  58.7 43.7 %collective-permute-start.9 = (f32[128,1024]{1,0:T(8,128)}, f32[128,1024]{1,0:T(8,128)}, u32[]{:S(2)}, u32[]{:S(2)}) collective-permute-start(f32[128,1024]{1,0:T(8,128)} %get-tuple-element.43), channel_id=1, source_target_pairs={{0,24},{8,16},{16,8},{24,0},{1,25},{9,17},{17,9},{25,1},{2,26},{10... | collective-permute-start | bytes 1572872 | tf_op jit(solution)/shard_map/ppermute | solution.py:667
  93.2 22.0 %collective-permute-start.4 = (f32[128,1024]{1,0:T(8,128)}, f32[128,1024]{1,0:T(8,128)S(1)}, u32[]{:S(2)}, u32[]{:S(2)}) collective-permute-start(f32[128,1024]{1,0:T(8,128)} %get-tuple-element.35), channel_id=1, source_target_pairs={{0,8},{8,0},{16,24},{24,16},{1,9},{9,1},{17,25},{25,17},{2,10},{10... | collective-permute-start | bytes 1572872 | tf_op jit(solution)/shard_map/ppermute | solution.py:667
  93.3 21.9 %collective-permute-start.5 = (f32[128,1024]{1,0:T(8,128)}, f32[128,1024]{1,0:T(8,128)S(1)}, u32[]{:S(2)}, u32[]{:S(2)}) collective-permute-start(f32[128,1024]{1,0:T(8,128)} %get-tuple-element.36), channel_id=1, source_target_pairs={{0,16},{8,24},{16,0},{24,8},{1,17},{9,25},{17,1},{25,9},{2,18},{10... | collective-permute-start | bytes 1572872 | tf_op jit(solution)/shard_map/ppermute | solution.py:667
  94.8 23.8 %collective-permute-start.6 = (f32[128,1024]{1,0:T(8,128)}, f32[128,1024]{1,0:T(8,128)}, u32[]{:S(2)}, u32[]{:S(2)}) collective-permute-start(f32[128,1024]{1,0:T(8,128)} %get-tuple-element.37), channel_id=1, source_target_pairs={{0,24},{8,16},{16,8},{24,0},{1,25},{9,17},{17,9},{25,1},{2,26},{10... | collective-permute-start | bytes 1572872 | tf_op jit(solution)/shard_map/ppermute | solution.py:667
  101.6 0.8 copy-start.1
  102.4 1.0 copy-start.2
  129.9 1.9 %collective-permute-start.10 = (f32[576,128]{1,0:T(8,128)}, f32[576,128]{1,0:T(8,128)S(1)}, u32[]{:S(2)}, u32[]{:S(2)}) collective-permute-start(f32[576,128]{1,0:T(8,128)} %bitcast.20), channel_id=1, source_target_pairs={{0,8},{8,0},{16,24},{24,16},{1,9},{9,1},{17,25},{25,17},{2,10},{10... | collective-permute-start | bytes 884744 | tf_op jit(solution)/shard_map/ppermute | solution.py:613
  132.8 6.2 %collective-permute-start.11 = (f32[288,128]{1,0:T(8,128)S(1)}, f32[288,128]{1,0:T(8,128)S(1)}, u32[]{:S(2)}, u32[]{:S(2)}) collective-permute-start(f32[288,128]{1,0:T(8,128)S(1)} %constant_dynamic-slice_fusion), channel_id=1, source_target_pairs={{0,16},{8,24},{16,0},{24,8},{1,17},{9,25},{17,1},{25,9},{2,18},{10... | collective-permute-start | bytes 442376 | tf_op jit(solution)/shard_map/ppermute | solution.py:599
  139.0 6.0 %collective-permute-start.12 = (f32[288,128]{1,0:T(8,128)S(1)}, f32[288,128]{1,0:T(8,128)S(1)}, u32[]{:S(2)}, u32[]{:S(2)}) collective-permute-start(f32[288,128]{1,0:T(8,128)S(1)} %dynamic-slice_add_fusion), channel_id=1, source_target_pairs={{0,1},{1,0},{2,3},{3,2},{4,5},{5,4},{6,7},{7,6},{8,9},{9,8},{10,11... | collective-permute-start | bytes 442376 | tf_op jit(solution)/shard_map/ppermute | solution.py:617
  145.0 6.8 %collective-permute-start.13 = (f32[288,128]{1,0:T(8,128)S(1)}, f32[288,128]{1,0:T(8,128)S(1)}, u32[]{:S(2)}, u32[]{:S(2)}) collective-permute-start(f32[288,128]{1,0:T(8,128)S(1)} %add.19), channel_id=1, source_target_pairs={{0,2},{1,3},{2,0},{3,1},{4,6},{5,7},{6,4},{7,5},{8,10},{9,11},{10,... | collective-permute-start | bytes 442376 | tf_op jit(solution)/shard_map/ppermute | solution.py:617
  151.8 7.8 %collective-permute-start.14 = (f32[288,128]{1,0:T(8,128)S(1)}, f32[288,128]{1,0:T(8,128)S(1)}, u32[]{:S(2)}, u32[]{:S(2)}) collective-permute-start(f32[288,128]{1,0:T(8,128)S(1)} %add.20), channel_id=1, source_target_pairs={{0,4},{1,5},{2,6},{3,7},{4,0},{5,1},{6,2},{7,3},{8,12},{9,13},{10,... | collective-permute-start | bytes 442376 | tf_op jit(solution)/shard_map/ppermute | solution.py:617
  159.6 5.2 %collective-permute-start.15 = (f32[288,128]{1,0:T(8,128)S(1)}, f32[288,128]{1,0:T(8,128)S(1)}, u32[]{:S(2)}, u32[]{:S(2)}) collective-permute-start(f32[288,128]{1,0:T(8,128)S(1)} %add.21), channel_id=1, source_target_pairs={{0,16},{8,24},{16,0},{24,8},{1,17},{9,25},{17,1},{25,9},{2,18},{10... | collective-permute-start | bytes 442376 | tf_op jit(solution)/shard_map/ppermute | solution.py:605
  164.9 9.1 %collective-permute-start.16 = (f32[576,128]{1,0:T(8,128)S(1)}, f32[576,128]{1,0:T(8,128)S(1)}, u32[]{:S(2)}, u32[]{:S(2)}) collective-permute-start(f32[576,128]{1,0:T(8,128)S(1)} %maximum_select_fusion.1), channel_id=1, source_target_pairs={{0,8},{8,0},{16,24},{24,16},{1,9},{9,1},{17,25},{25,17},{2,10},{10... | collective-permute-start | bytes 884744 | tf_op jit(solution)/shard_map/ppermute | solution.py:605
  169.4 4.6 %copy-start = (f32[69,2048]{1,0:T(8,128)S(1)}, f32[69,2048]{1,0:T(8,128)}, u32[]{:S(2)}) copy-start(f32[69,2048]{1,0:T(8,128)} %layer_ref.3) | copy-start | bytes 1695748

commit v6 on v4

--- a/solution.py
+++ b/solution.py
@@ -93,7 +93,7 @@
     )(start_field, ids)
 
 
-def diffuse_kernel(chunk, chunks, ends_ref, grp_ref, field_ref, ids_ref, runs_ref, *refs):
+def diffuse_kernel(chunk, chunks, n_tile, tile_ref, grp_ref, field_ref, ids_ref, runs_ref, *refs):
     edges, outs = refs[: 2 + 2 * (chunk > 0)], refs[2 + 2 * (chunk > 0) : -11]
     raw_ref, u0_ref, u1_ref, d_ref, a_ref, b_ref, fx_ref, v_ref, wide_ref, made_ref, sem = refs[-11:]
     rows, cols = ids_ref.shape
@@ -115,7 +115,12 @@
         for r in range(rows):
             wide_ref[STEPS + r, :, at] = ids_ref[r : r + 1, at].astype(F32)
 
-    level, pick, steep = runs_ref[0:LEVELS], runs_ref[LEVELS : LEVELS + 1], runs_ref[LEVELS + 1 : LEVELS + 2]
+    mine = pl.ds(pl.multiple_of(grp_ref[0] * LANES, LANES), LANES)
+    level, pick, steep = (
+        runs_ref[0:LEVELS, mine],
+        runs_ref[LEVELS : LEVELS + 1, mine],
+        runs_ref[LEVELS + 1 : LEVELS + 2, mine],
+    )
     table = 0.03 * jnp.exp(level * jnp.log(F32(1.35)))
     both = jnp.concatenate([table * (0.5 * steep), table * (0.5 * (1.0 - steep))], axis=1)
     pieces = []
@@ -127,7 +132,8 @@
     tables = jnp.concatenate(pieces, axis=0).astype(BF16)
     klass = (lax.broadcasted_iota(jnp.int32, (4 * LEVELS, LANES), 0) % LEVELS).astype(F32)
     pick8 = jnp.broadcast_to(pick, (SUB, LANES))
-    has_top, has_bottom = ends_ref[0], ends_ref[1]
+    has_top = jnp.where(tile_ref[0] > 0, F32(1.0), F32(0.0))
+    has_bottom = jnp.where(tile_ref[0] < n_tile - 1, F32(1.0), F32(0.0))
     zeros = jnp.zeros((SUB, LANES), F32)
 
     def inside(r):
@@ -227,7 +233,7 @@
         sent_out.wait()
 
 
-def diffuse(chunk, chunks, start_field, edges, ids, run_rows, ends, grp, blocks):
+def diffuse(chunk, chunks, start_field, edges, ids, run_rows, tile, n_tile, grp, blocks):
     runs, rows, cols = start_field.shape
     total = rows + 2 * STEPS
     low, high, _ = spans(cols, chunks)[chunk]
@@ -237,7 +243,7 @@
     edges = list(edges[chunk]) + (list(edges[chunk - 1]) if chunk else [])
     state = pltpu.VMEM((total, width + 2 * SUB, runs), F32)
     return pl.pallas_call(
-        functools.partial(diffuse_kernel, chunk, chunks),
+        functools.partial(diffuse_kernel, chunk, chunks, n_tile),
         in_specs=[SCALARS, SCALARS, ANY, SPACE, SPACE] + [SPACE] * len(edges),
         out_specs=[ANY] * blocks,
         out_shape=[jax.ShapeDtypeStruct((runs, rows * own // blocks), F32)] * blocks,
@@ -256,7 +262,7 @@
         ],
         cost_estimate=cost(100 * runs * total * width, 12 * runs * total * width),
         name="diffuse",
-    )(ends, grp, start_field, ids, run_rows, *edges)
+    )(tile, grp, start_field, ids, run_rows, *edges)
 
 
 PITCH = 80
@@ -600,10 +606,10 @@
 def on_device(
     start_field, class_ids, run_levels, steepness, step_pick, input_layer, output_layer, output_bias
 ):
-    local_runs, rows, cols = start_field.shape
+    _, rows, cols = start_field.shape
     n_grp, n_tile = lax.axis_size("grp"), lax.axis_size("tile")
-    tile = lax.axis_index("tile")
-    first_run = lax.axis_index("grp") * local_runs
+    tile = lax.axis_index("tile").astype(jnp.int32)[None]
+    grp = lax.axis_index("grp").astype(jnp.int32)[None]
     chunks = CHUNKS
     parts = spans(cols, chunks)
     runs_total, classes = run_levels.shape
@@ -627,8 +633,6 @@
         ],
         axis=0,
     )
-    run_rows_here = lax.dynamic_slice_in_dim(run_rows, first_run, local_runs, 1)
-    ends = jnp.stack([(tile > 0).astype(F32), (tile < n_tile - 1).astype(F32)])
     hidden, hidden_t, gain_t, project = hidden_units(run_rows, input_layer)
     bias_row = output_bias[None, :]
     guess = predict(hidden, output_layer, bias_row)
@@ -636,9 +640,8 @@
 
     state = None
     scale = 2.0 / runs_total
-    grp = lax.axis_index("grp").astype(jnp.int32)[None]
     for c in range(chunks):
-        snaps = diffuse(c, chunks, start_field, edges, class_ids, run_rows_here, ends, grp, n_grp)
+        snaps = diffuse(c, chunks, start_field, edges, class_ids, run_rows, tile, n_tile, grp, n_grp)
         targets = [snaps[0]]
         for offset in range(1, n_grp):
             pairs = [(i, i ^ offset) for i in range(n_grp)]

time: 175 us -> 175 us (level)
  transfers between devices with their start and end apart: 17 -> 17, of which waited for: 9 -> 9; matrix products, arithmetic and copies ran while one was open for 1% -> 0% of each run, Pallas kernels for 31% -> 31%
where the time goes in v6:
time: 175 us; the launch traced here: 174 us
  Pallas kernels  83.4 us (48%)
  waiting for transfers between devices  56.4 us (32%)
  starting transfers between devices  28.4 us (16%)
  local copies, waits for them, and re-layouts  2.94 us (2%)
  other arithmetic  1.81 us (1%)
    ppermute x2, waiting for transfers between devices, on_device(): above = lax.ppermute(bottom, 'tile', up)  34.9 us
    pallas_call x2, Pallas kernels, diffuse(): pl.pallas_call(functools.partial(diffuse_kernel, chunk, chunks, n_tile),...  29.8 us
    pallas_call x2, Pallas kernels, learn(): pl.pallas_call(functools.partial(learn_kernel, last, has_before, scale, s...  21 us
    ppermute x3, waiting for transfers between devices, sum_over_devices(): x = x + lax.ppermute(x, 'tile', [(i, i ^ bit) for i in range(tile)])  11.3 us
    pallas_call x1, Pallas kernels, predict(): pl.pallas_call(predict_kernel, grid=(cells // block,), in_specs=[pl.Block...  9.23 us
    ppermute x2, starting transfers between devices, on_device(): above = lax.ppermute(bottom, 'tile', up)  9.22 us
    ppermute x3, starting transfers between devices, sum_over_devices(): x = x + lax.ppermute(x, 'tile', [(i, i ^ bit) for i in range(tile)])  9.2 us
    pallas_call x2, Pallas kernels, update(): pl.pallas_call(update_kernel, grid=(count,), in_specs=[pl.BlockSpec((hid,...  9.02 us
  transfers between devices with their start and end apart: 17, of which 9 were waited for; matrix products, arithmetic and copies ran while one was open for 0% of the time, Pallas kernels for 31%

profile of v6, /device:TPU:0, one launch (start us, length us, event | category | flops | bytes accessed | tf_op | source)
XLA Modules:
  0.0 173.8 jit_solution(9044693274721662368)
XLA Ops:
  0.7 4.1 %pack_edges.3 = (f32[1072,128]{1,0:T(8,128)}, f32[1072,128]{1,0:T(8,128)}) custom-call(f32[128,16,512]{2,1,0:T(8,128)} %field_ref.7, s32[16,512]{1,0:T(8,128)} %ids_ref.7), custom_call_target="tpu_custom_call" | custom-call | bytes 3244032 | tf_op jit(solution)/shard_map/pack_edges/pallas_call | solution.py:82
  4.8 4.9 %collective-permute-start.2 = (f32[1072,128]{1,0:T(8,128)}, f32[1072,128]{1,0:T(8,128)S(1)}, u32[]{:S(2)}, u32[]{:S(2)}) collective-permute-start(f32[1072,128]{1,0:T(8,128)} %get-tuple-element.31), channel_id=1, source_target_pairs={{0,1},{1,2},{2,3},{3,4},{4,5},{5,6},{6,7},{8,9},{9,10},{10,11},{11... | collective-permute-start | bytes 1646600 | tf_op jit(solution)/shard_map/ppermute | solution.py:623
  9.7 1.3 collective-permute-start.3
  11.8 21.6 %collective-permute-done.2.refs_2_.refs_0_ = f32[1072,128]{1,0:T(8,128)S(1)} collective-permute-done((f32[1072,128]{1,0:T(8,128)}, f32[1072,128]{1,0:T(8,128)S(1)}, u32[]{:S(2)}, u32[]{:S(2)}) %collective-permute-start.2) | collective-permute-done | bytes 548896 | tf_op jit(solution)/shard_map/ppermute | solution.py:623
  33.5 14.9 %diffuse.3 = (f32[128,1024]{1,0:T(8,128)}, f32[128,1024]{1,0:T(8,128)}, f32[128,1024]{1,0:T(8,128)}, f32[128,1024]{1,0:T(8,128)}) custom-call(s32[1]{0:T(128)} %bitcast.5.tile_ref, s32[1]{0:T(128)} %bitcast.grp_ref.refs_0_, f32[128,16,512]{2,1,0:T(8,128)} %field_ref.7, s32[16,512]{1,0:T(8,128)} %ids_ref.7, f32[16,512]{1,0:T(8,128)} %maximum_maximum_fusion.runs_ref, ...), custom_call_target="tpu_custom_call" | custom-call | flops 81100800 | bytes 9732096 | tf_op jit(solution)/shard_map/diffuse/pallas_call | solution.py:245
  48.4 2.9 %pack_edges.2 = (f32[992,128]{1,0:T(8,128)}, f32[992,128]{1,0:T(8,128)}) custom-call(f32[128,16,512]{2,1,0:T(8,128)} %field_ref.7, s32[16,512]{1,0:T(8,128)} %ids_ref.7), custom_call_target="tpu_custom_call" | custom-call | bytes 3047424 | tf_op jit(solution)/shard_map/pack_edges/pallas_call | solution.py:82
  51.4 4.3 %collective-permute-start = (f32[992,128]{1,0:T(8,128)}, f32[992,128]{1,0:T(8,128)S(1)}, u32[]{:S(2)}, u32[]{:S(2)}) collective-permute-start(f32[992,128]{1,0:T(8,128)} %get-tuple-element.29), channel_id=1, source_target_pairs={{0,1},{1,2},{2,3},{3,4},{4,5},{5,6},{6,7},{8,9},{9,10},{10,11},{11... | collective-permute-start | bytes 1523720 | tf_op jit(solution)/shard_map/ppermute | solution.py:623
  55.7 1.5 collective-permute-start.1
  57.2 1.6 collective-permute-start.8
  58.8 6.3 %hidden_units.1 = (bf16[512,2048]{1,0:T(8,128)(2,1)}, bf16[2048,512]{1,0:T(8,128)(2,1)}, f32[2048,512]{1,0:T(8,128)}, bf16[512,128]{1,0:T(8,128)(2,1)}) custom-call(f32[16,512]{1,0:T(8,128)} %maximum_maximum_fusion.runs_ref, f32[69,2048]{1,0:T(8,128)} %layer_ref.3), custom_call_target="tpu_custom_call" | custom-call | flops 1073741824 | bytes 10485760 | tf_op jit(solution)/shard_map/hidden_units/pallas_call | solution.py:336
  65.1 13.2 %collective-permute-done.refs_0_ = f32[992,128]{1,0:T(8,128)S(1)} collective-permute-done((f32[992,128]{1,0:T(8,128)}, f32[992,128]{1,0:T(8,128)S(1)}, u32[]{:S(2)}, u32[]{:S(2)}) %collective-permute-start) | collective-permute-done | bytes 507936 | tf_op jit(solution)/shard_map/ppermute | solution.py:623
  78.3 14.9 %diffuse.2 = (f32[128,1024]{1,0:T(8,128)}, f32[128,1024]{1,0:T(8,128)}, f32[128,1024]{1,0:T(8,128)}, f32[128,1024]{1,0:T(8,128)}) custom-call(s32[1]{0:T(128)} %bitcast.5.tile_ref, s32[1]{0:T(128)} %bitcast.grp_ref.refs_0_, f32[128,16,512]{2,1,0:T(8,128)} %field_ref.7, s32[16,512]{1,0:T(8,128)} %ids_ref.7, f32[16,512]{1,0:T(8,128)} %maximum_maximum_fusion.runs_ref, ...), custom_call_target="tpu_custom_call" | custom-call | flops 81100800 | bytes 9732096 | tf_op jit(solution)/shard_map/diffuse/pallas_call | solution.py:245
  93.3 1.6 collective-permute-start.5
  95.2 9.2 %predict.1.refs_1_ = f32[512,2048]{1,0:T(8,128)} custom-call(bf16[512,2048]{1,0:T(8,128)(2,1)} %get-tuple-element.28.hidden_ref, bf16[2048,2048]{1,0:T(8,128)(2,1)} %weight_ref.5, f32[1,2048]{1,0:T(1,128)} %bitcast.13), custom_call_target="tpu_custom_call" | custom-call | flops 4294967296 | bytes 12582912 | tf_op jit(solution)/shard_map/predict/pallas_call | solution.py:375
  105.2 1.0 copy-done.2
  106.3 11.7 %learn.2 = (bf16[512,2048]{1,0:T(8,128)(2,1)}, f32[1,2048]{1,0:T(1,128)}, f32[2048,128]{1,0:T(8,128)}, bf16[2048,2048]{1,0:T(8,128)(2,1)}) custom-call(s32[1]{0:T(128)} %bitcast.grp_ref.refs_0_, f32[512,2048]{1,0:T(8,128)} %predict.1.refs_1_, f32[128,1024]{1,0:T(8,128)} %get-tuple-element.39.refs_2_, f32[128,1024]{1,0:T(8,128)S(1)} %collective-permute-done.7.refs_3_, ...), custom_call_target="tpu_custom_call" | custom-call | flops 4831838208 | bytes 14680064 | tf_op jit(solution)/shard_map/learn/pallas_call | solution.py:497
  118.7 9.4 %learn.3 = (bf16[512,2048]{1,0:T(8,128)(2,1)}, f32[1,2048]{1,0:T(1,128)}, f32[16,72,128]{2,1,0:T(8,128)}, bf16[512,1024]{1,0:T(8,128)(2,1)}) custom-call(s32[1]{0:T(128)} %bitcast.grp_ref.refs_0_, f32[512,2048]{1,0:T(8,128)} %predict.1.refs_1_, f32[128,1024]{1,0:T(8,128)} %get-tuple-element.33.refs_2_, ...), custom_call_target="tpu_custom_call", output_to_operand_aliasing={{0}: (10, {}), {1}: (11, {})} | custom-call | flops 2684354560 | bytes 10485760 | tf_op jit(solution)/shard_map/learn/pallas_call | solution.py:497
  128.1 1.0 constant_dynamic-slice_fusion.1
  129.5 1.2 collective-permute-done.10
  130.7 1.0 dynamic-slice_add_fusion
  131.7 1.6 collective-permute-start.11
  133.3 4.6 %collective-permute-done.11 = f32[288,128]{1,0:T(8,128)S(1)} collective-permute-done((f32[288,128]{1,0:T(8,128)S(1)}, f32[288,128]{1,0:T(8,128)S(1)}, u32[]{:S(2)}, u32[]{:S(2)}) %collective-permute-start.11) | collective-permute-done | bytes 147488 | tf_op jit(solution)/shard_map/ppermute | solution.py:583
  137.9 2.4 %collective-permute-start.12 = (f32[288,128]{1,0:T(8,128)S(1)}, f32[288,128]{1,0:T(8,128)S(1)}, u32[]{:S(2)}, u32[]{:S(2)}) collective-permute-start(f32[288,128]{1,0:T(8,128)S(1)} %dynamic-slice_add_fusion.1), channel_id=1, source_target_pairs={{0,1},{1,0},{2,3},{3,2},{4,5},{5,4},{6,7},{7,6},{8,9},{9,8},{10,11... | collective-permute-start | bytes 442376 | tf_op jit(solution)/shard_map/ppermute | solution.py:600
  140.4 3.5 %collective-permute-done.12 = f32[288,128]{1,0:T(8,128)S(1)} collective-permute-done((f32[288,128]{1,0:T(8,128)S(1)}, f32[288,128]{1,0:T(8,128)S(1)}, u32[]{:S(2)}, u32[]{:S(2)}) %collective-permute-start.12) | collective-permute-done | bytes 147488 | tf_op jit(solution)/shard_map/ppermute | solution.py:600
  143.9 3.7 %collective-permute-start.13 = (f32[288,128]{1,0:T(8,128)S(1)}, f32[288,128]{1,0:T(8,128)S(1)}, u32[]{:S(2)}, u32[]{:S(2)}) collective-permute-start(f32[288,128]{1,0:T(8,128)S(1)} %add.21), channel_id=1, source_target_pairs={{0,2},{1,3},{2,0},{3,1},{4,6},{5,7},{6,4},{7,5},{8,10},{9,11},{10,... | collective-permute-start | bytes 442376 | tf_op jit(solution)/shard_map/ppermute | solution.py:600
  147.6 3.1 %collective-permute-done.13 = f32[288,128]{1,0:T(8,128)S(1)} collective-permute-done((f32[288,128]{1,0:T(8,128)S(1)}, f32[288,128]{1,0:T(8,128)S(1)}, u32[]{:S(2)}, u32[]{:S(2)}) %collective-permute-start.13) | collective-permute-done | bytes 147488 | tf_op jit(solution)/shard_map/ppermute | solution.py:600
  150.7 3.1 %collective-permute-start.14 = (f32[288,128]{1,0:T(8,128)S(1)}, f32[288,128]{1,0:T(8,128)S(1)}, u32[]{:S(2)}, u32[]{:S(2)}) collective-permute-start(f32[288,128]{1,0:T(8,128)S(1)} %add.22), channel_id=1, source_target_pairs={{0,4},{1,5},{2,6},{3,7},{4,0},{5,1},{6,2},{7,3},{8,12},{9,13},{10,... | collective-permute-start | bytes 442376 | tf_op jit(solution)/shard_map/ppermute | solution.py:600
  153.8 4.7 %collective-permute-done.14 = f32[288,128]{1,0:T(8,128)S(1)} collective-permute-done((f32[288,128]{1,0:T(8,128)S(1)}, f32[288,128]{1,0:T(8,128)S(1)}, u32[]{:S(2)}, u32[]{:S(2)}) %collective-permute-start.14) | collective-permute-done | bytes 147488 | tf_op jit(solution)/shard_map/ppermute | solution.py:600
  158.5 1.6 collective-permute-start.15
  160.1 3.7 %collective-permute-done.15 = f32[288,128]{1,0:T(8,128)S(1)} collective-permute-done((f32[288,128]{1,0:T(8,128)S(1)}, f32[288,128]{1,0:T(8,128)S(1)}, u32[]{:S(2)}, u32[]{:S(2)}) %collective-permute-start.15) | collective-permute-done | bytes 147488 | tf_op jit(solution)/shard_map/ppermute | solution.py:589
  163.8 4.5 %update.2._ = bf16[2048,2048]{1,0:T(8,128)(2,1)} custom-call(bf16[2048,512]{1,0:T(8,128)(2,1)} %get-tuple-element.43.refs_10_.hidden_t_ref, bf16[512,1024]{1,0:T(8,128)(2,1)} %get-tuple-element.48.slope_ref, bf16[2048,2048]{1,0:T(8,128)(2,1)} %weight_ref.5, bf16[2048,2048]{1,0:T(8,128)(2,1)} %get-tuple-element.49._), custom_call_target="tpu_custom_call", output_to_operand_aliasing={{}: (3, {})} | custom-call | flops 1073741824 | bytes 5242880 | tf_op jit(solution)/shard_map/update/pallas_call | solution.py:535
  168.3 4.5 %update.3 = bf16[2048,2048]{1,0:T(8,128)(2,1)} custom-call(bf16[2048,512]{1,0:T(8,128)(2,1)} %get-tuple-element.43.refs_10_.hidden_t_ref, bf16[512,1024]{1,0:T(8,128)(2,1)} %get-tuple-element.48.slope_ref, bf16[2048,2048]{1,0:T(8,128)(2,1)} %weight_ref.5, bf16[2048,2048]{1,0:T(8,128)(2,1)} %update.2._), custom_call_target="tpu_custom_call", output_to_operand_aliasing={{}: (3, {})} | custom-call | flops 1073741824 | bytes 5242880 | tf_op jit(solution)/shard_map/update/pallas_call | solution.py:535
  (39 shorter events, 4.4 us)
Async XLA Ops:
  0.6 10.4 %copy-start.4 = (s32[512]{0:T(512)S(1)}, s32[512]{0:T(512)}, u32[]{:S(2)}) copy-start(s32[512]{0:T(512)} %param.12) | copy-start | bytes 6148
  0.6 10.5 %copy-start.3 = (s32[512,8]{0,1:T(8,128)S(1)}, s32[512,8]{0,1:T(8,128)}, u32[]{:S(2)}) copy-start(s32[512,8]{0,1:T(8,128)} %param.10) | copy-start | bytes 49156
  0.7 10.5 %copy-start.5 = (f32[512]{0:T(512)S(1)}, f32[512]{0:T(512)}, u32[]{:S(2)}) copy-start(f32[512]{0:T(512)} %param.11) | copy-start | bytes 6148
  4.8 28.7 %collective-permute-start.2 = (f32[1072,128]{1,0:T(8,128)}, f32[1072,128]{1,0:T(8,128)S(1)}, u32[]{:S(2)}, u32[]{:S(2)}) collective-permute-start(f32[1072,128]{1,0:T(8,128)} %get-tuple-element.31), channel_id=1, source_target_pairs={{0,1},{1,2},{2,3},{3,4},{4,5},{5,6},{6,7},{8,9},{9,10},{10,11},{11... | collective-permute-start | bytes 1646600 | tf_op jit(solution)/shard_map/ppermute | solution.py:623
  9.7 23.7 %collective-permute-start.3 = (f32[1072,128]{1,0:T(8,128)}, f32[1072,128]{1,0:T(8,128)S(1)}, u32[]{:S(2)}, u32[]{:S(2)}) collective-permute-start(f32[1072,128]{1,0:T(8,128)} %get-tuple-element.32), channel_id=1, source_target_pairs={{1,0},{2,1},{3,2},{4,3},{5,4},{6,5},{7,6},{9,8},{10,9},{11,10},{12... | collective-permute-start | bytes 1646600 | tf_op jit(solution)/shard_map/ppermute | solution.py:624
  48.4 46.5 %collective-permute-start.7 = (f32[128,1024]{1,0:T(8,128)}, f32[128,1024]{1,0:T(8,128)S(1)}, u32[]{:S(2)}, u32[]{:S(2)}) collective-permute-start(f32[128,1024]{1,0:T(8,128)} %get-tuple-element.40), channel_id=1, source_target_pairs={{0,8},{8,0},{16,24},{24,16},{1,9},{9,1},{17,25},{25,17},{2,10},{10... | collective-permute-start | bytes 1572872 | tf_op jit(solution)/shard_map/ppermute | solution.py:648
  51.4 26.9 %collective-permute-start = (f32[992,128]{1,0:T(8,128)}, f32[992,128]{1,0:T(8,128)S(1)}, u32[]{:S(2)}, u32[]{:S(2)}) collective-permute-start(f32[992,128]{1,0:T(8,128)} %get-tuple-element.29), channel_id=1, source_target_pairs={{0,1},{1,2},{2,3},{3,4},{4,5},{5,6},{6,7},{8,9},{9,10},{10,11},{11... | collective-permute-start | bytes 1523720 | tf_op jit(solution)/shard_map/ppermute | solution.py:623
  55.7 22.6 %collective-permute-start.1 = (f32[992,128]{1,0:T(8,128)}, f32[992,128]{1,0:T(8,128)S(1)}, u32[]{:S(2)}, u32[]{:S(2)}) collective-permute-start(f32[992,128]{1,0:T(8,128)} %get-tuple-element.30), channel_id=1, source_target_pairs={{1,0},{2,1},{3,2},{4,3},{5,4},{6,5},{7,6},{9,8},{10,9},{11,10},{12... | collective-permute-start | bytes 1523720 | tf_op jit(solution)/shard_map/ppermute | solution.py:624
  57.2 47.3 %collective-permute-start.8 = (f32[128,1024]{1,0:T(8,128)}, f32[128,1024]{1,0:T(8,128)S(1)}, u32[]{:S(2)}, u32[]{:S(2)}) collective-permute-start(f32[128,1024]{1,0:T(8,128)} %get-tuple-element.41), channel_id=1, source_target_pairs={{0,16},{8,24},{16,0},{24,8},{1,17},{9,25},{17,1},{25,9},{2,18},{10... | collective-permute-start | bytes 1572872 | tf_op jit(solution)/shard_map/ppermute | solution.py:648
  58.7 46.5 %collective-permute-start.9 = (f32[128,1024]{1,0:T(8,128)}, f32[128,1024]{1,0:T(8,128)}, u32[]{:S(2)}, u32[]{:S(2)}) collective-permute-start(f32[128,1024]{1,0:T(8,128)} %get-tuple-element.42), channel_id=1, source_target_pairs={{0,24},{8,16},{16,8},{24,0},{1,25},{9,17},{17,9},{25,1},{2,26},{10... | collective-permute-start | bytes 1572872 | tf_op jit(solution)/shard_map/ppermute | solution.py:648
  93.3 24.7 %collective-permute-start.4 = (f32[128,1024]{1,0:T(8,128)}, f32[128,1024]{1,0:T(8,128)S(1)}, u32[]{:S(2)}, u32[]{:S(2)}) collective-permute-start(f32[128,1024]{1,0:T(8,128)} %get-tuple-element.34), channel_id=1, source_target_pairs={{0,8},{8,0},{16,24},{24,16},{1,9},{9,1},{17,25},{25,17},{2,10},{10... | collective-permute-start | bytes 1572872 | tf_op jit(solution)/shard_map/ppermute | solution.py:648
  93.3 24.6 %collective-permute-start.5 = (f32[128,1024]{1,0:T(8,128)}, f32[128,1024]{1,0:T(8,128)S(1)}, u32[]{:S(2)}, u32[]{:S(2)}) collective-permute-start(f32[128,1024]{1,0:T(8,128)} %get-tuple-element.35), channel_id=1, source_target_pairs={{0,16},{8,24},{16,0},{24,8},{1,17},{9,25},{17,1},{25,9},{2,18},{10... | collective-permute-start | bytes 1572872 | tf_op jit(solution)/shard_map/ppermute | solution.py:648
  94.9 23.8 %collective-permute-start.6 = (f32[128,1024]{1,0:T(8,128)}, f32[128,1024]{1,0:T(8,128)}, u32[]{:S(2)}, u32[]{:S(2)}) collective-permute-start(f32[128,1024]{1,0:T(8,128)} %get-tuple-element.36), channel_id=1, source_target_pairs={{0,24},{8,16},{16,8},{24,0},{1,25},{9,17},{17,9},{25,1},{2,26},{10... | collective-permute-start | bytes 1572872 | tf_op jit(solution)/shard_map/ppermute | solution.py:648
  104.4 0.8 copy-start.1
  105.2 1.0 copy-start.2
  129.1 1.6 collective-permute-start.10
  131.7 6.2 %collective-permute-start.11 = (f32[288,128]{1,0:T(8,128)S(1)}, f32[288,128]{1,0:T(8,128)S(1)}, u32[]{:S(2)}, u32[]{:S(2)}) collective-permute-start(f32[288,128]{1,0:T(8,128)S(1)} %constant_dynamic-slice_fusion), channel_id=1, source_target_pairs={{0,16},{8,24},{16,0},{24,8},{1,17},{9,25},{17,1},{25,9},{2,18},{10... | collective-permute-start | bytes 442376 | tf_op jit(solution)/shard_map/ppermute | solution.py:583
  137.9 6.0 %collective-permute-start.12 = (f32[288,128]{1,0:T(8,128)S(1)}, f32[288,128]{1,0:T(8,128)S(1)}, u32[]{:S(2)}, u32[]{:S(2)}) collective-permute-start(f32[288,128]{1,0:T(8,128)S(1)} %dynamic-slice_add_fusion.1), channel_id=1, source_target_pairs={{0,1},{1,0},{2,3},{3,2},{4,5},{5,4},{6,7},{7,6},{8,9},{9,8},{10,11... | collective-permute-start | bytes 442376 | tf_op jit(solution)/shard_map/ppermute | solution.py:600
  143.9 6.8 %collective-permute-start.13 = (f32[288,128]{1,0:T(8,128)S(1)}, f32[288,128]{1,0:T(8,128)S(1)}, u32[]{:S(2)}, u32[]{:S(2)}) collective-permute-start(f32[288,128]{1,0:T(8,128)S(1)} %add.21), channel_id=1, source_target_pairs={{0,2},{1,3},{2,0},{3,1},{4,6},{5,7},{6,4},{7,5},{8,10},{9,11},{10,... | collective-permute-start | bytes 442376 | tf_op jit(solution)/shard_map/ppermute | solution.py:600
  150.7 7.8 %collective-permute-start.14 = (f32[288,128]{1,0:T(8,128)S(1)}, f32[288,128]{1,0:T(8,128)S(1)}, u32[]{:S(2)}, u32[]{:S(2)}) collective-permute-start(f32[288,128]{1,0:T(8,128)S(1)} %add.22), channel_id=1, source_target_pairs={{0,4},{1,5},{2,6},{3,7},{4,0},{5,1},{6,2},{7,3},{8,12},{9,13},{10,... | collective-permute-start | bytes 442376 | tf_op jit(solution)/shard_map/ppermute | solution.py:600
  158.5 5.2 %collective-permute-start.15 = (f32[288,128]{1,0:T(8,128)S(1)}, f32[288,128]{1,0:T(8,128)S(1)}, u32[]{:S(2)}, u32[]{:S(2)}) collective-permute-start(f32[288,128]{1,0:T(8,128)S(1)} %add.23), channel_id=1, source_target_pairs={{0,16},{8,24},{16,0},{24,8},{1,17},{9,25},{17,1},{25,9},{2,18},{10... | collective-permute-start | bytes 442376 | tf_op jit(solution)/shard_map/ppermute | solution.py:589
  163.8 9.1 %collective-permute-start.16 = (f32[576,128]{1,0:T(8,128)S(1)}, f32[576,128]{1,0:T(8,128)S(1)}, u32[]{:S(2)}, u32[]{:S(2)}) collective-permute-start(f32[576,128]{1,0:T(8,128)S(1)} %maximum_select_fusion.1), channel_id=1, source_target_pairs={{0,8},{8,0},{16,24},{24,16},{1,9},{9,1},{17,25},{25,17},{2,10},{10... | collective-permute-start | bytes 884744 | tf_op jit(solution)/shard_map/ppermute | solution.py:589
  168.3 4.6 %copy-start = (f32[69,2048]{1,0:T(8,128)S(1)}, f32[69,2048]{1,0:T(8,128)}, u32[]{:S(2)}) copy-start(f32[69,2048]{1,0:T(8,128)} %layer_ref.3) | copy-start | bytes 1695748
